TPU v7x, 256 devices: a whole 4x4x8 slice. The times are simulated.
256 devices in a mesh: tm: 32 (over y_hi, z, core), head: 4 (over x), rep: 2 (over y_lo).
Axes of the slice: x: 4, y: 4 (y_hi: 2, y_lo: 2; y = y_hi * 2 + y_lo), z: 8, core: 2. Of those that a mesh axis runs over, the one named last changes fastest.
Arguments:
- queries: bfloat16 [32768, 1536], P(('tm', 'rep'), 'head'), may hold values from -8 to 8
- kv_cache: bfloat16 [32768, 2, 1536], P('tm', None, 'head'), may hold values from -8 to 8
- out_weight: bfloat16 [1536, 3072], P('head'), may hold values from -0.15625 to 0.15625
- fetch_list: int32 [64, 32], P(('tm', 'rep')), may hold values from 0 to 247, as said below
- tile_lists: int32 [256, 16], P(('tm', 'rep')), may hold values from 0 to 31, as said below
- event_offsets: int32 [256], P(('tm', 'rep')), may hold values from 0 to 7
Outputs:
- mixed: bfloat16 [32768, 3072], P(('tm', 'rep'), 'head')
Inputs may be any that keep to these rules, and one draw needn't show every extreme that they name: `fetch_list`: each row names 32 distinct blocks, all with ids below (31) * 8, so none of the newest ones; one row names at most 2 blocks of one owner, and every row names exactly 2 blocks of some owner. `tile_lists`: each row names 16 distinct positions; the tiles of one device together name every position of its row of fetch_list.
All inputs are finite; a program needn't handle non-finite values.
Results may differ from a plain program's by a relative error of at most 0.013.
Values may be sent and summed in bfloat16 or wider, within the bound.
No kernel may reach another device: no remote copies, remote signals or barrier semaphores. Data moves between devices by JAX's collectives and lax.ppermute only.
A program may use at most 128 MiB of HBM per device.

v0:
```python
import math

import jax
import jax.numpy as jnp
from jax import lax
from jax.sharding import PartitionSpec as P

DH = 128
TILE = 128
CB_DEV = 8
CAP = 2


def from_root(shard, axis, root):
    mine = lax.axis_index(axis) == root
    return lax.psum(jnp.where(mine, shard, jnp.zeros_like(shard)), axis)


def owner_ranks(owners):
    entry_count = owners.shape[-1]
    index_row = jnp.arange(entry_count, dtype=jnp.int32)
    same_owner = owners[..., None, :] == owners[..., :, None]
    earlier = index_row[None, :] < index_row[:, None]
    return jnp.sum(same_owner & earlier, axis=-1)


def outgoing(requests, wanted, block_rows, me_owner):
    owners = requests // CB_DEV
    slot_ids = requests % CB_DEV
    rank_ids = owner_ranks(owners)
    is_mine = owners == me_owner
    hit_table = is_mine[:, :, None] & (rank_ids[:, :, None] == wanted[None, None, :])
    chosen = jnp.sum(jnp.where(hit_table, slot_ids[:, :, None], 0), axis=1)
    in_use = jnp.any(hit_table, axis=1)
    picked = jnp.take(block_rows, chosen, axis=0)
    return jnp.where(in_use[:, :, None, None, None], picked, jnp.zeros_like(picked))


def shards(queries, kv_cache, out_weight, fetch_list, tile_lists, event_offsets):
    me_owner = lax.axis_index("tm")
    feature_width = kv_cache.shape[2]
    head_count = feature_width // DH
    block_rows = kv_cache.reshape(CB_DEV, -1, 2, feature_width)
    block_len = block_rows.shape[1]
    own_owners = fetch_list[0] // CB_DEV
    own_ranks = owner_ranks(own_owners)
    requests = lax.all_gather(fetch_list, "tm", axis=0, tiled=True)
    outbound = outgoing(requests, jnp.arange(CAP, dtype=jnp.int32), block_rows, me_owner)
    arrived = lax.all_to_all(outbound, "tm", split_axis=0, concat_axis=0, tiled=True)
    flat_blocks = arrived.reshape(-1, block_len, 2, feature_width)
    fetched = jnp.take(flat_blocks, own_owners * CAP + own_ranks, axis=0)
    newest = lax.axis_size("tm") - 1
    panel_rows = from_root(kv_cache, "tm", newest)
    panel_keys = panel_rows[:, 0].reshape(-1, head_count, DH)
    panel_values = panel_rows[:, 1].reshape(-1, head_count, DH)
    slab_rows = panel_keys.shape[0]
    tile_count = queries.shape[0] // TILE
    per_step = math.gcd(tile_count, 4)
    query_groups = queries.reshape(tile_count // per_step, per_step, TILE, head_count, DH)
    list_groups = tile_lists.reshape(tile_count // per_step, per_step, -1)
    offset_groups = event_offsets.reshape(tile_count // per_step, per_step)
    score_scale = 1.0 / math.sqrt(DH)
    positions = jnp.arange(slab_rows, dtype=jnp.int32)

    def attend(pieces):
        query_block, list_rows, offsets = pieces
        picked = jnp.take(fetched, list_rows, axis=0).reshape(per_step, -1, 2, feature_width)
        far_keys = picked[:, :, 0].reshape(per_step, -1, head_count, DH)
        far_values = picked[:, :, 1].reshape(per_step, -1, head_count, DH)
        far_scores = (
            jnp.einsum("gqhd,gkhd->ghqk", query_block, far_keys, preferred_element_type=jnp.float32)
            * score_scale
        )
        near_scores = (
            jnp.einsum(
                "gqhd,khd->ghqk", query_block, panel_keys, preferred_element_type=jnp.float32
            )
            * score_scale
        )
        visible = positions[None, :] < (CB_DEV - offsets)[:, None] * block_len
        near_scores = jnp.where(visible[:, None, None, :], near_scores, -1e30)
        row_max = jnp.maximum(jnp.max(far_scores, axis=-1), jnp.max(near_scores, axis=-1))
        far_weights = jnp.exp(far_scores - row_max[..., None])
        near_weights = jnp.exp(near_scores - row_max[..., None])
        denom_sum = jnp.sum(far_weights, axis=-1) + jnp.sum(near_weights, axis=-1)
        blended = jnp.einsum(
            "ghqk,gkhd->gqhd",
            far_weights.astype(jnp.bfloat16),
            far_values,
            preferred_element_type=jnp.float32,
        )
        blended = blended + jnp.einsum(
            "ghqk,khd->gqhd",
            near_weights.astype(jnp.bfloat16),
            panel_values,
            preferred_element_type=jnp.float32,
        )
        blended = blended / jnp.transpose(denom_sum, (0, 2, 1))[..., None]
        return blended.astype(jnp.bfloat16).reshape(per_step, TILE, head_count * DH)

    attended = lax.map(attend, (query_groups, list_groups, offset_groups)).reshape(
        -1, head_count * DH
    )
    partial_value = jnp.dot(attended, out_weight, preferred_element_type=jnp.float32)
    return lax.psum_scatter(
        partial_value.astype(jnp.bfloat16), "head", scatter_dimension=1, tiled=True
    )


def solution(mesh):
    placed = (
        P(("tm", "rep"), "head"),
        P("tm", None, "head"),
        P("head", None),
        P(("tm", "rep"), None),
        P(("tm", "rep"), None),
        P(("tm", "rep")),
    )
    return jax.shard_map(
        shards, mesh=mesh, in_specs=placed, out_specs=P(("tm", "rep"), "head"), check_vma=False
    )
```

profile of v0, /device:TPU:64, one launch (start us, length us, event | category | flops | bytes accessed | tf_op | source)
XLA Modules:
  0.0 598.7 jit_solution(15882582718426881978)
XLA Ops:
  6.5 39.5 %all-gather = s32[32,1,32]{2,1,0:T(1,128)S(1)} all-gather(s32[1,1,32]{2,1,0:T(1,128)} %bitcast.112), channel_id=1, replica_groups=mesh['tm'=32,'head'=4,'rep'=2] {'tm'}, dimensions={0}, use_global_device_ids=true | all-gather | bytes 4224 | tf_op jit(solution)/shard_map/all_gather | solution.py:47
  46.1 0.8 convert_reduce_fusion
  46.9 0.1 select_reduce_fusion
  47.1 0.1 fusion.34
  47.2 0.1 copy.118
  47.3 0.1 reshape.205
  47.4 29.6 %gather_fusion = bf16[64,128,2,384]{3,2,1,0:T(2,128)(2,1)} fusion(bf16[8,128,2,384]{3,2,1,0:T(2,128)(2,1)} %bitcast.101, s32[1024]{0:T(1024)S(1)} %pad_clamp_fusion.2), kind=kCustom, calls=%fused_computation | custom fusion | bytes 25166080 | tf_op jit(solution)/shard_map/jit(_take)/gather | solution.py:35
  77.0 11.5 %copy.119 = bf16[64,128,2,384]{3,1,2,0:T(8,128)(2,1)} copy(bf16[64,128,2,384]{3,2,1,0:T(2,128)(2,1)} %gather_fusion) | data formatting | bytes 25165824 | tf_op jit(solution)/shard_map/jit(_take)/gather | solution.py:35
  88.5 0.1 copy.117
  88.6 0.1 copy.116
  88.7 11.0 %select_select_fusion = bf16[32,2,128,2,384]{4,2,3,1,0:T(8,128)(2,1)} fusion(bf16[32,2,128,2,384]{4,2,3,1,0:T(8,128)(2,1)} %bitcast.102, pred[32,2]{1,0:T(8,128)(4,1)S(1)} %copy.117, pred[32,2]{1,0:T(8,128)(4,1)S(1)} %copy.116), kind=kLoop, calls=%fused_computation.7 | loop fusion | flops 12582912 | bytes 25165952 | tf_op jit(solution)/shard_map/jit(_where)/select_n | solution.py:36
  99.8 9.9 %all-to-all-start = ((bf16[32,2,128,2,384]{4,2,3,1,0:T(8,128)(2,1)}), bf16[32,2,128,2,384]{4,2,3,1,0:T(8,128)(2,1)}, u32[]{:S(2)}, u32[]{:S(2)}) async-start(bf16[32,2,128,2,384]{4,2,3,1,0:T(8,128)(2,1)} %select_select_fusion), calls=%async_computation | async-start | bytes 25165824 | tf_op jit(solution)/shard_map/all_to_all | solution.py:49
  109.7 0.0 copy-start.3
  109.7 0.0 copy-start.4
  109.7 0.0 copy-start.5
  109.8 0.0 all-reduce.2.cloned.1.call-start
  109.8 5.0 copy.126
  114.8 1.3 broadcast_select_fusion.1
  116.1 0.0 all-reduce.2.cloned.1.call-update
  116.1 0.0 reduce-scatter.2.cloned.1.call-start
  116.2 0.1 broadcast_bitcast_fusion
  116.3 0.1 reshape.221
  116.4 0.2 copy.123
  116.6 0.1 squeeze.28
  116.7 0.2 convert_reduce_fusion.1
  116.9 0.6 pad_clamp_fusion.1
  117.6 0.6 compare_and_fusion.1
  118.1 0.1 iota_compare_fusion.1
  118.2 337.6 %all-reduce.2.cloned.1.call-done = bf16[1024,2,384]{0,2,1:T(8,128)(2,1)} async-done(((bf16[1024,2,384]{0,2,1:T(8,128)(2,1)}), bf16[1024,2,384]{0,2,1:T(8,128)(2,1)}) %all-reduce.2.cloned.1.call-update) | async-done | bytes 1572880 | tf_op jit(solution)/shard_map/psum | solution.py:16
  455.8 1.5 fusion.42
  457.3 4.3 fusion.9
  461.6 8.7 %gather_fusion.1 = bf16[32,128,2,384]{3,1,2,0:T(8,128)(2,1)} fusion(bf16[64,128,2,384]{3,1,2,0:T(8,128)(2,1)} %bitcast.7, s32[1024]{0:T(1024)} %pad_clamp_fusion.1), kind=kCustom, calls=%fused_computation.1 | custom fusion | bytes 12583040 | tf_op jit(solution)/shard_map/jit(_take)/gather | solution.py:51
  470.4 6.2 %broadcast_select_fusion = bf16[32,128,2,384]{3,1,2,0:T(8,128)(2,1)} fusion(bf16[32,128,2,384]{3,1,2,0:T(8,128)(2,1)} %gather_fusion.1, pred[32]{0:T(512)(128)(4,1)} %compare_and_fusion.1), kind=kLoop, calls=%fused_computation.15 | loop fusion | flops 3145728 | bytes 12582944 | tf_op jit(solution)/shard_map/jit(_take)/select_n | solution.py:51
  476.5 9.9 %gather_fusion.2 = bf16[64,128,2,384]{3,1,2,0:T(8,128)(2,1)} fusion(bf16[32,128,2,384]{3,1,2,0:T(8,128)(2,1)} %broadcast_select_fusion, s32[1024]{0:T(1024)S(1)} %pad_clamp_fusion), kind=kCustom, calls=%fused_computation.2 | custom fusion | bytes 25166080 | tf_op jit(solution)/shard_map/while/body/eval_jaxpr/jit(_take)/gather | solution.py:67
  486.4 7.0 %copy.120 = bf16[64,128,2,384]{3,1,0,2:T(8,128)(2,1)S(1)} copy(bf16[64,128,2,384]{3,1,2,0:T(8,128)(2,1)} %gather_fusion.2) | data formatting | bytes 25165824 | tf_op jit(solution)/shard_map/while/body/eval_jaxpr/jit(_take)/gather | solution.py:67
  493.4 3.0 bitcast_select_fusion
  496.4 5.7 fusion.41
  502.1 8.7 %copy.121 = bf16[4,2048,1,384]{1,3,0,2:T(8,128)(2,1)} copy(bf16[4,2048,1,384]{3,1,0,2:T(8,128)(2,1)} %get-tuple-element.24) | data formatting | bytes 12582912 | tf_op jit(solution)/shard_map/while/body/eval_jaxpr/slice | solution.py:69
  510.8 8.6 %copy.122 = bf16[4,2048,1,384]{1,3,0,2:T(8,128)(2,1)} copy(bf16[4,2048,1,384]{3,1,0,2:T(8,128)(2,1)} %get-tuple-element.23) | data formatting | bytes 12582912 | tf_op jit(solution)/shard_map/while/body/eval_jaxpr/slice | solution.py:68
  519.4 4.7 bitcast_reduce_fusion
  524.1 2.1 fusion.1
  526.2 5.4 fusion.12
  531.6 4.7 fusion.7
  536.3 0.6 fusion.24
  537.0 0.3 copy.134
  537.3 3.5 convolution_convert_fusion
  540.8 0.0 reduce-scatter.2.cloned.1.call-update
  540.8 51.0 %reduce-scatter.2.cloned.1.call-done = bf16[512,768]{1,0:T(8,128)(2,1)} async-done(((bf16[512,3072]{1,0:T(8,128)(2,1)}), bf16[512,768]{1,0:T(8,128)(2,1)}) %reduce-scatter.2.cloned.1.call-update) | async-done | bytes 786448 | tf_op jit(solution)/shard_map/reduce_scatter | solution.py:105
  (27 shorter events, 0.2 us)
Async XLA Ops:
  6.5 530.8 %copy-start = (bf16[384,3072]{1,0:T(8,128)(2,1)S(1)}, bf16[384,3072]{1,0:T(8,128)(2,1)}, u32[]{:S(2)}) copy-start(bf16[384,3072]{1,0:T(8,128)(2,1)} %param.8) | copy-start | bytes 7077892
  99.8 361.8 %all-to-all-start = ((bf16[32,2,128,2,384]{4,2,3,1,0:T(8,128)(2,1)}), bf16[32,2,128,2,384]{4,2,3,1,0:T(8,128)(2,1)}, u32[]{:S(2)}, u32[]{:S(2)}) async-start(bf16[32,2,128,2,384]{4,2,3,1,0:T(8,128)(2,1)} %select_select_fusion), calls=%async_computation | async-start | bytes 25165824 | tf_op jit(solution)/shard_map/all_to_all | solution.py:49
  109.7 6.5 %copy-start.3 = (s32[4,16]{1,0:T(4,128)S(1)}, s32[4,16]{1,0:T(4,128)}, u32[]{:S(2)}) copy-start(s32[4,16]{1,0:T(4,128)} %param.10) | copy-start | bytes 772
  109.7 6.7 %copy-start.1 = (bf16[512,384]{1,0:T(8,128)(2,1)S(1)}, bf16[512,384]{1,0:T(8,128)(2,1)}, u32[]{:S(2)}) copy-start(bf16[512,384]{1,0:T(8,128)(2,1)} %param.6) | copy-start | bytes 1179652
  109.7 7.0 %copy-start.4 = (s32[1,32]{1,0:T(1,128)S(1)}, s32[1,32]{1,0:T(1,128)}, u32[]{:S(2)}) copy-start(s32[1,32]{1,0:T(1,128)} %param.9) | copy-start | bytes 388
  109.7 7.8 %copy-start.5 = (s32[4]{0:T(128)S(1)}, s32[4]{0:T(128)}, u32[]{:S(2)}) copy-start(s32[4]{0:T(128)} %param.11) | copy-start | bytes 52
  109.8 346.1 %all-reduce.2.cloned.1.call-start = ((), (), s32[]{:S(2)}) async-start(), calls=%async_computation.2 | async-start | bytes 3145728 | tf_op jit(solution)/shard_map/psum | solution.py:16
  116.1 475.7 %reduce-scatter.2.cloned.1.call-start = ((), (), s32[]{:S(2)}) async-start(), calls=%async_computation.3 | async-start | bytes 3932160 | tf_op jit(solution)/shard_map/reduce_scatter | solution.py:105
  519.4 4.7 copy-start.2
Sparse Core Ops, SparseCore 0:
  116.2 339.5 all-reduce.1
  541.0 50.8 reduce-scatter.1
where the time goes:
time: 601 us; the launch traced here: 599 us
  waiting for transfers between devices  389 us (65%)
  local copies, waits for them, and re-layouts  97.5 us (16%)
  blocking collectives  39.5 us (7%)
  other arithmetic  30.8 us (5%)
  matrix products  18.6 us (3%)
  between operations  13.7 us (2%)
  starting transfers between devices  10 us (2%)
    psum x1, waiting for transfers between devices, from_root(): return lax.psum(jnp.where(mine, shard, jnp.zeros_like(shard)), axis)  338 us
    reduce_scatter x1, waiting for transfers between devices, shards(): lax.psum_scatter(partial_value.astype(jnp.bfloat16), 'head', scatter_dime...  51 us
    gather x2, local copies, waits for them, and re-layouts, outgoing(): picked = jnp.take(block_rows, chosen, axis=0)  41.1 us
    all_gather x1, blocking collectives, shards(): requests = lax.all_gather(fetch_list, 'tm', axis=0, tiled=True)  39.5 us
    gather x2, local copies, waits for them, and re-layouts, attend(): jnp.take(fetched, list_rows, axis=0).reshape(per_step, -1, 2, feature_width)  16.9 us
    slice x2, local copies, waits for them, and re-layouts, attend(): far_keys = picked[:, :, 0].reshape(per_step, -1, head_count, DH)  14.3 us
  transfers between devices with their start and end apart: 3, of which 2 were waited for; matrix products, arithmetic and copies ran while one was open for 2% of the time, Pallas kernels for 0%

commit v1 on v0

v1 whole, which is shorter than its diff:
```python
import math

import jax
import jax.numpy as jnp
from jax import lax
from jax.experimental import pallas as pl
from jax.experimental.pallas import tpu as pltpu
from jax.sharding import Mesh, PartitionSpec as P

DH = 128
TILE = 128
BLK = 128
CB_DEV = 8
SEL = 16
HALF = CB_DEV // 2
GROUP = 4
NEG = -1e30
COLUMN = ("yh", "yl")
N_COL = 4
N_X = 4
LSE_ROWS = 16


def shift(n, by):
    return [(i, (i + by) % n) for i in range(n)]


def split3(x):
    a = x.astype(jnp.bfloat16)
    rest = x - a.astype(jnp.float32)
    b = rest.astype(jnp.bfloat16)
    c = (rest - b.astype(jnp.float32)).astype(jnp.bfloat16)
    return a, b, c


def attend_kernel(counts, lists, q0, q1, q2, q3, kv, out, acc, ml):
    heads = kv.shape[1]
    scale = 1.0 / math.sqrt(DH)
    qs = (q0, q1, q2, q3)
    for r in range(4):
        q_ref = qs[r]

        @pl.loop(0, 4)
        def _(t, r=r, q_ref=q_ref):
            tile = r * 4 + t
            n = counts[tile]
            acc[...] = jnp.zeros_like(acc)
            ml[...] = jnp.full_like(ml, NEG)
            ml[8:16, :] = jnp.zeros((8, TILE), jnp.float32)
            row = pl.multiple_of(t * TILE, TILE)

            @pl.loop(0, (n + GROUP - 1) // GROUP)
            def _(g):
                base = g * GROUP
                blocks = [lists[tile, base + k] for k in range(GROUP)]
                for h in range(heads):
                    q = q_ref[pl.ds(row, TILE), h * DH : (h + 1) * DH]
                    scores = []
                    for k in range(GROUP):
                        s = lax.dot_general(
                            kv[blocks[k], h, 0],
                            q,
                            (((1,), (1,)), ((), ())),
                            preferred_element_type=jnp.float32,
                        )
                        if k:
                            s = jnp.where(base + k < n, s, NEG)
                        scores.append(s)
                    top = scores[0]
                    for s in scores[1:]:
                        top = jnp.maximum(top, s)
                    old = ml[h : h + 1, :]
                    new = jnp.maximum(old, jnp.max(top, axis=0, keepdims=True))
                    fade = jnp.exp((old - new) * scale)
                    total = None
                    mixed = None
                    for k in range(GROUP):
                        w = jnp.exp((scores[k] - new) * scale)
                        total = w if total is None else total + w
                        part = jnp.dot(
                            kv[blocks[k], h, 1],
                            w.astype(jnp.bfloat16),
                            preferred_element_type=jnp.float32,
                        )
                        mixed = part if mixed is None else mixed + part
                    ml[h : h + 1, :] = new
                    ml[8 + h : 9 + h, :] = ml[8 + h : 9 + h, :] * fade + jnp.sum(
                        total, axis=0, keepdims=True
                    )
                    acc[h] = acc[h] * fade + mixed

            for h in range(heads):
                l = ml[8 + h : 9 + h, :]
                some = l > 0.0
                lse = jnp.where(
                    some, ml[h : h + 1, :] * scale + jnp.log(jnp.where(some, l, 1.0)), NEG
                )
                inv = jnp.where(some, 1.0 / jnp.where(some, l, 1.0), 0.0)
                out[tile, h * DH : (h + 1) * DH, :] = (acc[h] * inv).astype(jnp.bfloat16)
                ml[h : h + 1, :] = lse
            a, b, c = split3(ml[0:8, :])
            out[tile, heads * DH : heads * DH + 8, :] = a
            out[tile, heads * DH + 8 : heads * DH + 16, :] = b
            out[tile, heads * DH + 16 : heads * DH + 24, :] = c
            out[tile, heads * DH + 24 : heads * DH + 32, :] = c


def attend(counts, lists, qs, kv):
    blocks, heads = kv.shape[:2]
    rows = heads * DH + 32
    return pl.pallas_call(
        attend_kernel,
        out_shape=jax.ShapeDtypeStruct((16, rows, TILE), jnp.bfloat16),
        in_specs=[pl.BlockSpec(memory_space=pltpu.SMEM)] * 2
        + [pl.BlockSpec(memory_space=pltpu.VMEM)] * 5,
        out_specs=pl.BlockSpec(memory_space=pltpu.VMEM),
        scratch_shapes=[
            pltpu.VMEM((heads, DH, TILE), jnp.float32),
            pltpu.VMEM((16, TILE), jnp.float32),
        ],
        compiler_params=pltpu.CompilerParams(vmem_limit_bytes=48 << 20),
        name="attend",
    )(counts, lists, *qs, kv)


def combine_kernel(p0, p1, p2, p3, out):
    parts = (p0, p1, p2, p3)
    heads = out.shape[1] // DH
    base = heads * DH
    for t in range(out.shape[0] // TILE):
        lses = []
        for p in parts:
            x = p[t, base : base + 24, :].astype(jnp.float32)
            lses.append(x[0:8] + x[8:16] + x[16:24])
        top = jnp.maximum(jnp.maximum(lses[0], lses[1]), jnp.maximum(lses[2], lses[3]))
        ws = [jnp.exp(x - top) for x in lses]
        inv = 1.0 / (ws[0] + ws[1] + ws[2] + ws[3])
        ws = [w * inv for w in ws]
        for h in range(heads):
            total = None
            for p, w in zip(parts, ws):
                x = p[t, h * DH : (h + 1) * DH, :].astype(jnp.float32) * w[h : h + 1, :]
                total = x if total is None else total + x
            out[t * TILE : (t + 1) * TILE, h * DH : (h + 1) * DH] = total.T.astype(jnp.bfloat16)


def combine(parts):
    tiles, rows, _ = parts[0].shape
    width = rows - 32
    return pl.pallas_call(
        combine_kernel,
        out_shape=jax.ShapeDtypeStruct((tiles * TILE, width), jnp.bfloat16),
        in_specs=[pl.BlockSpec(memory_space=pltpu.VMEM)] * 4,
        out_specs=pl.BlockSpec(memory_space=pltpu.VMEM),
        name="combine",
    )(*parts)


def block_lists(meta):
    yh, yl = lax.axis_index("yh"), lax.axis_index("yl")
    ids = meta[:, : 4 * SEL].reshape(-1, SEL)
    offsets = meta[:, 4 * SEL : 4 * SEL + 4].reshape(-1, 1)
    owners, slots = ids // CB_DEV, ids % CB_DEV
    n_owner = lax.axis_size("z") * lax.axis_size("core")
    here = (owners // n_owner == yh) & (slots % 2 == yl)
    local = (owners % n_owner) * HALF + slots // 2
    near = jnp.arange(HALF, dtype=jnp.int32)[None, :]
    seen = (near * 2 + yl < CB_DEV - offsets) & (yh == lax.axis_size("yh") - 1)
    near = jnp.broadcast_to((n_owner - 1) * HALF + near, seen.shape)
    here = jnp.concatenate([here, seen], axis=1)
    local = jnp.concatenate([local, near], axis=1)
    width = here.shape[1]
    order = jnp.arange(width, dtype=jnp.int32)
    place = jnp.sum(here[:, None, :] & (order[None, :] < order[:, None])[None], axis=2)
    hit = here[:, None, :] & (place[:, None, :] == order[None, :, None])
    lists = jnp.sum(jnp.where(hit, local[:, None, :], 0), axis=2)
    lists = jnp.pad(lists, ((0, 0), (0, 32 - width)))
    return jnp.sum(here, axis=1).astype(jnp.int32), lists.astype(jnp.int32)


def shards(queries, kv_cache, out_weight, fetch_list, tile_lists, event_offsets):
    yl, x = lax.axis_index("yl"), lax.axis_index("x")
    width = kv_cache.shape[2]
    heads = width // DH
    mine = kv_cache.reshape(HALF, 2, BLK, 2, heads, DH)
    mine = lax.dynamic_index_in_dim(mine, yl, axis=1, keepdims=False)
    keys = mine[:, :, 0].transpose(0, 2, 1, 3)
    values = mine[:, :, 1].transpose(0, 2, 3, 1)
    squares = jnp.stack([keys, values], axis=2)
    column = lax.all_gather(squares, ("z", "core"), axis=0, tiled=True)

    ids = jnp.take(fetch_list[0], tile_lists, axis=0)
    meta = jnp.concatenate([ids.reshape(-1), event_offsets, jnp.zeros((60,), jnp.int32)])[None]
    metas, qs = [meta], [queries]
    for r in range(1, N_COL):
        metas.append(lax.ppermute(meta, COLUMN, shift(N_COL, r)))
        qs.append(lax.ppermute(queries, COLUMN, shift(N_COL, r)))
    counts, lists = block_lists(jnp.concatenate(metas, axis=0))

    out_cols = out_weight.shape[1] // N_X
    pieces = out_weight.reshape(width, N_X, out_cols)
    weights = [lax.dynamic_index_in_dim(pieces, x, axis=1, keepdims=False)]
    for r in range(1, N_X):
        piece = lax.dynamic_index_in_dim(pieces, (x + r) % N_X, axis=1, keepdims=False)
        weights.append(lax.ppermute(piece, "x", shift(N_X, r)))
    weights = jnp.concatenate(weights, axis=0)

    partial = attend(counts, lists, qs, column)
    parts = [partial[0:4]]
    for r in range(1, N_COL):
        parts.append(lax.ppermute(partial[4 * r : 4 * r + 4], COLUMN, shift(N_COL, -r)))
    attended = combine(parts)
    rows = [attended]
    for r in range(1, N_X):
        rows.append(lax.ppermute(attended, "x", shift(N_X, r)))
    rows = jnp.concatenate(rows, axis=1)
    return jnp.dot(rows, weights, preferred_element_type=jnp.float32).astype(jnp.bfloat16)


def solution(mesh):
    fine = Mesh(mesh.devices.reshape(2, 8, 2, N_X, 2), ("yh", "z", "core", "x", "yl"))
    tm = ("yh", "z", "core")
    placed = (
        P((*tm, "yl"), "x"),
        P(tm, None, "x"),
        P("x", None),
        P((*tm, "yl"), None),
        P((*tm, "yl"), None),
        P((*tm, "yl")),
    )
    return jax.shard_map(
        shards, mesh=fine, in_specs=placed, out_specs=P((*tm, "yl"), "x"), check_vma=False
    )
```

time: 601 us -> 201 us (0.33)
  waiting for transfers between devices: 389 us -> 90.3 us
  local copies, waits for them, and re-layouts: 97.5 us -> 16.3 us
  blocking collectives: 39.5 us -> 0 us
  Pallas kernels: 0 us -> 30.4 us
  starting transfers between devices: 10 us -> 39.9 us
  other arithmetic: 30.8 us -> 3.71 us
  matrix products: 18.6 us -> 3.96 us
    psum x1 -> x0, waiting for transfers between devices: 338 us -> none  [from_root(): return lax.psum(jnp.where(mine, shard, jnp.zeros_like(shard)), axis)]
    gather x5 -> x2, local copies, waits for them, and re-layouts: 66.8 us -> 0.86 us  [shards(): ids = jnp.take(fetch_list[0], tile_lists, axis=0)]
    reduce_scatter x1 -> x0, waiting for transfers between devices: 51 us -> none  [shards(): lax.psum_scatter(partial_value.astype(jnp.bfloat16), 'head', scatter_dime...]
    all_gather x0 -> x1, waiting for transfers between devices: none -> 48.9 us  [shards(): column = lax.all_gather(squares, ('z', 'core'), axis=0, tiled=True)]
    ppermute x0 -> x15, waiting for transfers between devices: none -> 41.4 us  [the longest x3 14 us: shards(): rows.append(lax.ppermute(attended, 'x', shift(N_X, r)))]
    ppermute x0 -> x15, starting transfers between devices: none -> 39.9 us  [the longest x3 20.2 us: shards(): lax.ppermute(partial[4 * r:4 * r + 4], COLUMN, shift(N_COL, -r))]
    all_gather x1 -> x0, blocking collectives: 39.5 us -> none  [shards(): requests = lax.all_gather(fetch_list, 'tm', axis=0, tiled=True)]
    pallas_call x0 -> x2, Pallas kernels: none -> 30.4 us  [the longest x1 27.8 us: attend(): pl.pallas_call(attend_kernel, out_shape=jax.ShapeDtypeStruct((16, rows, T...]
  transfers between devices with their start and end apart: 3 -> 16, of which waited for: 2 -> 8; matrix products, arithmetic and copies ran while one was open for 2% -> 5% of each run, Pallas kernels for 0% -> 1%
where the time goes in v1:
time: 201 us; the launch traced here: 198 us
  waiting for transfers between devices  90.3 us (45%)
  starting transfers between devices  39.9 us (20%)
  Pallas kernels  30.4 us (15%)
  local copies, waits for them, and re-layouts  16.3 us (8%)
  between operations  13.6 us (7%)
  matrix products  3.96 us (2%)
  other arithmetic  3.71 us (2%)
    all_gather x1, waiting for transfers between devices, shards(): column = lax.all_gather(squares, ('z', 'core'), axis=0, tiled=True)  48.9 us
    pallas_call x1, Pallas kernels, attend(): pl.pallas_call(attend_kernel, out_shape=jax.ShapeDtypeStruct((16, rows, T...  27.8 us
    ppermute x3, starting transfers between devices, shards(): lax.ppermute(partial[4 * r:4 * r + 4], COLUMN, shift(N_COL, -r))  20.2 us
    ppermute x3, waiting for transfers between devices, shards(): rows.append(lax.ppermute(attended, 'x', shift(N_X, r)))  14 us
    ppermute x3, waiting for transfers between devices, shards(): lax.ppermute(partial[4 * r:4 * r + 4], COLUMN, shift(N_COL, -r))  13 us
    ppermute x3, waiting for transfers between devices, shards(): qs.append(lax.ppermute(queries, COLUMN, shift(N_COL, r)))  9.76 us
    unnamed x14, local copies, waits for them, and re-layouts  6.16 us
    ppermute x3, starting transfers between devices, shards(): weights.append(lax.ppermute(piece, 'x', shift(N_X, r)))  5.85 us
  transfers between devices with their start and end apart: 16, of which 8 were waited for; matrix products, arithmetic and copies ran while one was open for 5% of the time, Pallas kernels for 1%

profile of v1, /device:TPU:64, one launch (start us, length us, event | category | flops | bytes accessed | tf_op | source)
XLA Modules:
  0.0 198.2 jit_solution(12122340264682997080)
XLA Ops:
  6.5 3.6 %copy.38 = bf16[1024,2,384]{0,2,1:T(8,128)(2,1)S(1)} copy(bf16[1024,2,384]{2,1,0:T(2,128)(2,1)} %param.7) | data formatting | bytes 3145728 | tf_op args[1]
  10.1 1.1 reshape.57
  11.3 1.6 constant_dynamic-slice_fusion.4
  12.9 1.5 copy.39
  14.4 0.2 copy.49
  14.8 1.2 copy.41
  16.2 0.8 gather_fusion
  17.2 1.6 collective-permute-start
  18.8 2.9 %collective-permute-start.1 = (s32[1,128]{1,0:T(1,128)S(1)}, s32[1,128]{1,0:T(1,128)}, u32[]{:S(2)}, u32[]{:S(2)}) collective-permute-start(s32[1,128]{1,0:T(1,128)S(1)} %add_bitcast_fusion), channel_id=1, source_target_pairs={{0,128},{1,129},{128,0},{129,1},{2,130},{3,131},{130,2},{131,3},{4... | collective-permute-start | bytes 1544 | tf_op jit(solution)/shard_map/ppermute | solution.py:196
  21.7 1.3 collective-permute-start.2
  23.1 0.7 collective-permute-start.3
  23.7 0.8 collective-permute-start.4
  24.5 0.5 multiply_add_fusion
  25.0 0.6 iota_add_fusion
  25.6 0.7 pad.16.clone
  26.3 2.5 %copy.42 = bf16[384,3072]{0,1:T(8,128)(2,1)} copy(bf16[384,3072]{1,0:T(8,128)(2,1)S(1)} %copy-done.3) | data formatting | bytes 4718592 | tf_op args[2]
  28.9 1.9 collective-permute-start.5
  30.7 0.7 pad_add_fusion.2
  31.7 0.7 compare_and_fusion
  32.3 0.2 convert_reduce_fusion.1
  32.6 0.4 convert_reduce_fusion
  33.1 0.4 select_reduce_fusion
  33.6 9.1 %collective-permute-done.3.q1 = bf16[512,384]{1,0:T(8,128)(2,1)S(1)} collective-permute-done((bf16[512,384]{1,0:T(8,128)(2,1)S(1)}, bf16[512,384]{1,0:T(8,128)(2,1)S(1)}, u32[]{:S(2)}, u32[]{:S(2)}) %collective-permute-start.3) | collective-permute-done | bytes 393248 | tf_op jit(solution)/shard_map/ppermute | solution.py:197
  42.7 0.6 collective-permute-done.5.q3
  43.3 48.9 %all-gather.2.cloned.1.call-done.kv = bf16[64,3,2,128,128]{4,3,2,1,0:T(8,128)(2,1)} async-done(((bf16[4,3,2,128,128]{4,3,2,1,0:T(8,128)(2,1)}), bf16[64,3,2,128,128]{4,3,2,1,0:T(8,128)(2,1)}) %all-gather.2.cloned.1.call-update) | async-done | bytes 12582928 | tf_op jit(solution)/shard_map/all_gather | solution.py:190
  92.2 27.8 %attend.1 = bf16[16,416,128]{2,1,0:T(8,128)(2,1)S(1)} custom-call(s32[16]{0:T(128)S(1)} %get-tuple-element.5.counts, s32[16,32]{1,0:T(8,128)S(1)} %pad.4.lists, bf16[512,384]{1,0:T(8,128)(2,1)S(1)} %copy-done.1, bf16[512,384]{1,0:T(8,128)(2,1)S(1)} %collective-permute-done.3.q1, bf16[512,384]{1,0:T(8,128)(2,1)S(1)} %collective-permute-done.4.q2, ...), custom_call_target="tpu_custom_call" | custom-call | tf_op jit(solution)/shard_map/attend/pallas_call | solution.py:111
  120.1 1.1 fusion.33
  121.2 7.2 %collective-permute-start.6 = (bf16[4,416,128]{2,1,0:T(8,128)(2,1)}, bf16[4,416,128]{2,1,0:T(8,128)(2,1)}, u32[]{:S(2)}, u32[]{:S(2)}) collective-permute-start(bf16[4,416,128]{2,1,0:T(8,128)(2,1)} %get-tuple-element.13), channel_id=1, source_target_pairs={{0,129},{1,0},{128,1},{129,128},{2,131},{3,2},{130,3},{131,130},{4... | collective-permute-start | bytes 1277960 | tf_op jit(solution)/shard_map/ppermute | solution.py:211
  128.4 0.2 constant_dynamic-slice_fusion.3
  128.6 0.3 copy.44
  128.9 1.5 collective-permute-start.12
  130.5 12.5 %collective-permute-start.7 = (bf16[4,416,128]{2,1,0:T(8,128)(2,1)}, bf16[4,416,128]{2,1,0:T(8,128)(2,1)}, u32[]{:S(2)}, u32[]{:S(2)}) collective-permute-start(bf16[4,416,128]{2,1,0:T(8,128)(2,1)} %get-tuple-element.12), channel_id=1, source_target_pairs={{0,128},{1,129},{128,0},{129,1},{2,130},{3,131},{130,2},{131,3},{4... | collective-permute-start | bytes 1277960 | tf_op jit(solution)/shard_map/ppermute | solution.py:211
  143.0 0.4 collective-permute-start.8
  143.4 0.3 copy.45
  143.7 2.8 %collective-permute-start.13 = (bf16[384,768]{1,0:T(8,128)(2,1)S(1)}, bf16[384,768]{1,0:T(8,128)(2,1)}, u32[]{:S(2)}, u32[]{:S(2)}) collective-permute-start(bf16[384,768]{1,0:T(8,128)(2,1)S(1)} %bitcast.32), channel_id=1, source_target_pairs={{0,4},{2,6},{4,0},{6,2},{1,5},{3,7},{5,1},{7,3},{8,12},{10,14},{12... | collective-permute-start | bytes 1769480 | tf_op jit(solution)/shard_map/ppermute | solution.py:205
  146.4 0.3 copy.46
  146.7 1.5 collective-permute-start.14
  148.2 5.8 %collective-permute-done.7.p2 = bf16[4,416,128]{2,1,0:T(8,128)(2,1)} collective-permute-done((bf16[4,416,128]{2,1,0:T(8,128)(2,1)}, bf16[4,416,128]{2,1,0:T(8,128)(2,1)}, u32[]{:S(2)}, u32[]{:S(2)}) %collective-permute-start.7) | collective-permute-done | bytes 426016 | tf_op jit(solution)/shard_map/ppermute | solution.py:211
  154.1 7.2 %collective-permute-done.8.p3 = bf16[4,416,128]{2,1,0:T(8,128)(2,1)} collective-permute-done((bf16[4,416,128]{2,1,0:T(8,128)(2,1)S(1)}, bf16[4,416,128]{2,1,0:T(8,128)(2,1)}, u32[]{:S(2)}, u32[]{:S(2)}) %collective-permute-start.8) | collective-permute-done | bytes 426016 | tf_op jit(solution)/shard_map/ppermute | solution.py:211
  161.2 2.6 %combine.1 = bf16[512,384]{1,0:T(8,128)(2,1)} custom-call(bf16[4,416,128]{2,1,0:T(8,128)(2,1)} %get-tuple-element.14.p0, bf16[4,416,128]{2,1,0:T(8,128)(2,1)} %collective-permute-done.6.p1, bf16[4,416,128]{2,1,0:T(8,128)(2,1)} %collective-permute-done.7.p2, bf16[4,416,128]{2,1,0:T(8,128)(2,1)} %collective-permute-done.8.p3), custom_call_target="tpu_custom_call" | custom-call | tf_op jit(solution)/shard_map/combine/pallas_call | solution.py:150
  163.8 2.7 %collective-permute-start.10 = (bf16[512,384]{1,0:T(8,128)(2,1)}, bf16[512,384]{1,0:T(8,128)(2,1)S(1)}, u32[]{:S(2)}, u32[]{:S(2)}) collective-permute-start(bf16[512,384]{1,0:T(8,128)(2,1)} %combine.1), channel_id=1, source_target_pairs={{0,4},{2,6},{4,0},{6,2},{1,5},{3,7},{5,1},{7,3},{8,12},{10,14},{12... | collective-permute-start | bytes 1179656 | tf_op jit(solution)/shard_map/ppermute | solution.py:215
  166.5 1.5 collective-permute-start.11
  168.0 0.6 collective-permute-start.9
  168.6 0.3 copy.43
  168.8 4.5 %collective-permute-done.14 = bf16[384,768]{1,0:T(8,128)(2,1)} collective-permute-done((bf16[384,768]{1,0:T(8,128)(2,1)S(1)}, bf16[384,768]{1,0:T(8,128)(2,1)}, u32[]{:S(2)}, u32[]{:S(2)}) %collective-permute-start.14) | collective-permute-done | bytes 589856 | tf_op jit(solution)/shard_map/ppermute | solution.py:205
  173.4 4.2 %collective-permute-done.10 = bf16[512,384]{1,0:T(8,128)(2,1)S(1)} collective-permute-done((bf16[512,384]{1,0:T(8,128)(2,1)}, bf16[512,384]{1,0:T(8,128)(2,1)S(1)}, u32[]{:S(2)}, u32[]{:S(2)}) %collective-permute-start.10) | collective-permute-done | bytes 393248 | tf_op jit(solution)/shard_map/ppermute | solution.py:215
  177.6 9.8 %collective-permute-done.11 = bf16[512,384]{1,0:T(8,128)(2,1)} collective-permute-done((bf16[512,384]{1,0:T(8,128)(2,1)}, bf16[512,384]{1,0:T(8,128)(2,1)}, u32[]{:S(2)}, u32[]{:S(2)}) %collective-permute-start.11) | collective-permute-done | bytes 393248 | tf_op jit(solution)/shard_map/ppermute | solution.py:215
  187.4 4.0 %fusion.15 = bf16[512,768]{1,0:T(8,128)(2,1)} fusion(bf16[384,768]{1,0:T(8,128)(2,1)} %collective-permute-done.14, bf16[384,768]{1,0:T(8,128)(2,1)} %collective-permute-done.13, bf16[384,768]{1,0:T(8,128)(2,1)} %collective-permute-done.12, bf16[384,768]{1,0:T(8,128)(2,1)S(1)} %bitcast.34, bf16[512,384]{1,0:T(8,128)(2,1)} %collective-permute-done.11, ...), kind=kOutput, calls=%fused_computation.16 | convolution fusion | flops 1224081408 | bytes 4718592 | tf_op jit(solution)/shard_map/dot_general | solution.py:217
  (43 shorter events, 1.0 us)
Async XLA Ops:
  6.5 9.6 %copy-start = (s32[1,32]{1,0:T(1,128)S(1)}, s32[1,32]{1,0:T(1,128)}, u32[]{:S(2)}) copy-start(s32[1,32]{1,0:T(1,128)} %param.9) | copy-start | bytes 388
  6.5 85.7 %all-gather.2.cloned.1.call-start = ((), (), s32[]{:S(2)}) async-start(), calls=%async_computation | async-start | bytes 13369344 | tf_op jit(solution)/shard_map/all_gather | solution.py:190
  14.7 1.4 copy-start.4
  14.8 2.3 %copy-start.5 = (s32[4]{0:T(128)S(1)}, s32[4]{0:T(128)}, u32[]{:S(2)}) copy-start(s32[4]{0:T(128)} %param.11) | copy-start | bytes 52
  14.8 8.2 %copy-start.1 = (bf16[512,384]{1,0:T(8,128)(2,1)S(1)}, bf16[512,384]{1,0:T(8,128)(2,1)}, u32[]{:S(2)}) copy-start(bf16[512,384]{1,0:T(8,128)(2,1)} %q0.1) | copy-start | bytes 1179652
  14.8 11.5 %copy-start.3 = (bf16[384,3072]{1,0:T(8,128)(2,1)S(1)}, bf16[384,3072]{1,0:T(8,128)(2,1)}, u32[]{:S(2)}) copy-start(bf16[384,3072]{1,0:T(8,128)(2,1)} %param.8) | copy-start | bytes 7077892
  17.2 11.6 %collective-permute-start = (s32[1,128]{1,0:T(1,128)S(1)}, s32[1,128]{1,0:T(1,128)}, u32[]{:S(2)}, u32[]{:S(2)}) collective-permute-start(s32[1,128]{1,0:T(1,128)S(1)} %add_bitcast_fusion), channel_id=1, source_target_pairs={{0,1},{1,128},{128,129},{129,0},{2,3},{3,130},{130,131},{131,2},{4... | collective-permute-start | bytes 1544 | tf_op jit(solution)/shard_map/ppermute | solution.py:196
  18.8 11.9 %collective-permute-start.1 = (s32[1,128]{1,0:T(1,128)S(1)}, s32[1,128]{1,0:T(1,128)}, u32[]{:S(2)}, u32[]{:S(2)}) collective-permute-start(s32[1,128]{1,0:T(1,128)S(1)} %add_bitcast_fusion), channel_id=1, source_target_pairs={{0,128},{1,129},{128,0},{129,1},{2,130},{3,131},{130,2},{131,3},{4... | collective-permute-start | bytes 1544 | tf_op jit(solution)/shard_map/ppermute | solution.py:196
  21.7 9.0 %collective-permute-start.2 = (s32[1,128]{1,0:T(1,128)S(1)}, s32[1,128]{1,0:T(1,128)}, u32[]{:S(2)}, u32[]{:S(2)}) collective-permute-start(s32[1,128]{1,0:T(1,128)S(1)} %add_bitcast_fusion), channel_id=1, source_target_pairs={{0,129},{1,0},{128,1},{129,128},{2,131},{3,2},{130,3},{131,130},{4... | collective-permute-start | bytes 1544 | tf_op jit(solution)/shard_map/ppermute | solution.py:196
  23.1 19.7 %collective-permute-start.3 = (bf16[512,384]{1,0:T(8,128)(2,1)S(1)}, bf16[512,384]{1,0:T(8,128)(2,1)S(1)}, u32[]{:S(2)}, u32[]{:S(2)}) collective-permute-start(bf16[512,384]{1,0:T(8,128)(2,1)S(1)} %copy-done.1), channel_id=1, source_target_pairs={{0,1},{1,128},{128,129},{129,0},{2,3},{3,130},{130,131},{131,2},{4... | collective-permute-start | bytes 1179656 | tf_op jit(solution)/shard_map/ppermute | solution.py:197
  23.7 19.0 %collective-permute-start.4 = (bf16[512,384]{1,0:T(8,128)(2,1)S(1)}, bf16[512,384]{1,0:T(8,128)(2,1)S(1)}, u32[]{:S(2)}, u32[]{:S(2)}) collective-permute-start(bf16[512,384]{1,0:T(8,128)(2,1)S(1)} %copy-done.1), channel_id=1, source_target_pairs={{0,128},{1,129},{128,0},{129,1},{2,130},{3,131},{130,2},{131,3},{4... | collective-permute-start | bytes 1179656 | tf_op jit(solution)/shard_map/ppermute | solution.py:197
  28.9 14.5 %collective-permute-start.5 = (bf16[512,384]{1,0:T(8,128)(2,1)S(1)}, bf16[512,384]{1,0:T(8,128)(2,1)S(1)}, u32[]{:S(2)}, u32[]{:S(2)}) collective-permute-start(bf16[512,384]{1,0:T(8,128)(2,1)S(1)} %copy-done.1), channel_id=1, source_target_pairs={{0,129},{1,0},{128,1},{129,128},{2,131},{3,2},{130,3},{131,130},{4... | collective-permute-start | bytes 1179656 | tf_op jit(solution)/shard_map/ppermute | solution.py:197
  120.1 8.3 %copy-start.2 = (bf16[384,3072]{0,1:T(8,128)(2,1)S(1)}, bf16[384,3072]{0,1:T(8,128)(2,1)}, u32[]{:S(2)}) copy-start(bf16[384,3072]{0,1:T(8,128)(2,1)} %copy.42) | copy-start | bytes 7077892
  121.2 25.5 %collective-permute-start.6 = (bf16[4,416,128]{2,1,0:T(8,128)(2,1)}, bf16[4,416,128]{2,1,0:T(8,128)(2,1)}, u32[]{:S(2)}, u32[]{:S(2)}) collective-permute-start(bf16[4,416,128]{2,1,0:T(8,128)(2,1)} %get-tuple-element.13), channel_id=1, source_target_pairs={{0,129},{1,0},{128,1},{129,128},{2,131},{3,2},{130,3},{131,130},{4... | collective-permute-start | bytes 1277960 | tf_op jit(solution)/shard_map/ppermute | solution.py:211
  128.9 39.1 %collective-permute-start.12 = (bf16[384,768]{1,0:T(8,128)(2,1)S(1)}, bf16[384,768]{1,0:T(8,128)(2,1)}, u32[]{:S(2)}, u32[]{:S(2)}) collective-permute-start(bf16[384,768]{1,0:T(8,128)(2,1)S(1)} %bitcast.31), channel_id=1, source_target_pairs={{0,2},{2,4},{4,6},{6,0},{1,3},{3,5},{5,7},{7,1},{8,10},{10,12},{12... | collective-permute-start | bytes 1769480 | tf_op jit(solution)/shard_map/ppermute | solution.py:205
  130.5 23.6 %collective-permute-start.7 = (bf16[4,416,128]{2,1,0:T(8,128)(2,1)}, bf16[4,416,128]{2,1,0:T(8,128)(2,1)}, u32[]{:S(2)}, u32[]{:S(2)}) collective-permute-start(bf16[4,416,128]{2,1,0:T(8,128)(2,1)} %get-tuple-element.12), channel_id=1, source_target_pairs={{0,128},{1,129},{128,0},{129,1},{2,130},{3,131},{130,2},{131,3},{4... | collective-permute-start | bytes 1277960 | tf_op jit(solution)/shard_map/ppermute | solution.py:211
  143.0 18.3 %collective-permute-start.8 = (bf16[4,416,128]{2,1,0:T(8,128)(2,1)S(1)}, bf16[4,416,128]{2,1,0:T(8,128)(2,1)}, u32[]{:S(2)}, u32[]{:S(2)}) collective-permute-start(bf16[4,416,128]{2,1,0:T(8,128)(2,1)S(1)} %get-tuple-element.11), channel_id=1, source_target_pairs={{0,1},{1,128},{128,129},{129,0},{2,3},{3,130},{130,131},{131,2},{4... | collective-permute-start | bytes 1277960 | tf_op jit(solution)/shard_map/ppermute | solution.py:211
  143.7 25.2 %collective-permute-start.13 = (bf16[384,768]{1,0:T(8,128)(2,1)S(1)}, bf16[384,768]{1,0:T(8,128)(2,1)}, u32[]{:S(2)}, u32[]{:S(2)}) collective-permute-start(bf16[384,768]{1,0:T(8,128)(2,1)S(1)} %bitcast.32), channel_id=1, source_target_pairs={{0,4},{2,6},{4,0},{6,2},{1,5},{3,7},{5,1},{7,3},{8,12},{10,14},{12... | collective-permute-start | bytes 1769480 | tf_op jit(solution)/shard_map/ppermute | solution.py:205
  146.7 26.7 %collective-permute-start.14 = (bf16[384,768]{1,0:T(8,128)(2,1)S(1)}, bf16[384,768]{1,0:T(8,128)(2,1)}, u32[]{:S(2)}, u32[]{:S(2)}) collective-permute-start(bf16[384,768]{1,0:T(8,128)(2,1)S(1)} %bitcast.33), channel_id=1, source_target_pairs={{0,6},{2,0},{4,2},{6,4},{1,7},{3,1},{5,3},{7,5},{8,14},{10,8},{12,... | collective-permute-start | bytes 1769480 | tf_op jit(solution)/shard_map/ppermute | solution.py:205
  163.8 13.7 %collective-permute-start.10 = (bf16[512,384]{1,0:T(8,128)(2,1)}, bf16[512,384]{1,0:T(8,128)(2,1)S(1)}, u32[]{:S(2)}, u32[]{:S(2)}) collective-permute-start(bf16[512,384]{1,0:T(8,128)(2,1)} %combine.1), channel_id=1, source_target_pairs={{0,4},{2,6},{4,0},{6,2},{1,5},{3,7},{5,1},{7,3},{8,12},{10,14},{12... | collective-permute-start | bytes 1179656 | tf_op jit(solution)/shard_map/ppermute | solution.py:215
  166.5 20.9 %collective-permute-start.11 = (bf16[512,384]{1,0:T(8,128)(2,1)}, bf16[512,384]{1,0:T(8,128)(2,1)}, u32[]{:S(2)}, u32[]{:S(2)}) collective-permute-start(bf16[512,384]{1,0:T(8,128)(2,1)} %combine.1), channel_id=1, source_target_pairs={{0,6},{2,0},{4,2},{6,4},{1,7},{3,1},{5,3},{7,5},{8,14},{10,8},{12,... | collective-permute-start | bytes 1179656 | tf_op jit(solution)/shard_map/ppermute | solution.py:215
  168.0 19.4 %collective-permute-start.9 = (bf16[512,384]{1,0:T(8,128)(2,1)}, bf16[512,384]{1,0:T(8,128)(2,1)S(1)}, u32[]{:S(2)}, u32[]{:S(2)}) collective-permute-start(bf16[512,384]{1,0:T(8,128)(2,1)} %combine.1), channel_id=1, source_target_pairs={{0,2},{2,4},{4,6},{6,0},{1,3},{3,5},{5,7},{7,1},{8,10},{10,12},{12... | collective-permute-start | bytes 1179656 | tf_op jit(solution)/shard_map/ppermute | solution.py:215
Sparse Core Ops, SparseCore 0:
  16.2 76.0 all-gather.1

commit v2 on v0

v2 whole, which is shorter than its diff:
```python
import functools
import math

import jax
import jax.numpy as jnp
from jax import lax
from jax.experimental import pallas as pl
from jax.experimental.pallas import tpu as pltpu
from jax.sharding import Mesh, PartitionSpec as P

DH = 128
TILE = 128
BLK = 128
CB_DEV = 8
SEL = 16
HALF = CB_DEV // 2
PAIR = 2
NEG = -1e30
COLUMN = ("yh", "yl")
N_COL = 4
N_X = 4
N_Z = 8
EXTRA = 16
ITEMS = 256
SPANS = ((0, 16), (16, 32), (32, 48), (48, 56), (56, 64))


def shift(n, by):
    return [(i, (i + by) % n) for i in range(n)]


def hop(x, axis, n, by, name):
    with jax.named_scope("s_" + name):
        return lax.ppermute(x, axis, shift(n, by))


def twin(x, name):
    with jax.named_scope("s_" + name):
        return lax.ppermute(x, "core", [(0, 1), (1, 0)])


def ring(x, name):
    up = [(z * 2, ((z + 1) % N_Z) * 2) for z in range(N_Z)]
    down = [(z * 2 + 1, ((z - 1) % N_Z) * 2 + 1) for z in range(N_Z)]
    with jax.named_scope("s_" + name):
        return lax.ppermute(x, ("z", "core"), up + down)


def after(x, *others):
    return lax.optimization_barrier((x, *others))[0]


def fetch_kernel(parity, kv, out, sems):
    heads = out.shape[1]
    copies = []
    for k in range(HALF):
        rows = pl.ds((2 * k + parity[0]) * BLK, BLK)
        for h in range(heads):
            copies.append(
                pltpu.make_async_copy(
                    kv.at[rows, :, pl.ds(h * DH, DH)], out.at[k, h], sems.at[k * heads + h]
                )
            )
    for copy in copies:
        copy.start()
    for copy in copies:
        copy.wait()


def squares_kernel(rows, out):
    at = lax.broadcasted_iota(jnp.int32, (BLK, 2 * BLK), 0) * 2
    col = lax.broadcasted_iota(jnp.int32, (BLK, 2 * BLK), 1)
    keys = (col == at).astype(jnp.bfloat16)
    values = (col == at + 1).astype(jnp.bfloat16)
    for k in range(out.shape[0]):
        for h in range(out.shape[1]):
            x = rows[k, h]
            out[k, h, 0] = jnp.dot(keys, x, preferred_element_type=jnp.float32).astype(jnp.bfloat16)
            out[k, h, 1] = lax.dot_general(
                x, values, (((0,), (1,)), ((), ())), preferred_element_type=jnp.float32
            ).astype(jnp.bfloat16)


def squares_of(kv_cache, parity):
    heads = kv_cache.shape[2] // DH
    vmem = pl.BlockSpec(memory_space=pltpu.VMEM)
    rows = pl.pallas_call(
        fetch_kernel,
        out_shape=jax.ShapeDtypeStruct((HALF, heads, BLK, 2, DH), jnp.bfloat16),
        in_specs=[pl.BlockSpec(memory_space=pltpu.SMEM), pl.BlockSpec(memory_space=pl.ANY)],
        out_specs=vmem,
        scratch_shapes=[pltpu.SemaphoreType.DMA((HALF * heads,))],
        name="fetch",
    )(parity.reshape(1).astype(jnp.int32), kv_cache)
    return pl.pallas_call(
        squares_kernel,
        out_shape=jax.ShapeDtypeStruct((HALF, heads, 2, BLK, DH), jnp.bfloat16),
        in_specs=[vmem],
        out_specs=vmem,
        name="squares",
    )(rows.reshape(HALF, heads, 2 * BLK, DH))


def attend_kernel(heads, n_kv, spans, first, *refs):
    ends, tiles_of, bases, counts, lists, q = refs[:6]
    kvs = refs[6 : 6 + n_kv]
    refs = refs[6 + n_kv :]
    if not first:
        acc_in, stat_in = refs[:2]
        refs = refs[2:]
    if spans:
        outs = refs[: len(spans)]
        acc, stat, kv, scores, sems = refs[len(spans) :]
    else:
        acc, stat, kv, scores, sems = refs
    scale = 1.0 / math.sqrt(DH)
    scale2 = scale * math.log2(math.e)
    n_heads = len(heads)
    n_tiles = q.shape[0]
    copies, at = [], 0
    for i, ref in enumerate(kvs):
        size = ref.shape[0]
        copies.append(pltpu.make_async_copy(ref, kv.at[pl.ds(at, size)], sems.at[i]))
        at += size
    for copy in copies:
        copy.start()

    @pl.loop(0, n_tiles)
    def _(tile):
        if first:
            acc[tile] = jnp.zeros(acc.shape[1:], jnp.float32)
            stat[tile, 0:8, :] = jnp.full((8, TILE), NEG, jnp.float32)
            stat[tile, 8:16, :] = jnp.zeros((8, TILE), jnp.float32)
        else:
            acc[tile] = acc_in[tile]
            stat[tile] = stat_in[tile]

    acc[n_tiles] = jnp.zeros(acc.shape[1:], jnp.float32)
    stat[n_tiles] = jnp.zeros(stat.shape[1:], jnp.float32)
    for copy in copies:
        copy.wait()

    def blocks_of(item):
        tile = jnp.minimum(tiles_of[item], n_tiles - 1)
        return tile, [lists[tile, bases[item] + k] for k in range(PAIR)]

    def score(item, slot):
        tile, blocks = blocks_of(item)
        for i, h in enumerate(heads):
            for k in range(PAIR):
                scores[slot, i, k] = lax.dot_general(
                    kv[blocks[k], i, 0],
                    q[tile, :, h * DH : (h + 1) * DH],
                    (((1,), (1,)), ((), ())),
                    preferred_element_type=jnp.float32,
                )

    def blend(item, slot):
        target = tiles_of[item]
        tile, blocks = blocks_of(item)
        left = counts[tile] - bases[item]
        lost = [jnp.where(k < left, 0.0, -NEG) for k in range(PAIR)]
        old, sums = stat[target, 0:8, :], stat[target, 8:16, :]
        rows, news, fades, adds, mixes = [], [], [], [], []
        for i in range(n_heads):
            tops = [
                jnp.max(scores[slot, i, k].reshape(BLK // 8, 8, TILE), axis=0) - lost[k]
                for k in range(PAIR)
            ]
            top = jnp.max(functools.reduce(jnp.maximum, tops), axis=0, keepdims=True)
            new = jnp.maximum(old[i : i + 1, :], top)
            news.append(new)
            fades.append(jnp.exp2((old[i : i + 1, :] - new) * scale2))
            weights = [
                jnp.exp2((scores[slot, i, k] - (new + lost[k])) * scale2) for k in range(PAIR)
            ]
            total = functools.reduce(jnp.add, weights).reshape(BLK // 8, 8, TILE)
            adds.append(jnp.sum(jnp.sum(total, axis=0), axis=0, keepdims=True))
            mixes.append(
                functools.reduce(
                    jnp.add,
                    [
                        jnp.dot(
                            kv[blocks[k], i, 1],
                            weights[k].astype(jnp.bfloat16),
                            preferred_element_type=jnp.float32,
                        )
                        for k in range(PAIR)
                    ],
                )
            )
        accs = [acc[target, i] * fades[i] + mixes[i] for i in range(n_heads)]
        for i in range(n_heads):
            acc[target, i] = accs[i]
            stat[target, i : i + 1, :] = news[i]
            stat[target, 8 + i : 9 + i, :] = sums[i : i + 1, :] * fades[i] + adds[i]

    total_items = ends[n_tiles - 1]

    @pl.when(total_items > 0)
    def _():
        score(0, 0)

        @pl.loop(0, (total_items + 1) // 2)
        def _(j):
            score(2 * j + 1, 1)
            blend(2 * j, 0)
            score(2 * j + 2, 0)
            blend(2 * j + 1, 1)

    for (tile0, tiles), out in zip(spans or (), outs if spans else ()):
        finish(n_heads, scale, tile0, tiles, acc, stat, out)


def finish(n_heads, scale, tile0, tiles, acc, stat, out):
    @pl.loop(0, tiles)
    def _(at):
        tile = tile0 + at
        total = stat[tile, 8:16, :]
        some = total > 0.0
        safe = jnp.where(some, total, 1.0)
        lse = jnp.where(some, stat[tile, 0:8, :] * scale + jnp.log(safe), NEG)
        inv = jnp.where(some, 1.0 / safe, 0.0)
        for i in range(n_heads):
            out[at, i * DH : (i + 1) * DH, :] = (acc[tile, i] * inv[i : i + 1, :]).astype(
                jnp.bfloat16
            )
        a = lse.astype(jnp.bfloat16).astype(jnp.float32)
        b = (lse - a).astype(jnp.bfloat16).astype(jnp.float32)
        c = lse - a - b
        stat[tile, 0:4, :] = a[0:4, :]
        stat[tile, 4:8, :] = b[0:4, :]
        stat[tile, 8:12, :] = c[0:4, :]
        stat[tile, 12:16, :] = c[0:4, :]
        out[at, n_heads * DH :, :] = stat[tile].astype(jnp.bfloat16)


def attend(heads, plan, q, kvs, state, spans=None):
    n_heads, tiles = len(heads), q.shape[0]
    first = state is None
    state = () if first else state
    vmem = pl.BlockSpec(memory_space=pltpu.VMEM)
    keep = [(tiles + 1, n_heads, DH, TILE), (tiles + 1, 16, TILE)]
    if spans:
        shapes = tuple(
            jax.ShapeDtypeStruct((n, n_heads * DH + EXTRA, TILE), jnp.bfloat16) for _, n in spans
        )
        scratch = [pltpu.VMEM(shape, jnp.float32) for shape in keep]
    else:
        shapes = tuple(jax.ShapeDtypeStruct(shape, jnp.float32) for shape in keep)
        scratch = []
    blocks = sum(x.shape[0] for x in kvs)
    return pl.pallas_call(
        functools.partial(attend_kernel, heads, len(kvs), spans, first),
        out_shape=shapes,
        in_specs=[pl.BlockSpec(memory_space=pltpu.SMEM)] * 5
        + [vmem]
        + [pl.BlockSpec(memory_space=pl.ANY)] * len(kvs)
        + [vmem] * len(state),
        out_specs=(vmem,) * len(shapes),
        scratch_shapes=[
            *scratch,
            pltpu.VMEM((blocks, n_heads, 2, BLK, DH), jnp.bfloat16),
            pltpu.VMEM((2, n_heads, PAIR, BLK, TILE), jnp.float32),
            pltpu.SemaphoreType.DMA((len(kvs),)),
        ],
        compiler_params=pltpu.CompilerParams(vmem_limit_bytes=14 << 20),
        cost_estimate=pl.CostEstimate(
            flops=blocks * tiles * n_heads * 20_000_000,
            bytes_accessed=blocks * n_heads * 65536,
            transcendentals=0,
        ),
        name="attend",
    )(*plan, q, *kvs, *state)


def blend_parts(parts, tile, heads):
    base = heads * DH
    lses = []
    for p in parts:
        x = p[tile, base : base + EXTRA, :].astype(jnp.float32)
        lses.append(x[0:4] + x[4:8] + x[8:12])
    top = functools.reduce(jnp.maximum, lses)
    ws = [jnp.exp(x - top) for x in lses]
    total = functools.reduce(jnp.add, ws)
    inv = 1.0 / total
    ws = [w * inv for w in ws]
    sums = []
    for h in range(heads):
        xs = [p[tile, h * DH : (h + 1) * DH, :].astype(jnp.float32) for p in parts]
        sums.append(functools.reduce(jnp.add, [x * w[h : h + 1, :] for x, w in zip(xs, ws)]))
    return sums, top + jnp.log(total)


def merge_kernel(a0, a1, b0, b1, out0, out1, stat):
    heads = (out0.shape[1] - EXTRA) // DH
    for parts, out in (((a0, a1), out0), ((b0, b1), out1)):
        for tile in range(out.shape[0]):
            sums, lse = blend_parts(parts, tile, heads)
            for h in range(heads):
                out[tile, h * DH : (h + 1) * DH, :] = sums[h].astype(jnp.bfloat16)
            a = lse.astype(jnp.bfloat16).astype(jnp.float32)
            b = (lse - a).astype(jnp.bfloat16).astype(jnp.float32)
            c = lse - a - b
            stat[0:4, :] = a
            stat[4:8, :] = b
            stat[8:12, :] = c
            stat[12:16, :] = c
            out[tile, heads * DH :, :] = stat[...].astype(jnp.bfloat16)


def merge(a0, a1, b0, b1):
    vmem = pl.BlockSpec(memory_space=pltpu.VMEM)
    return pl.pallas_call(
        merge_kernel,
        out_shape=(jax.ShapeDtypeStruct(a0.shape, a0.dtype),) * 2,
        in_specs=[vmem] * 4,
        out_specs=(vmem, vmem),
        scratch_shapes=[pltpu.VMEM((EXTRA, TILE), jnp.float32)],
        compiler_params=pltpu.CompilerParams(vmem_limit_bytes=8 << 20),
        name="merge",
    )(a0, a1, b0, b1)


def combine_kernel(own, p0, p1, out):
    heads = out.shape[1] // DH
    for tile in range(own.shape[0]):
        sums, _ = blend_parts((own, p0, p1), tile, heads)
        rows = slice(tile * TILE, (tile + 1) * TILE)
        for h in range(heads):
            out[rows, h * DH : (h + 1) * DH] = sums[h].T.astype(jnp.bfloat16)


def combine(own, p0, p1):
    tiles, rows, _ = own.shape
    vmem = pl.BlockSpec(memory_space=pltpu.VMEM)
    return pl.pallas_call(
        combine_kernel,
        out_shape=jax.ShapeDtypeStruct((tiles * TILE, rows - EXTRA), jnp.bfloat16),
        in_specs=[vmem] * 3,
        out_specs=vmem,
        compiler_params=pltpu.CompilerParams(vmem_limit_bytes=8 << 20),
        name="combine",
    )(own, p0, p1)


def project_kernel(n, more, *refs):
    out = refs[-1]
    half = out.shape[0] // 2
    step = 256
    for k in range(2):
        rows = slice(k * half, (k + 1) * half)
        for c in range(0, out.shape[1], step):
            cols = slice(c, c + step)
            parts = [
                jnp.dot(
                    refs[2 * i + k][...],
                    refs[2 * n + i][:, cols],
                    preferred_element_type=jnp.float32,
                )
                for i in range(n)
            ]
            if more:
                parts.append(refs[3 * n][rows, cols])
            out[rows, cols] = functools.reduce(jnp.add, parts).astype(out.dtype)


def project(pairs, weights, total=None):
    rows, cols = 2 * pairs[0][0].shape[0], weights[0].shape[1]
    more = () if total is None else (total,)
    flat = [x for pair in pairs for x in pair]
    vmem = pl.BlockSpec(memory_space=pltpu.VMEM)
    return pl.pallas_call(
        functools.partial(project_kernel, len(pairs), bool(more)),
        out_shape=jax.ShapeDtypeStruct((rows, cols), jnp.bfloat16 if more else jnp.float32),
        in_specs=[vmem] * (len(flat) + len(weights) + len(more)),
        out_specs=vmem,
        compiler_params=pltpu.CompilerParams(vmem_limit_bytes=14 << 20),
        cost_estimate=pl.CostEstimate(flops=10**9, bytes_accessed=4 << 20, transcendentals=0),
        name="project",
    )(*flat, *weights, *more)


def block_lists(meta):
    yh, yl = lax.axis_index("yh"), lax.axis_index("yl")
    z, core = lax.axis_index("z"), lax.axis_index("core")
    ids = meta[:, : 4 * SEL].reshape(-1, SEL)
    offsets = meta[:, 4 * SEL : 4 * SEL + 4].reshape(-1, 1)
    n_owner = N_Z * 2
    owners, slots = ids // CB_DEV, ids % CB_DEV
    here = (owners // n_owner == yh) & (slots % 2 == yl)
    near = jnp.arange(HALF, dtype=jnp.int32)[None, :]
    seen = (near * 2 + yl < CB_DEV - offsets) & (yh == lax.axis_size("yh") - 1)
    here = jnp.concatenate([here, seen], axis=1)
    owners = jnp.concatenate([owners % n_owner, jnp.full(seen.shape, n_owner - 1, jnp.int32)], axis=1)
    half = jnp.concatenate([slots // 2, jnp.broadcast_to(near, seen.shape)], axis=1)
    dist = (owners // 2 - z) % N_Z
    other = jnp.where(owners % 2 != core, 1, 0)
    ahead = dist < N_Z // 2
    step = jnp.where(ahead, dist, N_Z - dist)
    this_ring = ahead == (core == 1)
    mid = CB_DEV + 16 * (step - 1)
    mid = mid + jnp.where(this_ring, other * 8, HALF + (1 - other) * 8)
    place = jnp.where(dist == 0, other * HALF, jnp.where(dist == N_Z // 2, 56 + other * HALF, mid)) + half
    width = here.shape[1]
    order = jnp.arange(width, dtype=jnp.int32)
    lo = jnp.array([a for a, _ in SPANS], jnp.int32)[:, None, None]
    hi = jnp.array([b for _, b in SPANS], jnp.int32)[:, None, None]
    here = here[None] & (place[None] >= lo) & (place[None] < hi)
    place = place[None] - lo
    rank = jnp.sum(here[..., None, :] & (order[None, :] < order[:, None]), axis=-1)
    hit = here[..., None, :] & (rank[..., None, :] == order[:, None])
    lists = jnp.sum(jnp.where(hit, place[..., None, :], 0), axis=-1)
    lists = jnp.pad(lists, ((0, 0), (0, 0), (0, 24 - width)))
    counts = jnp.sum(here, axis=-1).astype(jnp.int32)
    return [work(counts[i], lists[i].astype(jnp.int32)) for i in range(len(SPANS))]


def work(counts, lists):
    tiles = counts.shape[0]
    pairs = (counts + PAIR - 1) // PAIR
    order = jnp.arange(tiles, dtype=jnp.int32)
    ends = jnp.sum(jnp.where(order[None, :] <= order[:, None], pairs[None, :], 0), axis=1)
    items = jnp.arange(ITEMS, dtype=jnp.int32)
    past = items[None, :] >= ends[:, None]
    tile_of = jnp.sum(past, axis=0).astype(jnp.int32)
    before = jnp.sum(jnp.where(past, pairs[:, None], 0), axis=0)
    bases = jnp.where(tile_of < tiles, (items - before) * PAIR, 0)
    return ends, tile_of, bases, counts, lists


def shards(queries, kv_cache, out_weight, fetch_list, tile_lists, event_offsets):
    yl, x = lax.axis_index("yl"), lax.axis_index("x")
    width = kv_cache.shape[2]
    mine = squares_of(kv_cache, yl)

    q_back = hop(queries, COLUMN, N_COL, 1, "q_back")
    q_next = hop(queries, COLUMN, N_COL, -1, "q_next")

    heads = (0, 1, 2)
    tw = twin(mine, "tw")
    a1 = ring(after(mine, tw), "a1")
    b1 = ring(tw, "b1")
    out_cols = out_weight.shape[1] // N_X
    out_weight = after(out_weight, tw)
    pieces = jnp.stack([out_weight[:, r * out_cols : (r + 1) * out_cols] for r in range(N_X)])
    by_peer = lax.all_to_all(pieces, "x", split_axis=0, concat_axis=0, tiled=True)
    weights = [
        lax.dynamic_index_in_dim(by_peer, (x - r) % N_X, axis=0, keepdims=False)
        for r in range(N_X)
    ]

    ids = jnp.take(after(fetch_list, a1)[0], tile_lists, axis=0)
    meta = jnp.concatenate([ids.reshape(-1), event_offsets, jnp.zeros((60,), jnp.int32)])[None]
    metas = [meta, *(hop(meta, COLUMN, N_COL, r, "meta") for r in range(1, N_COL))]
    plans = block_lists(jnp.concatenate(metas, axis=0))
    q_far = hop(after(q_back, a1), COLUMN, N_COL, 1, "q_far")
    q = jnp.concatenate([queries, q_back, q_far, q_next], axis=0)
    q = q.reshape(N_COL * 4, TILE, width)

    a2 = ring(after(a1, pieces), "a2")
    state = attend(heads, plans[0], q, [mine, tw, a1, twin(a1, "ta1")], None)
    b2 = ring(b1, "b2")
    a3 = ring(after(a2, state[1]), "a3")
    state = attend(heads, plans[1], q, [b1, twin(b1, "tb1"), a2, twin(a2, "ta2")], state)
    b3 = ring(b2, "b3")
    a4 = ring(after(a3, state[1]), "a4")
    state = attend(heads, plans[2], q, [b2, twin(b2, "tb2"), a3, twin(a3, "ta3")], state)
    state = attend(heads, plans[3], q, [b3, twin(b3, "tb3")], state)
    a4 = after(a4, state[1], *weights)
    ends = [a4, twin(a4, "ta4")]

    far0, far1, prv0, prv1, nxt0, nxt1, near0, near1 = attend(
        heads, plans[4], q, ends, state, tuple((t, 2) for t in (8, 10, 12, 14, 4, 6, 0, 2))
    )
    far0, far1 = hop(far0, COLUMN, N_COL, 1, "f0"), hop(far1, COLUMN, N_COL, -1, "f1")
    prv1, nxt0 = hop(prv1, COLUMN, N_COL, 1, "prv1"), hop(nxt0, COLUMN, N_COL, -1, "nxt0")
    prv0, nxt1 = merge(far0, prv0, far1, nxt1)
    prv0, nxt1 = hop(prv0, COLUMN, N_COL, 1, "prv0"), hop(nxt1, COLUMN, N_COL, -1, "nxt1")
    rows0, rows1 = combine(near0, prv0, nxt0), combine(near1, prv1, nxt1)

    left0, right1 = hop(rows0, "x", N_X, 1, "left0"), hop(rows1, "x", N_X, -1, "right1")
    left1, right0 = hop(rows1, "x", N_X, 1, "left1"), hop(rows0, "x", N_X, -1, "right0")
    far0, far1 = hop(left0, "x", N_X, 1, "l2"), hop(right1, "x", N_X, -1, "r2")
    total = project(
        [(rows0, rows1), (left0, left1), (right0, right1)], [weights[r] for r in (0, 1, 3)]
    )
    return project([(far0, far1)], [weights[2]], total)


def solution(mesh):
    fine = Mesh(mesh.devices.reshape(2, N_Z, 2, N_X, 2), ("yh", "z", "core", "x", "yl"))
    tm = ("yh", "z", "core")
    placed = (
        P((*tm, "yl"), "x"),
        P(tm, None, "x"),
        P("x", None),
        P((*tm, "yl"), None),
        P((*tm, "yl"), None),
        P((*tm, "yl")),
    )
    return jax.shard_map(
        shards, mesh=fine, in_specs=placed, out_specs=P((*tm, "yl"), "x"), check_vma=False
    )
```

time: 601 us -> 140 us (0.23)
  the two profiles are of different devices: /device:TPU:64 before, /device:TPU:32 now
where the time goes in v2:
time: 140 us; the launch traced here: 138 us
  starting transfers between devices  58.6 us (42%)
  Pallas kernels  34.6 us (25%)
  waiting for transfers between devices  31 us (22%)
  other arithmetic  8.55 us (6%)
  local copies, waits for them, and re-layouts  5.18 us (4%)
    ppermute x18, starting transfers between devices, hop(): return lax.ppermute(x, axis, shift(n, by))  37.4 us
    pallas_call x5, Pallas kernels, attend(): pl.pallas_call(functools.partial(attend_kernel, heads, len(kvs), spans, f...  26.1 us
    ppermute x18, waiting for transfers between devices, hop(): return lax.ppermute(x, axis, shift(n, by))  17.8 us
    ppermute x7, starting transfers between devices, ring(): return lax.ppermute(x, ('z', 'core'), up + down)  13.6 us
    ppermute x7, waiting for transfers between devices, ring(): return lax.ppermute(x, ('z', 'core'), up + down)  11.4 us
    all_to_all x1, starting transfers between devices, shards(): lax.all_to_all(pieces, 'x', split_axis=0, concat_axis=0, tiled=True)  4.63 us
    ppermute x8, starting transfers between devices, twin(): return lax.ppermute(x, 'core', [(0, 1), (1, 0)])  2.92 us
    pallas_call x2, Pallas kernels, project(): pl.pallas_call(functools.partial(project_kernel, len(pairs), bool(more)),...  2.88 us
  transfers between devices with their start and end apart: 34, of which 13 were waited for; matrix products, arithmetic and copies ran while one was open for 9% of the time, Pallas kernels for 18%

profile of v2, /device:TPU:32, one launch (start us, length us, event | category | flops | bytes accessed | tf_op | source)
XLA Modules:
  0.0 138.2 jit_solution(516917908013536323)
XLA Ops:
  0.0 2.3 %fetch.1 = bf16[4,3,128,2,128]{4,3,2,1,0:T(2,128)(2,1)} custom-call(s32[1]{0:T(128)} %bitcast.parity, bf16[1024,2,384]{2,1,0:T(2,128)(2,1)} %kv.1), custom_call_target="tpu_custom_call" | custom-call | tf_op jit(solution)/shard_map/fetch/pallas_call | solution.py:87
  2.3 2.6 %squares.1.refs_6_ = bf16[4,3,2,128,128]{4,3,2,1,0:T(8,128)(2,1)} custom-call(bf16[4,3,256,128]{3,2,1,0:T(8,128)(2,1)} %bitcast.69), custom_call_target="tpu_custom_call" | custom-call | tf_op jit(solution)/shard_map/squares/pallas_call | solution.py:95
  4.9 1.6 %collective-permute-start.5 = (bf16[512,384]{1,0:T(8,128)(2,1)}, bf16[512,384]{1,0:T(8,128)(2,1)}, u32[]{:S(2)}, u32[]{:S(2)}) collective-permute-start(bf16[512,384]{1,0:T(8,128)(2,1)} %param.8), channel_id=1, source_target_pairs={{0,1},{1,128},{128,129},{129,0},{2,3},{3,130},{130,131},{131,2},{4... | collective-permute-start | bytes 1179656 | tf_op jit(solution)/shard_map/s_q_back/ppermute | solution.py:34
  6.5 1.7 %collective-permute-start.7 = (bf16[512,384]{1,0:T(8,128)(2,1)}, bf16[512,384]{1,0:T(8,128)(2,1)}, u32[]{:S(2)}, u32[]{:S(2)}) collective-permute-start(bf16[512,384]{1,0:T(8,128)(2,1)} %param.8), channel_id=1, source_target_pairs={{0,129},{1,0},{128,1},{129,128},{2,131},{3,2},{130,3},{131,130},{4... | collective-permute-start | bytes 1179656 | tf_op jit(solution)/shard_map/s_q_next/ppermute | solution.py:34
  8.2 2.0 %collective-permute-start.1 = (bf16[4,3,2,128,128]{4,3,2,1,0:T(8,128)(2,1)}, bf16[4,3,2,128,128]{4,3,2,1,0:T(8,128)(2,1)}, u32[]{:S(2)}, u32[]{:S(2)}) collective-permute-start(bf16[4,3,2,128,128]{4,3,2,1,0:T(8,128)(2,1)} %squares.1.refs_6_), channel_id=1, source_target_pairs={{0,16},{16,32},{32,48},{48,64},{64,80},{80,96},{96,112},{112,0},{8... | collective-permute-start | bytes 2359304 | tf_op jit(solution)/shard_map/s_a1/ppermute | solution.py:46
  10.3 2.0 %collective-permute-start.11 = (bf16[4,3,2,128,128]{4,3,2,1,0:T(8,128)(2,1)S(1)}, bf16[4,3,2,128,128]{4,3,2,1,0:T(8,128)(2,1)}, u32[]{:S(2)}, u32[]{:S(2)}) collective-permute-start(bf16[4,3,2,128,128]{4,3,2,1,0:T(8,128)(2,1)S(1)} %collective-permute-done.refs_7_), channel_id=1, source_target_pairs={{0,16},{16,32},{32,48},{48,64},{64,80},{80,96},{96,112},{112,0},{8... | collective-permute-start | bytes 2359304 | tf_op jit(solution)/shard_map/s_b1/ppermute | solution.py:46
  12.4 1.7 %pad_maximum_fusion = bf16[4,384,768]{2,1,0:T(8,128)(2,1)} fusion(bf16[1,384,768]{2,1,0:T(8,128)(2,1)S(1)} %get-tuple-element.74, bf16[1,384,768]{2,1,0:T(8,128)(2,1)S(1)} %get-tuple-element.75, bf16[1,384,768]{2,1,0:T(8,128)(2,1)S(1)} %get-tuple-element.76, bf16[1,384,768]{2,1,0:T(8,128)(2,1)S(1)} %get-tuple-element.73), kind=kLoop, calls=%fused_computation.1 | loop fusion | flops 3538944 | bytes 4718592 | tf_op jit(solution)/shard_map/stack | solution.py:446
  14.1 4.6 %all-to-all-start = ((bf16[4,384,768]{2,1,0:T(8,128)(2,1)}), bf16[4,384,768]{2,1,0:T(8,128)(2,1)}, u32[]{:S(2)}, u32[]{:S(2)}) async-start(bf16[4,384,768]{2,1,0:T(8,128)(2,1)} %pad_maximum_fusion), calls=%async_computation | async-start | bytes 4718592 | tf_op jit(solution)/shard_map/all_to_all | solution.py:447
  18.8 1.8 %collective-permute-done.1.refs_8_ = bf16[4,3,2,128,128]{4,3,2,1,0:T(8,128)(2,1)} collective-permute-done((bf16[4,3,2,128,128]{4,3,2,1,0:T(8,128)(2,1)}, bf16[4,3,2,128,128]{4,3,2,1,0:T(8,128)(2,1)}, u32[]{:S(2)}, u32[]{:S(2)}) %collective-permute-start.1) | collective-permute-done | bytes 786464 | tf_op jit(solution)/shard_map/s_a1/ppermute | solution.py:46
  22.3 2.9 %collective-permute-start.3 = (s32[1,128]{1,0:T(1,128)S(1)}, s32[1,128]{1,0:T(1,128)S(1)}, u32[]{:S(2)}, u32[]{:S(2)}) collective-permute-start(s32[1,128]{1,0:T(1,128)S(1)} %add_bitcast_fusion), channel_id=1, source_target_pairs={{0,128},{1,129},{128,0},{129,1},{2,130},{3,131},{130,2},{131,3},{4... | collective-permute-start | bytes 1544 | tf_op jit(solution)/shard_map/s_meta/ppermute | solution.py:34
  25.2 1.3 collective-permute-start.4
  26.6 2.4 %collective-permute-done.11.refs_6_ = bf16[4,3,2,128,128]{4,3,2,1,0:T(8,128)(2,1)} collective-permute-done((bf16[4,3,2,128,128]{4,3,2,1,0:T(8,128)(2,1)S(1)}, bf16[4,3,2,128,128]{4,3,2,1,0:T(8,128)(2,1)}, u32[]{:S(2)}, u32[]{:S(2)}) %collective-permute-start.11) | collective-permute-done | bytes 786464 | tf_op jit(solution)/shard_map/s_b1/ppermute | solution.py:46
  29.7 1.9 %collective-permute-start.8 = (bf16[4,3,2,128,128]{4,3,2,1,0:T(8,128)(2,1)}, bf16[4,3,2,128,128]{4,3,2,1,0:T(8,128)(2,1)}, u32[]{:S(2)}, u32[]{:S(2)}) collective-permute-start(bf16[4,3,2,128,128]{4,3,2,1,0:T(8,128)(2,1)} %collective-permute-done.1.refs_8_), channel_id=1, source_target_pairs={{0,16},{16,32},{32,48},{48,64},{64,80},{80,96},{96,112},{112,0},{8... | collective-permute-start | bytes 2359304 | tf_op jit(solution)/shard_map/s_a2/ppermute | solution.py:46
  33.1 1.8 %convert_reduce_fusion = s32[5,16,20]{1,2,0:T(8,128)S(1)} fusion(pred[20,20]{1,0:T(8,128)(4,1)S(1)} %iota_compare_fusion.6, pred[5,16,20]{2,1,0:T(8,128)(4,1)S(1)} %get-tuple-element.68), kind=kLoop, calls=%fused_computation.5 | loop fusion | flops 94400 | bytes 8400 | tf_op jit(solution)/shard_map/reduce_sum | solution.py:411
  35.0 1.8 %select_reduce_fusion = s32[5,16,20]{1,2,0:T(8,128)S(1)} fusion(s32[5,16,20]{2,1,0:T(8,128)S(1)} %get-tuple-element.82, s32[5,16,20]{2,1,0:T(8,128)S(1)} %copy.9, pred[5,16,20]{2,1,0:T(8,128)(4,1)S(1)} %get-tuple-element.68), kind=kLoop, calls=%fused_computation.3 | loop fusion | flops 126400 | bytes 20800 | tf_op jit(solution)/shard_map/reduce_sum | solution.py:413
  37.4 2.5 %collective-permute-start.15 = (bf16[4,3,2,128,128]{4,3,2,1,0:T(8,128)(2,1)}, bf16[4,3,2,128,128]{4,3,2,1,0:T(8,128)(2,1)}, u32[]{:S(2)}, u32[]{:S(2)}) collective-permute-start(bf16[4,3,2,128,128]{4,3,2,1,0:T(8,128)(2,1)} %collective-permute-done.11.refs_6_), channel_id=1, source_target_pairs={{0,16},{16,32},{32,48},{48,64},{64,80},{80,96},{96,112},{112,0},{8... | collective-permute-start | bytes 2359304 | tf_op jit(solution)/shard_map/s_b2/ppermute | solution.py:46
  40.9 1.5 %pad_maximum_fusion.1 = bf16[2048,384]{1,0:T(8,128)(2,1)S(1)} fusion(bf16[512,384]{1,0:T(8,128)(2,1)} %collective-permute-done.7, bf16[512,384]{1,0:T(8,128)(2,1)} %collective-permute-done.6, bf16[512,384]{1,0:T(8,128)(2,1)} %collective-permute-done.5, bf16[512,384]{1,0:T(8,128)(2,1)} %param.8), kind=kLoop, calls=%fused_computation.2 | loop fusion | flops 6291456 | bytes 3145728 | tf_op jit(solution)/shard_map/concatenate | solution.py:458
  42.4 5.7 %attend.5 = (f32[17,3,128,128]{3,2,1,0:T(8,128)S(1)}, f32[17,16,128]{2,1,0:T(8,128)S(1)}) custom-call(s32[16]{0:T(128)S(1)} %select_reduce_fusion.9.refs_0_, s32[256]{0:T(256)S(1)} %get-tuple-element.64.refs_1_, s32[256]{0:T(256)S(1)} %compare_select_fusion.4.refs_2_, s32[16]{0:T(128)S(1)} %get-tuple-element.87.refs_3_, ...), custom_call_target="tpu_custom_call" | custom-call | flops 15360000000 | bytes 3145728 | tf_op jit(solution)/shard_map/attend/pallas_call | solution.py:253
  48.1 1.7 %copy-done.2 = f32[17,3,128,128]{3,2,1,0:T(8,128)} copy-done((f32[17,3,128,128]{3,2,1,0:T(8,128)}, f32[17,3,128,128]{3,2,1,0:T(8,128)S(1)}, u32[]{:S(2)}) %copy-start.2) | copy-done | bytes 3342360
  49.9 2.4 %collective-permute-start.10 = (bf16[4,3,2,128,128]{4,3,2,1,0:T(8,128)(2,1)}, bf16[4,3,2,128,128]{4,3,2,1,0:T(8,128)(2,1)S(1)}, u32[]{:S(2)}, u32[]{:S(2)}) collective-permute-start(bf16[4,3,2,128,128]{4,3,2,1,0:T(8,128)(2,1)} %collective-permute-done.8.refs_8_), channel_id=1, source_target_pairs={{0,16},{16,32},{32,48},{48,64},{64,80},{80,96},{96,112},{112,0},{8... | collective-permute-start | bytes 2359304 | tf_op jit(solution)/shard_map/s_a3/ppermute | solution.py:46
  53.1 1.6 %collective-permute-start.16 = (bf16[4,3,2,128,128]{4,3,2,1,0:T(8,128)(2,1)}, bf16[4,3,2,128,128]{4,3,2,1,0:T(8,128)(2,1)}, u32[]{:S(2)}, u32[]{:S(2)}) collective-permute-start(bf16[4,3,2,128,128]{4,3,2,1,0:T(8,128)(2,1)} %collective-permute-done.15.refs_6_), channel_id=1, source_target_pairs={{0,16},{16,32},{32,48},{48,64},{64,80},{80,96},{96,112},{112,0},{8... | collective-permute-start | bytes 2359304 | tf_op jit(solution)/shard_map/s_b3/ppermute | solution.py:46
  54.7 1.9 %dynamic-slice_bitcast_fusion = (bf16[384,768]{1,0:T(8,128)(2,1)S(1)}, bf16[384,768]{1,0:T(8,128)(2,1)S(1)}, bf16[384,768]{1,0:T(8,128)(2,1)S(1)}, bf16[384,768]{1,0:T(8,128)(2,1)S(1)}) fusion(bf16[4,384,768]{2,1,0:T(8,128)(2,1)} %all-to-all-done, s32[]{:T(128)S(6)} %select_n.257, s32[]{:T(128)S(6)} %select_n.255, s32[]{:T(128)S(6)} %select_n.253, ...), kind=kLoop, calls=%fused_computation.7 | loop fusion | bytes 4718608 | tf_op jit(solution)/shard_map/jit(dynamic_index_in_dim)/squeeze | solution.py:449
  56.6 6.1 %collective-permute-done.10.refs_8_ = bf16[4,3,2,128,128]{4,3,2,1,0:T(8,128)(2,1)S(1)} collective-permute-done((bf16[4,3,2,128,128]{4,3,2,1,0:T(8,128)(2,1)}, bf16[4,3,2,128,128]{4,3,2,1,0:T(8,128)(2,1)S(1)}, u32[]{:S(2)}, u32[]{:S(2)}) %collective-permute-start.10) | collective-permute-done | bytes 786464 | tf_op jit(solution)/shard_map/s_a3/ppermute | solution.py:46
  62.7 6.1 %attend.6 = (f32[17,3,128,128]{3,2,1,0:T(8,128)S(1)}, f32[17,16,128]{2,1,0:T(8,128)S(1)}) custom-call(s32[16]{0:T(128)S(1)} %select_reduce_fusion.8.refs_0_, s32[256]{0:T(256)S(1)} %get-tuple-element.62.refs_1_, s32[256]{0:T(256)S(1)} %compare_select_fusion.3.refs_2_, s32[16]{0:T(128)S(1)} %get-tuple-element.88.refs_3_, ...), custom_call_target="tpu_custom_call" | custom-call | flops 15360000000 | bytes 3145728 | tf_op jit(solution)/shard_map/attend/pallas_call | solution.py:253
  68.8 1.2 collective-permute-start.14
  70.1 1.1 collective-permute-done.16.refs_6_
  71.2 1.2 collective-permute-start.17
  72.4 6.7 %attend.7 = (f32[17,3,128,128]{3,2,1,0:T(8,128)S(1)}, f32[17,16,128]{2,1,0:T(8,128)S(1)}) custom-call(s32[16]{0:T(128)S(1)} %select_reduce_fusion.6.refs_0_, s32[256]{0:T(256)S(1)} %get-tuple-element.58.refs_1_, s32[256]{0:T(256)S(1)} %compare_select_fusion.1.refs_2_, s32[16]{0:T(128)S(1)} %get-tuple-element.85.refs_3_, ...), custom_call_target="tpu_custom_call" | custom-call | flops 15360000000 | bytes 3145728 | tf_op jit(solution)/shard_map/attend/pallas_call | solution.py:253
  79.2 3.8 %attend.8 = (f32[17,3,128,128]{3,2,1,0:T(8,128)S(1)}, f32[17,16,128]{2,1,0:T(8,128)S(1)}) custom-call(s32[16]{0:T(128)S(1)} %select_reduce_fusion.7.refs_0_, s32[256]{0:T(256)S(1)} %get-tuple-element.60.refs_1_, s32[256]{0:T(256)S(1)} %compare_select_fusion.2.refs_2_, s32[16]{0:T(128)S(1)} %get-tuple-element.89.refs_3_, ...), custom_call_target="tpu_custom_call" | custom-call | flops 7680000000 | bytes 1572864 | tf_op jit(solution)/shard_map/attend/pallas_call | solution.py:253
  83.8 1.7 %collective-permute-done.20.refs_7_ = bf16[4,3,2,128,128]{4,3,2,1,0:T(8,128)(2,1)S(1)} collective-permute-done((bf16[4,3,2,128,128]{4,3,2,1,0:T(8,128)(2,1)S(1)}, bf16[4,3,2,128,128]{4,3,2,1,0:T(8,128)(2,1)S(1)}, u32[]{:S(2)}, u32[]{:S(2)}) %collective-permute-start.20) | collective-permute-done | bytes 786464 | tf_op jit(solution)/shard_map/s_ta4/ppermute | solution.py:39
  85.5 3.8 %attend.9 = (bf16[2,400,128]{2,1,0:T(8,128)(2,1)S(1)}, bf16[2,400,128]{2,1,0:T(8,128)(2,1)S(1)}, bf16[2,400,128]{2,1,0:T(8,128)(2,1)S(1)}, bf16[2,400,128]{2,1,0...) custom-call(s32[16]{0:T(128)S(1)} %select_reduce_fusion.10.refs_0_, ...), custom_call_target="tpu_custom_call" | custom-call | flops 7680000000 | bytes 1572864 | tf_op jit(solution)/shard_map/attend/pallas_call | solution.py:253
  89.6 12.3 %collective-permute-start.22 = (bf16[2,400,128]{2,1,0:T(8,128)(2,1)S(1)}, bf16[2,400,128]{2,1,0:T(8,128)(2,1)S(1)}, u32[]{:S(2)}, u32[]{:S(2)}) collective-permute-start(bf16[2,400,128]{2,1,0:T(8,128)(2,1)S(1)} %get-tuple-element.50), channel_id=1, source_target_pairs={{0,129},{1,0},{128,1},{129,128},{2,131},{3,2},{130,3},{131,130},{4... | collective-permute-start | bytes 614408 | tf_op jit(solution)/shard_map/s_f1/ppermute | solution.py:34
  101.8 2.8 %collective-permute-start.27 = (bf16[2,400,128]{2,1,0:T(8,128)(2,1)S(1)}, bf16[2,400,128]{2,1,0:T(8,128)(2,1)S(1)}, u32[]{:S(2)}, u32[]{:S(2)}) collective-permute-start(bf16[2,400,128]{2,1,0:T(8,128)(2,1)S(1)} %get-tuple-element.55), channel_id=1, source_target_pairs={{0,1},{1,128},{128,129},{129,0},{2,3},{3,130},{130,131},{131,2},{4... | collective-permute-start | bytes 614408 | tf_op jit(solution)/shard_map/s_prv1/ppermute | solution.py:34
  104.6 2.6 %collective-permute-done.21.a0 = bf16[2,400,128]{2,1,0:T(8,128)(2,1)S(1)} collective-permute-done((bf16[2,400,128]{2,1,0:T(8,128)(2,1)S(1)}, bf16[2,400,128]{2,1,0:T(8,128)(2,1)S(1)}, u32[]{:S(2)}, u32[]{:S(2)}) %collective-permute-start.21) | collective-permute-done | bytes 204832 | tf_op jit(solution)/shard_map/s_f0/ppermute | solution.py:34
  107.2 1.9 %collective-permute-done.22.b0 = bf16[2,400,128]{2,1,0:T(8,128)(2,1)S(1)} collective-permute-done((bf16[2,400,128]{2,1,0:T(8,128)(2,1)S(1)}, bf16[2,400,128]{2,1,0:T(8,128)(2,1)S(1)}, u32[]{:S(2)}, u32[]{:S(2)}) %collective-permute-start.22) | collective-permute-done | bytes 204832 | tf_op jit(solution)/shard_map/s_f1/ppermute | solution.py:34
  109.4 2.1 %collective-permute-start.28 = (bf16[2,400,128]{2,1,0:T(8,128)(2,1)S(1)}, bf16[2,400,128]{2,1,0:T(8,128)(2,1)S(1)}, u32[]{:S(2)}, u32[]{:S(2)}) collective-permute-start(bf16[2,400,128]{2,1,0:T(8,128)(2,1)S(1)} %get-tuple-element.56), channel_id=1, source_target_pairs={{0,129},{1,0},{128,1},{129,128},{2,131},{3,2},{130,3},{131,130},{4... | collective-permute-start | bytes 614408 | tf_op jit(solution)/shard_map/s_nxt1/ppermute | solution.py:34
  111.5 2.1 %collective-permute-start.24 = (bf16[2,400,128]{2,1,0:T(8,128)(2,1)S(1)}, bf16[2,400,128]{2,1,0:T(8,128)(2,1)S(1)}, u32[]{:S(2)}, u32[]{:S(2)}) collective-permute-start(bf16[2,400,128]{2,1,0:T(8,128)(2,1)S(1)} %get-tuple-element.53), channel_id=1, source_target_pairs={{0,129},{1,0},{128,1},{129,128},{2,131},{3,2},{130,3},{131,130},{4... | collective-permute-start | bytes 614408 | tf_op jit(solution)/shard_map/s_nxt0/ppermute | solution.py:34
  113.6 3.9 %collective-permute-done.28.p1 = bf16[2,400,128]{2,1,0:T(8,128)(2,1)S(1)} collective-permute-done((bf16[2,400,128]{2,1,0:T(8,128)(2,1)S(1)}, bf16[2,400,128]{2,1,0:T(8,128)(2,1)S(1)}, u32[]{:S(2)}, u32[]{:S(2)}) %collective-permute-start.28) | collective-permute-done | bytes 204832 | tf_op jit(solution)/shard_map/s_nxt1/ppermute | solution.py:34
  117.7 2.6 %collective-permute-start.29 = (bf16[256,384]{1,0:T(8,128)(2,1)S(1)}, bf16[256,384]{1,0:T(8,128)(2,1)S(1)}, u32[]{:S(2)}, u32[]{:S(2)}) collective-permute-start(bf16[256,384]{1,0:T(8,128)(2,1)S(1)} %combine.3.refs_1_), channel_id=1, source_target_pairs={{0,6},{2,0},{4,2},{6,4},{1,7},{3,1},{5,3},{7,5},{8,14},{10,8},{12,... | collective-permute-start | bytes 589832 | tf_op jit(solution)/shard_map/s_right1/ppermute | solution.py:34
  120.7 1.3 collective-permute-start.25
  122.0 1.6 %collective-permute-start.31 = (bf16[256,384]{1,0:T(8,128)(2,1)S(1)}, bf16[256,384]{1,0:T(8,128)(2,1)S(1)}, u32[]{:S(2)}, u32[]{:S(2)}) collective-permute-start(bf16[256,384]{1,0:T(8,128)(2,1)S(1)} %combine.3.refs_1_), channel_id=1, source_target_pairs={{0,2},{2,4},{4,6},{6,0},{1,3},{3,5},{5,7},{7,1},{8,10},{10,12},{12... | collective-permute-start | bytes 589832 | tf_op jit(solution)/shard_map/s_left1/ppermute | solution.py:34
  123.6 1.6 %collective-permute-start.32 = (bf16[256,384]{1,0:T(8,128)(2,1)S(1)}, bf16[256,384]{1,0:T(8,128)(2,1)S(1)}, u32[]{:S(2)}, u32[]{:S(2)}) collective-permute-start(bf16[256,384]{1,0:T(8,128)(2,1)S(1)} %combine.2.refs_0_), channel_id=1, source_target_pairs={{0,6},{2,0},{4,2},{6,4},{1,7},{3,1},{5,3},{7,5},{8,14},{10,8},{12,... | collective-permute-start | bytes 589832 | tf_op jit(solution)/shard_map/s_right0/ppermute | solution.py:34
  125.3 1.9 %collective-permute-start.30 = (bf16[256,384]{1,0:T(8,128)(2,1)S(1)}, bf16[256,384]{1,0:T(8,128)(2,1)S(1)}, u32[]{:S(2)}, u32[]{:S(2)}) collective-permute-start(bf16[256,384]{1,0:T(8,128)(2,1)S(1)} %collective-permute-done.29.refs_5_), channel_id=1, source_target_pairs={{0,6},{2,0},{4,2},{6,4},{1,7},{3,1},{5,3},{7,5},{8,14},{10,8},{12,... | collective-permute-start | bytes 589832 | tf_op jit(solution)/shard_map/s_r2/ppermute | solution.py:34
  127.1 2.7 %collective-permute-done.25.refs_2_ = bf16[256,384]{1,0:T(8,128)(2,1)S(1)} collective-permute-done((bf16[256,384]{1,0:T(8,128)(2,1)S(1)}, bf16[256,384]{1,0:T(8,128)(2,1)S(1)}, u32[]{:S(2)}, u32[]{:S(2)}) %collective-permute-start.25) | collective-permute-done | bytes 196640 | tf_op jit(solution)/shard_map/s_left0/ppermute | solution.py:34
  129.9 3.6 %collective-permute-done.31.refs_3_ = bf16[256,384]{1,0:T(8,128)(2,1)S(1)} collective-permute-done((bf16[256,384]{1,0:T(8,128)(2,1)S(1)}, bf16[256,384]{1,0:T(8,128)(2,1)S(1)}, u32[]{:S(2)}, u32[]{:S(2)}) %collective-permute-start.31) | collective-permute-done | bytes 196640 | tf_op jit(solution)/shard_map/s_left1/ppermute | solution.py:34
  133.5 1.4 %project.2.refs_3_ = f32[512,768]{1,0:T(8,128)S(1)} custom-call(bf16[256,384]{1,0:T(8,128)(2,1)S(1)} %combine.2.refs_0_, bf16[256,384]{1,0:T(8,128)(2,1)S(1)} %combine.3.refs_1_, bf16[256,384]{1,0:T(8,128)(2,1)S(1)} %collective-permute-done.25.refs_2_, bf16[256,384]{1,0:T(8,128)(2,1)S(1)} %collective-permute-done.31.refs_3_, ...), custom_call_target="tpu_custom_call" | custom-call | flops 1000000000 | bytes 4194304 | tf_op jit(solution)/shard_map/project/pallas_call | solution.py:373
  134.9 1.8 %collective-permute-done.26.refs_0_ = bf16[256,384]{1,0:T(8,128)(2,1)S(1)} collective-permute-done((bf16[256,384]{1,0:T(8,128)(2,1)S(1)}, bf16[256,384]{1,0:T(8,128)(2,1)S(1)}, u32[]{:S(2)}, u32[]{:S(2)}) %collective-permute-start.26) | collective-permute-done | bytes 196640 | tf_op jit(solution)/shard_map/s_l2/ppermute | solution.py:34
  136.8 1.5 %project.3 = bf16[512,768]{1,0:T(8,128)(2,1)} custom-call(bf16[256,384]{1,0:T(8,128)(2,1)S(1)} %collective-permute-done.26.refs_0_, bf16[256,384]{1,0:T(8,128)(2,1)S(1)} %collective-permute-done.30.refs_1_, bf16[384,768]{1,0:T(8,128)(2,1)S(1)} %get-tuple-element.70.refs_2_, f32[512,768]{1,0:T(8,128)S(1)} %project.2.refs_3_), custom_call_target="tpu_custom_call" | custom-call | flops 1000000000 | bytes 4194304 | tf_op jit(solution)/shard_map/project/pallas_call | solution.py:373
  (100 shorter events, 8.8 us)
Async XLA Ops:
  0.0 20.5 %copy-start = (s32[1,32]{1,0:T(1,128)S(1)}, s32[1,32]{1,0:T(1,128)}, u32[]{:S(2)}) copy-start(s32[1,32]{1,0:T(1,128)} %param.11) | copy-start | bytes 388
  0.0 8.2 %copy-start.5 = (s32[4,16]{1,0:T(4,128)S(1)}, s32[4,16]{1,0:T(4,128)}, u32[]{:S(2)}) copy-start(s32[4,16]{1,0:T(4,128)} %param.12) | copy-start | bytes 772
  0.0 12.3 %copy-start.4 = (bf16[384,3072]{1,0:T(8,128)(2,1)S(1)}, bf16[384,3072]{1,0:T(8,128)(2,1)}, u32[]{:S(2)}) copy-start(bf16[384,3072]{1,0:T(8,128)(2,1)} %param.10) | copy-start | bytes 7077892
  4.9 3.2 %collective-permute-start = (bf16[4,3,2,128,128]{4,3,2,1,0:T(8,128)(2,1)}, bf16[4,3,2,128,128]{4,3,2,1,0:T(8,128)(2,1)S(1)}, u32[]{:S(2)}, u32[]{:S(2)}) collective-permute-start(bf16[4,3,2,128,128]{4,3,2,1,0:T(8,128)(2,1)} %squares.1.refs_6_), channel_id=1, source_target_pairs={{0,8},{8,0},{1,9},{9,1},{2,10},{10,2},{3,11},{11,3},{4,12},{12,4},... | collective-permute-start | bytes 2359304 | tf_op jit(solution)/shard_map/s_tw/ppermute | solution.py:39
  4.9 20.3 %collective-permute-start.5 = (bf16[512,384]{1,0:T(8,128)(2,1)}, bf16[512,384]{1,0:T(8,128)(2,1)}, u32[]{:S(2)}, u32[]{:S(2)}) collective-permute-start(bf16[512,384]{1,0:T(8,128)(2,1)} %param.8), channel_id=1, source_target_pairs={{0,1},{1,128},{128,129},{129,0},{2,3},{3,130},{130,131},{131,2},{4... | collective-permute-start | bytes 1179656 | tf_op jit(solution)/shard_map/s_q_back/ppermute | solution.py:34
  6.5 30.9 %collective-permute-start.7 = (bf16[512,384]{1,0:T(8,128)(2,1)}, bf16[512,384]{1,0:T(8,128)(2,1)}, u32[]{:S(2)}, u32[]{:S(2)}) collective-permute-start(bf16[512,384]{1,0:T(8,128)(2,1)} %param.8), channel_id=1, source_target_pairs={{0,129},{1,0},{128,1},{129,128},{2,131},{3,2},{130,3},{131,130},{4... | collective-permute-start | bytes 1179656 | tf_op jit(solution)/shard_map/s_q_next/ppermute | solution.py:34
  8.2 12.4 %collective-permute-start.1 = (bf16[4,3,2,128,128]{4,3,2,1,0:T(8,128)(2,1)}, bf16[4,3,2,128,128]{4,3,2,1,0:T(8,128)(2,1)}, u32[]{:S(2)}, u32[]{:S(2)}) collective-permute-start(bf16[4,3,2,128,128]{4,3,2,1,0:T(8,128)(2,1)} %squares.1.refs_6_), channel_id=1, source_target_pairs={{0,16},{16,32},{32,48},{48,64},{64,80},{80,96},{96,112},{112,0},{8... | collective-permute-start | bytes 2359304 | tf_op jit(solution)/shard_map/s_a1/ppermute | solution.py:46
  10.3 18.7 %collective-permute-start.11 = (bf16[4,3,2,128,128]{4,3,2,1,0:T(8,128)(2,1)S(1)}, bf16[4,3,2,128,128]{4,3,2,1,0:T(8,128)(2,1)}, u32[]{:S(2)}, u32[]{:S(2)}) collective-permute-start(bf16[4,3,2,128,128]{4,3,2,1,0:T(8,128)(2,1)S(1)} %collective-permute-done.refs_7_), channel_id=1, source_target_pairs={{0,16},{16,32},{32,48},{48,64},{64,80},{80,96},{96,112},{112,0},{8... | collective-permute-start | bytes 2359304 | tf_op jit(solution)/shard_map/s_b1/ppermute | solution.py:46
  14.1 7.4 %copy-start.9 = (s32[4]{0:T(128)S(1)}, s32[4]{0:T(128)}, u32[]{:S(2)}) copy-start(s32[4]{0:T(128)} %param.13) | copy-start | bytes 52
  14.1 18.6 %copy-start.6 = (s32[5]{0:T(128)S(1)}, s32[5]{0:T(128)}, u32[]{:S(2)}) copy-start(s32[5]{0:T(128)} %constant.234.clone) | copy-start | bytes 64
  14.1 18.6 %copy-start.7 = (s32[5]{0:T(128)S(1)}, s32[5]{0:T(128)}, u32[]{:S(2)}) copy-start(s32[5]{0:T(128)} %constant.235.clone) | copy-start | bytes 64
  14.1 18.6 %copy-start.8 = (s32[5]{0:T(128)S(1)}, s32[5]{0:T(128)}, u32[]{:S(2)}) copy-start(s32[5]{0:T(128)} %constant.243) | copy-start | bytes 64
  14.1 40.5 %all-to-all-start = ((bf16[4,384,768]{2,1,0:T(8,128)(2,1)}), bf16[4,384,768]{2,1,0:T(8,128)(2,1)}, u32[]{:S(2)}, u32[]{:S(2)}) async-start(bf16[4,384,768]{2,1,0:T(8,128)(2,1)} %pad_maximum_fusion), calls=%async_computation | async-start | bytes 4718592 | tf_op jit(solution)/shard_map/all_to_all | solution.py:447
  21.3 21.1 %copy-start.1 = (bf16[4,3,2,128,128]{4,3,2,1,0:T(8,128)(2,1)S(1)}, bf16[4,3,2,128,128]{4,3,2,1,0:T(8,128)(2,1)}, u32[]{:S(2)}) copy-start(bf16[4,3,2,128,128]{4,3,2,1,0:T(8,128)(2,1)} %squares.1.refs_6_) | copy-start | bytes 2359300
  21.6 8.1 %collective-permute-start.2 = (s32[1,128]{1,0:T(1,128)S(1)}, s32[1,128]{1,0:T(1,128)S(1)}, u32[]{:S(2)}, u32[]{:S(2)}) collective-permute-start(s32[1,128]{1,0:T(1,128)S(1)} %add_bitcast_fusion), channel_id=1, source_target_pairs={{0,1},{1,128},{128,129},{129,0},{2,3},{3,130},{130,131},{131,2},{4... | collective-permute-start | bytes 1544 | tf_op jit(solution)/shard_map/s_meta/ppermute | solution.py:34
  22.3 9.3 %collective-permute-start.3 = (s32[1,128]{1,0:T(1,128)S(1)}, s32[1,128]{1,0:T(1,128)S(1)}, u32[]{:S(2)}, u32[]{:S(2)}) collective-permute-start(s32[1,128]{1,0:T(1,128)S(1)} %add_bitcast_fusion), channel_id=1, source_target_pairs={{0,128},{1,129},{128,0},{129,1},{2,130},{3,131},{130,2},{131,3},{4... | collective-permute-start | bytes 1544 | tf_op jit(solution)/shard_map/s_meta/ppermute | solution.py:34
  25.2 6.6 %collective-permute-start.4 = (s32[1,128]{1,0:T(1,128)S(1)}, s32[1,128]{1,0:T(1,128)S(1)}, u32[]{:S(2)}, u32[]{:S(2)}) collective-permute-start(s32[1,128]{1,0:T(1,128)S(1)} %add_bitcast_fusion), channel_id=1, source_target_pairs={{0,129},{1,0},{128,1},{129,128},{2,131},{3,2},{130,3},{131,130},{4... | collective-permute-start | bytes 1544 | tf_op jit(solution)/shard_map/s_meta/ppermute | solution.py:34
  29.0 11.9 %collective-permute-start.6 = (bf16[512,384]{1,0:T(8,128)(2,1)}, bf16[512,384]{1,0:T(8,128)(2,1)}, u32[]{:S(2)}, u32[]{:S(2)}) collective-permute-start(bf16[512,384]{1,0:T(8,128)(2,1)} %collective-permute-done.5), channel_id=1, source_target_pairs={{0,1},{1,128},{128,129},{129,0},{2,3},{3,130},{130,131},{131,2},{4... | collective-permute-start | bytes 1179656 | tf_op jit(solution)/shard_map/s_q_far/ppermute | solution.py:34
  29.7 20.1 %collective-permute-start.8 = (bf16[4,3,2,128,128]{4,3,2,1,0:T(8,128)(2,1)}, bf16[4,3,2,128,128]{4,3,2,1,0:T(8,128)(2,1)}, u32[]{:S(2)}, u32[]{:S(2)}) collective-permute-start(bf16[4,3,2,128,128]{4,3,2,1,0:T(8,128)(2,1)} %collective-permute-done.1.refs_8_), channel_id=1, source_target_pairs={{0,16},{16,32},{32,48},{48,64},{64,80},{80,96},{96,112},{112,0},{8... | collective-permute-start | bytes 2359304 | tf_op jit(solution)/shard_map/s_a2/ppermute | solution.py:46
  31.6 10.7 %collective-permute-start.9 = (bf16[4,3,2,128,128]{4,3,2,1,0:T(8,128)(2,1)}, bf16[4,3,2,128,128]{4,3,2,1,0:T(8,128)(2,1)}, u32[]{:S(2)}, u32[]{:S(2)}) collective-permute-start(bf16[4,3,2,128,128]{4,3,2,1,0:T(8,128)(2,1)} %collective-permute-done.1.refs_8_), channel_id=1, source_target_pairs={{0,8},{8,0},{1,9},{9,1},{2,10},{10,2},{3,11},{11,3},{4,12},{12,4},... | collective-permute-start | bytes 2359304 | tf_op jit(solution)/shard_map/s_ta1/ppermute | solution.py:39
  31.8 30.9 %collective-permute-start.12 = (bf16[4,3,2,128,128]{4,3,2,1,0:T(8,128)(2,1)}, bf16[4,3,2,128,128]{4,3,2,1,0:T(8,128)(2,1)}, u32[]{:S(2)}, u32[]{:S(2)}) collective-permute-start(bf16[4,3,2,128,128]{4,3,2,1,0:T(8,128)(2,1)} %collective-permute-done.11.refs_6_), channel_id=1, source_target_pairs={{0,8},{8,0},{1,9},{9,1},{2,10},{10,2},{3,11},{11,3},{4,12},{12,4},... | collective-permute-start | bytes 2359304 | tf_op jit(solution)/shard_map/s_tb1/ppermute | solution.py:39
  37.4 15.0 %collective-permute-start.15 = (bf16[4,3,2,128,128]{4,3,2,1,0:T(8,128)(2,1)}, bf16[4,3,2,128,128]{4,3,2,1,0:T(8,128)(2,1)}, u32[]{:S(2)}, u32[]{:S(2)}) collective-permute-start(bf16[4,3,2,128,128]{4,3,2,1,0:T(8,128)(2,1)} %collective-permute-done.11.refs_6_), channel_id=1, source_target_pairs={{0,16},{16,32},{32,48},{48,64},{64,80},{80,96},{96,112},{112,0},{8... | collective-permute-start | bytes 2359304 | tf_op jit(solution)/shard_map/s_b2/ppermute | solution.py:46
  48.1 1.7 %copy-start.2 = (f32[17,3,128,128]{3,2,1,0:T(8,128)}, f32[17,3,128,128]{3,2,1,0:T(8,128)S(1)}, u32[]{:S(2)}) copy-start(f32[17,3,128,128]{3,2,1,0:T(8,128)S(1)} %get-tuple-element.38.refs_10_) | copy-start | bytes 10027012
  49.9 12.8 %collective-permute-start.10 = (bf16[4,3,2,128,128]{4,3,2,1,0:T(8,128)(2,1)}, bf16[4,3,2,128,128]{4,3,2,1,0:T(8,128)(2,1)S(1)}, u32[]{:S(2)}, u32[]{:S(2)}) collective-permute-start(bf16[4,3,2,128,128]{4,3,2,1,0:T(8,128)(2,1)} %collective-permute-done.8.refs_8_), channel_id=1, source_target_pairs={{0,16},{16,32},{32,48},{48,64},{64,80},{80,96},{96,112},{112,0},{8... | collective-permute-start | bytes 2359304 | tf_op jit(solution)/shard_map/s_a3/ppermute | solution.py:46
  52.2 10.5 %collective-permute-start.13 = (bf16[4,3,2,128,128]{4,3,2,1,0:T(8,128)(2,1)}, bf16[4,3,2,128,128]{4,3,2,1,0:T(8,128)(2,1)}, u32[]{:S(2)}, u32[]{:S(2)}) collective-permute-start(bf16[4,3,2,128,128]{4,3,2,1,0:T(8,128)(2,1)} %collective-permute-done.8.refs_8_), channel_id=1, source_target_pairs={{0,8},{8,0},{1,9},{9,1},{2,10},{10,2},{3,11},{11,3},{4,12},{12,4},... | collective-permute-start | bytes 2359304 | tf_op jit(solution)/shard_map/s_ta2/ppermute | solution.py:39
  52.5 19.9 %collective-permute-start.18 = (bf16[4,3,2,128,128]{4,3,2,1,0:T(8,128)(2,1)}, bf16[4,3,2,128,128]{4,3,2,1,0:T(8,128)(2,1)}, u32[]{:S(2)}, u32[]{:S(2)}) collective-permute-start(bf16[4,3,2,128,128]{4,3,2,1,0:T(8,128)(2,1)} %collective-permute-done.15.refs_6_), channel_id=1, source_target_pairs={{0,8},{8,0},{1,9},{9,1},{2,10},{10,2},{3,11},{11,3},{4,12},{12,4},... | collective-permute-start | bytes 2359304 | tf_op jit(solution)/shard_map/s_tb2/ppermute | solution.py:39
  53.1 18.2 %collective-permute-start.16 = (bf16[4,3,2,128,128]{4,3,2,1,0:T(8,128)(2,1)}, bf16[4,3,2,128,128]{4,3,2,1,0:T(8,128)(2,1)}, u32[]{:S(2)}, u32[]{:S(2)}) collective-permute-start(bf16[4,3,2,128,128]{4,3,2,1,0:T(8,128)(2,1)} %collective-permute-done.15.refs_6_), channel_id=1, source_target_pairs={{0,16},{16,32},{32,48},{48,64},{64,80},{80,96},{96,112},{112,0},{8... | collective-permute-start | bytes 2359304 | tf_op jit(solution)/shard_map/s_b3/ppermute | solution.py:46
  54.6 8.1 %copy-start.3 = (f32[17,3,128,128]{3,2,1,0:T(8,128)S(1)}, f32[17,3,128,128]{3,2,1,0:T(8,128)}, u32[]{:S(2)}) copy-start(f32[17,3,128,128]{3,2,1,0:T(8,128)} %copy-done.2) | copy-start | bytes 10027012
  62.7 9.7 %collective-permute-start.19 = (bf16[4,3,2,128,128]{4,3,2,1,0:T(8,128)(2,1)S(1)}, bf16[4,3,2,128,128]{4,3,2,1,0:T(8,128)(2,1)S(1)}, u32[]{:S(2)}, u32[]{:S(2)}) collective-permute-start(bf16[4,3,2,128,128]{4,3,2,1,0:T(8,128)(2,1)S(1)} %collective-permute-done.10.refs_8_), channel_id=1, source_target_pairs={{0,8},{8,0},{1,9},{9,1},{2,10},{10,2},{3,11},{11,3},{4,12},{12,4},... | collective-permute-start | bytes 2359304 | tf_op jit(solution)/shard_map/s_ta3/ppermute | solution.py:39
  68.8 14.1 %collective-permute-start.14 = (bf16[4,3,2,128,128]{4,3,2,1,0:T(8,128)(2,1)S(1)}, bf16[4,3,2,128,128]{4,3,2,1,0:T(8,128)(2,1)S(1)}, u32[]{:S(2)}, u32[]{:S(2)}) collective-permute-start(bf16[4,3,2,128,128]{4,3,2,1,0:T(8,128)(2,1)S(1)} %collective-permute-done.10.refs_8_), channel_id=1, source_target_pairs={{0,16},{16,32},{32,48},{48,64},{64,80},{80,96},{96,112},{112,0},{8... | collective-permute-start | bytes 2359304 | tf_op jit(solution)/shard_map/s_a4/ppermute | solution.py:46
  71.2 7.9 %collective-permute-start.17 = (bf16[4,3,2,128,128]{4,3,2,1,0:T(8,128)(2,1)}, bf16[4,3,2,128,128]{4,3,2,1,0:T(8,128)(2,1)S(1)}, u32[]{:S(2)}, u32[]{:S(2)}) collective-permute-start(bf16[4,3,2,128,128]{4,3,2,1,0:T(8,128)(2,1)} %collective-permute-done.16.refs_6_), channel_id=1, source_target_pairs={{0,8},{8,0},{1,9},{9,1},{2,10},{10,2},{3,11},{11,3},{4,12},{12,4},... | collective-permute-start | bytes 2359304 | tf_op jit(solution)/shard_map/s_tb3/ppermute | solution.py:39
  82.9 2.6 %collective-permute-start.20 = (bf16[4,3,2,128,128]{4,3,2,1,0:T(8,128)(2,1)S(1)}, bf16[4,3,2,128,128]{4,3,2,1,0:T(8,128)(2,1)S(1)}, u32[]{:S(2)}, u32[]{:S(2)}) collective-permute-start(bf16[4,3,2,128,128]{4,3,2,1,0:T(8,128)(2,1)S(1)} %collective-permute-done.14.refs_6_), channel_id=1, source_target_pairs={{0,8},{8,0},{1,9},{9,1},{2,10},{10,2},{3,11},{11,3},{4,12},{12,4},... | collective-permute-start | bytes 2359304 | tf_op jit(solution)/shard_map/s_ta4/ppermute | solution.py:39
  89.3 17.9 %collective-permute-start.21 = (bf16[2,400,128]{2,1,0:T(8,128)(2,1)S(1)}, bf16[2,400,128]{2,1,0:T(8,128)(2,1)S(1)}, u32[]{:S(2)}, u32[]{:S(2)}) collective-permute-start(bf16[2,400,128]{2,1,0:T(8,128)(2,1)S(1)} %get-tuple-element.48), channel_id=1, source_target_pairs={{0,1},{1,128},{128,129},{129,0},{2,3},{3,130},{130,131},{131,2},{4... | collective-permute-start | bytes 614408 | tf_op jit(solution)/shard_map/s_f0/ppermute | solution.py:34
  89.6 19.6 %collective-permute-start.22 = (bf16[2,400,128]{2,1,0:T(8,128)(2,1)S(1)}, bf16[2,400,128]{2,1,0:T(8,128)(2,1)S(1)}, u32[]{:S(2)}, u32[]{:S(2)}) collective-permute-start(bf16[2,400,128]{2,1,0:T(8,128)(2,1)S(1)} %get-tuple-element.50), channel_id=1, source_target_pairs={{0,129},{1,0},{128,1},{129,128},{2,131},{3,2},{130,3},{131,130},{4... | collective-permute-start | bytes 614408 | tf_op jit(solution)/shard_map/s_f1/ppermute | solution.py:34
  101.8 11.7 %collective-permute-start.27 = (bf16[2,400,128]{2,1,0:T(8,128)(2,1)S(1)}, bf16[2,400,128]{2,1,0:T(8,128)(2,1)S(1)}, u32[]{:S(2)}, u32[]{:S(2)}) collective-permute-start(bf16[2,400,128]{2,1,0:T(8,128)(2,1)S(1)} %get-tuple-element.55), channel_id=1, source_target_pairs={{0,1},{1,128},{128,129},{129,0},{2,3},{3,130},{130,131},{131,2},{4... | collective-permute-start | bytes 614408 | tf_op jit(solution)/shard_map/s_prv1/ppermute | solution.py:34
  109.4 8.1 %collective-permute-start.28 = (bf16[2,400,128]{2,1,0:T(8,128)(2,1)S(1)}, bf16[2,400,128]{2,1,0:T(8,128)(2,1)S(1)}, u32[]{:S(2)}, u32[]{:S(2)}) collective-permute-start(bf16[2,400,128]{2,1,0:T(8,128)(2,1)S(1)} %get-tuple-element.56), channel_id=1, source_target_pairs={{0,129},{1,0},{128,1},{129,128},{2,131},{3,2},{130,3},{131,130},{4... | collective-permute-start | bytes 614408 | tf_op jit(solution)/shard_map/s_nxt1/ppermute | solution.py:34
  111.5 8.8 %collective-permute-start.24 = (bf16[2,400,128]{2,1,0:T(8,128)(2,1)S(1)}, bf16[2,400,128]{2,1,0:T(8,128)(2,1)S(1)}, u32[]{:S(2)}, u32[]{:S(2)}) collective-permute-start(bf16[2,400,128]{2,1,0:T(8,128)(2,1)S(1)} %get-tuple-element.53), channel_id=1, source_target_pairs={{0,129},{1,0},{128,1},{129,128},{2,131},{3,2},{130,3},{131,130},{4... | collective-permute-start | bytes 614408 | tf_op jit(solution)/shard_map/s_nxt0/ppermute | solution.py:34
  113.5 7.0 %collective-permute-start.23 = (bf16[2,400,128]{2,1,0:T(8,128)(2,1)S(1)}, bf16[2,400,128]{2,1,0:T(8,128)(2,1)S(1)}, u32[]{:S(2)}, u32[]{:S(2)}) collective-permute-start(bf16[2,400,128]{2,1,0:T(8,128)(2,1)S(1)} %get-tuple-element.52), channel_id=1, source_target_pairs={{0,1},{1,128},{128,129},{129,0},{2,3},{3,130},{130,131},{131,2},{4... | collective-permute-start | bytes 614408 | tf_op jit(solution)/shard_map/s_prv0/ppermute | solution.py:34
  117.7 7.5 %collective-permute-start.29 = (bf16[256,384]{1,0:T(8,128)(2,1)S(1)}, bf16[256,384]{1,0:T(8,128)(2,1)S(1)}, u32[]{:S(2)}, u32[]{:S(2)}) collective-permute-start(bf16[256,384]{1,0:T(8,128)(2,1)S(1)} %combine.3.refs_1_), channel_id=1, source_target_pairs={{0,6},{2,0},{4,2},{6,4},{1,7},{3,1},{5,3},{7,5},{8,14},{10,8},{12,... | collective-permute-start | bytes 589832 | tf_op jit(solution)/shard_map/s_right1/ppermute | solution.py:34
  120.7 9.1 %collective-permute-start.25 = (bf16[256,384]{1,0:T(8,128)(2,1)S(1)}, bf16[256,384]{1,0:T(8,128)(2,1)S(1)}, u32[]{:S(2)}, u32[]{:S(2)}) collective-permute-start(bf16[256,384]{1,0:T(8,128)(2,1)S(1)} %combine.2.refs_0_), channel_id=1, source_target_pairs={{0,2},{2,4},{4,6},{6,0},{1,3},{3,5},{5,7},{7,1},{8,10},{10,12},{12... | collective-permute-start | bytes 589832 | tf_op jit(solution)/shard_map/s_left0/ppermute | solution.py:34
  122.0 11.5 %collective-permute-start.31 = (bf16[256,384]{1,0:T(8,128)(2,1)S(1)}, bf16[256,384]{1,0:T(8,128)(2,1)S(1)}, u32[]{:S(2)}, u32[]{:S(2)}) collective-permute-start(bf16[256,384]{1,0:T(8,128)(2,1)S(1)} %combine.3.refs_1_), channel_id=1, source_target_pairs={{0,2},{2,4},{4,6},{6,0},{1,3},{3,5},{5,7},{7,1},{8,10},{10,12},{12... | collective-permute-start | bytes 589832 | tf_op jit(solution)/shard_map/s_left1/ppermute | solution.py:34
  123.6 9.9 %collective-permute-start.32 = (bf16[256,384]{1,0:T(8,128)(2,1)S(1)}, bf16[256,384]{1,0:T(8,128)(2,1)S(1)}, u32[]{:S(2)}, u32[]{:S(2)}) collective-permute-start(bf16[256,384]{1,0:T(8,128)(2,1)S(1)} %combine.2.refs_0_), channel_id=1, source_target_pairs={{0,6},{2,0},{4,2},{6,4},{1,7},{3,1},{5,3},{7,5},{8,14},{10,8},{12,... | collective-permute-start | bytes 589832 | tf_op jit(solution)/shard_map/s_right0/ppermute | solution.py:34
  125.3 9.7 %collective-permute-start.30 = (bf16[256,384]{1,0:T(8,128)(2,1)S(1)}, bf16[256,384]{1,0:T(8,128)(2,1)S(1)}, u32[]{:S(2)}, u32[]{:S(2)}) collective-permute-start(bf16[256,384]{1,0:T(8,128)(2,1)S(1)} %collective-permute-done.29.refs_5_), channel_id=1, source_target_pairs={{0,6},{2,0},{4,2},{6,4},{1,7},{3,1},{5,3},{7,5},{8,14},{10,8},{12,... | collective-permute-start | bytes 589832 | tf_op jit(solution)/shard_map/s_r2/ppermute | solution.py:34
  129.9 6.9 %collective-permute-start.26 = (bf16[256,384]{1,0:T(8,128)(2,1)S(1)}, bf16[256,384]{1,0:T(8,128)(2,1)S(1)}, u32[]{:S(2)}, u32[]{:S(2)}) collective-permute-start(bf16[256,384]{1,0:T(8,128)(2,1)S(1)} %collective-permute-done.25.refs_2_), channel_id=1, source_target_pairs={{0,2},{2,4},{4,6},{6,0},{1,3},{3,5},{5,7},{7,1},{8,10},{10,12},{12... | collective-permute-start | bytes 589832 | tf_op jit(solution)/shard_map/s_l2/ppermute | solution.py:34

commit v3 on v2

--- a/solution.py
+++ b/solution.py
@@ -147,13 +147,12 @@
     def score(item, slot):
         tile, blocks = blocks_of(item)
         for i, h in enumerate(heads):
-            for k in range(PAIR):
-                scores[slot, i, k] = lax.dot_general(
-                    kv[blocks[k], i, 0],
-                    q[tile, :, h * DH : (h + 1) * DH],
-                    (((1,), (1,)), ((), ())),
-                    preferred_element_type=jnp.float32,
-                )
+            scores[slot, i] = lax.dot_general(
+                jnp.concatenate([kv[block, i, 0] for block in blocks], axis=0),
+                q[tile, :, h * DH : (h + 1) * DH],
+                (((1,), (1,)), ((), ())),
+                preferred_element_type=jnp.float32,
+            )
 
     def blend(item, slot):
         target = tiles_of[item]
@@ -161,32 +160,24 @@
         left = counts[tile] - bases[item]
         lost = [jnp.where(k < left, 0.0, -NEG) for k in range(PAIR)]
         old, sums = stat[target, 0:8, :], stat[target, 8:16, :]
-        rows, news, fades, adds, mixes = [], [], [], [], []
+        news, fades, adds, mixes = [], [], [], []
         for i in range(n_heads):
+            parts = [scores[slot, i, k * BLK : (k + 1) * BLK] for k in range(PAIR)]
             tops = [
-                jnp.max(scores[slot, i, k].reshape(BLK // 8, 8, TILE), axis=0) - lost[k]
-                for k in range(PAIR)
+                jnp.max(s.reshape(BLK // 8, 8, TILE), axis=0) - gone for s, gone in zip(parts, lost)
             ]
             top = jnp.max(functools.reduce(jnp.maximum, tops), axis=0, keepdims=True)
             new = jnp.maximum(old[i : i + 1, :], top)
             news.append(new)
             fades.append(jnp.exp2((old[i : i + 1, :] - new) * scale2))
-            weights = [
-                jnp.exp2((scores[slot, i, k] - (new + lost[k])) * scale2) for k in range(PAIR)
-            ]
+            weights = [jnp.exp2((s - (new + gone)) * scale2) for s, gone in zip(parts, lost)]
             total = functools.reduce(jnp.add, weights).reshape(BLK // 8, 8, TILE)
             adds.append(jnp.sum(jnp.sum(total, axis=0), axis=0, keepdims=True))
             mixes.append(
-                functools.reduce(
-                    jnp.add,
-                    [
-                        jnp.dot(
-                            kv[blocks[k], i, 1],
-                            weights[k].astype(jnp.bfloat16),
-                            preferred_element_type=jnp.float32,
-                        )
-                        for k in range(PAIR)
-                    ],
+                jnp.dot(
+                    jnp.concatenate([kv[block, i, 1] for block in blocks], axis=1),
+                    jnp.concatenate([w.astype(jnp.bfloat16) for w in weights], axis=0),
+                    preferred_element_type=jnp.float32,
                 )
             )
         accs = [acc[target, i] * fades[i] + mixes[i] for i in range(n_heads)]
@@ -261,7 +252,7 @@
         scratch_shapes=[
             *scratch,
             pltpu.VMEM((blocks, n_heads, 2, BLK, DH), jnp.bfloat16),
-            pltpu.VMEM((2, n_heads, PAIR, BLK, TILE), jnp.float32),
+            pltpu.VMEM((2, n_heads, PAIR * BLK, TILE), jnp.float32),
             pltpu.SemaphoreType.DMA((len(kvs),)),
         ],
         compiler_params=pltpu.CompilerParams(vmem_limit_bytes=14 << 20),
@@ -450,25 +441,26 @@
         for r in range(N_X)
     ]
 
-    ids = jnp.take(after(fetch_list, a1)[0], tile_lists, axis=0)
+    ids = jnp.take(after(fetch_list, pieces)[0], tile_lists, axis=0)
     meta = jnp.concatenate([ids.reshape(-1), event_offsets, jnp.zeros((60,), jnp.int32)])[None]
     metas = [meta, *(hop(meta, COLUMN, N_COL, r, "meta") for r in range(1, N_COL))]
-    plans = block_lists(jnp.concatenate(metas, axis=0))
+    plans = block_lists(after(jnp.concatenate(metas, axis=0), a1))
     q_far = hop(after(q_back, a1), COLUMN, N_COL, 1, "q_far")
     q = jnp.concatenate([queries, q_back, q_far, q_next], axis=0)
     q = q.reshape(N_COL * 4, TILE, width)
 
     a2 = ring(after(a1, pieces), "a2")
-    state = attend(heads, plans[0], q, [mine, tw, a1, twin(a1, "ta1")], None)
     b2 = ring(b1, "b2")
-    a3 = ring(after(a2, state[1]), "a3")
-    state = attend(heads, plans[1], q, [b1, twin(b1, "tb1"), a2, twin(a2, "ta2")], state)
-    b3 = ring(b2, "b3")
-    a4 = ring(after(a3, state[1]), "a4")
+    a3 = ring(a2, "a3")
+    ta1, tb1 = twin(a1, "ta1"), twin(b1, "tb1")
+    state = attend(heads, plans[0], q, [mine, tw, a1, ta1], None)
+    b3 = ring(after(b2, state[1]), "b3")
+    a4 = ring(a3, "a4")
+    state = attend(heads, plans[1], q, [b1, after(tb1, by_peer), a2, twin(a2, "ta2")], state)
+    b3, a4 = after(b3, state[1]), after(a4, state[1])
     state = attend(heads, plans[2], q, [b2, twin(b2, "tb2"), a3, twin(a3, "ta3")], state)
     state = attend(heads, plans[3], q, [b3, twin(b3, "tb3")], state)
-    a4 = after(a4, state[1], *weights)
-    ends = [a4, twin(a4, "ta4")]
+    ends = [after(a4, *weights), twin(a4, "ta4")]
 
     far0, far1, prv0, prv1, nxt0, nxt1, near0, near1 = attend(
         heads, plans[4], q, ends, state, tuple((t, 2) for t in (8, 10, 12, 14, 4, 6, 0, 2))

time: 140 us -> 133 us (0.950)
  the two profiles are of different devices: /device:TPU:32 before, /device:TPU:64 now
where the time goes in v3:
time: 133 us; the launch traced here: 134 us
  starting transfers between devices  51.1 us (38%)
  waiting for transfers between devices  36.4 us (27%)
  Pallas kernels  31.6 us (24%)
  other arithmetic  8.55 us (6%)
  local copies, waits for them, and re-layouts  6.06 us (5%)
    ppermute x18, starting transfers between devices, hop(): return lax.ppermute(x, axis, shift(n, by))  31.5 us
    pallas_call x5, Pallas kernels, attend(): pl.pallas_call(functools.partial(attend_kernel, heads, len(kvs), spans, f...  23.2 us
    ppermute x18, waiting for transfers between devices, hop(): return lax.ppermute(x, axis, shift(n, by))  19.1 us
    ppermute x7, waiting for transfers between devices, ring(): return lax.ppermute(x, ('z', 'core'), up + down)  16.6 us
    ppermute x7, starting transfers between devices, ring(): return lax.ppermute(x, ('z', 'core'), up + down)  14.7 us
    all_to_all x1, starting transfers between devices, shards(): lax.all_to_all(pieces, 'x', split_axis=0, concat_axis=0, tiled=True)  4.65 us
    pallas_call x2, Pallas kernels, project(): pl.pallas_call(functools.partial(project_kernel, len(pairs), bool(more)),...  2.86 us
  transfers between devices with their start and end apart: 34, of which 14 were waited for; matrix products, arithmetic and copies ran while one was open for 9% of the time, Pallas kernels for 16%

profile of v3, /device:TPU:64, one launch (start us, length us, event | category | flops | bytes accessed | tf_op | source)
XLA Modules:
  0.0 134.1 jit_solution(18048238445464346836)
XLA Ops:
  0.0 2.3 %fetch.1 = bf16[4,3,128,2,128]{4,3,2,1,0:T(2,128)(2,1)} custom-call(s32[1]{0:T(128)} %bitcast.parity, bf16[1024,2,384]{2,1,0:T(2,128)(2,1)} %kv.1), custom_call_target="tpu_custom_call" | custom-call | tf_op jit(solution)/shard_map/fetch/pallas_call | solution.py:87
  2.3 2.6 %squares.1.refs_6_ = bf16[4,3,2,128,128]{4,3,2,1,0:T(8,128)(2,1)} custom-call(bf16[4,3,256,128]{3,2,1,0:T(8,128)(2,1)} %bitcast.69), custom_call_target="tpu_custom_call" | custom-call | tf_op jit(solution)/shard_map/squares/pallas_call | solution.py:95
  4.9 1.6 %collective-permute-start.5 = (bf16[512,384]{1,0:T(8,128)(2,1)}, bf16[512,384]{1,0:T(8,128)(2,1)}, u32[]{:S(2)}, u32[]{:S(2)}) collective-permute-start(bf16[512,384]{1,0:T(8,128)(2,1)} %param.8), channel_id=1, source_target_pairs={{0,1},{1,128},{128,129},{129,0},{2,3},{3,130},{130,131},{131,2},{4... | collective-permute-start | bytes 1179656 | tf_op jit(solution)/shard_map/s_q_back/ppermute | solution.py:34
  6.6 0.8 collective-permute-done.refs_7_
  7.4 1.9 %collective-permute-start.4 = (bf16[4,3,2,128,128]{4,3,2,1,0:T(8,128)(2,1)}, bf16[4,3,2,128,128]{4,3,2,1,0:T(8,128)(2,1)}, u32[]{:S(2)}, u32[]{:S(2)}) collective-permute-start(bf16[4,3,2,128,128]{4,3,2,1,0:T(8,128)(2,1)} %squares.1.refs_6_), channel_id=1, source_target_pairs={{0,16},{16,32},{32,48},{48,64},{64,80},{80,96},{96,112},{112,0},{8... | collective-permute-start | bytes 2359304 | tf_op jit(solution)/shard_map/s_a1/ppermute | solution.py:46
  9.5 1.7 %pad_maximum_fusion = bf16[4,384,768]{2,1,0:T(8,128)(2,1)} fusion(bf16[1,384,768]{2,1,0:T(8,128)(2,1)S(1)} %get-tuple-element.80, bf16[1,384,768]{2,1,0:T(8,128)(2,1)S(1)} %get-tuple-element.81, bf16[1,384,768]{2,1,0:T(8,128)(2,1)S(1)} %get-tuple-element.82, bf16[1,384,768]{2,1,0:T(8,128)(2,1)S(1)} %get-tuple-element.79), kind=kLoop, calls=%fused_computation.1 | loop fusion | flops 3538944 | bytes 4718592 | tf_op jit(solution)/shard_map/stack | solution.py:437
  12.2 1.6 %collective-permute-start.1 = (s32[1,128]{1,0:T(1,128)S(1)}, s32[1,128]{1,0:T(1,128)S(1)}, u32[]{:S(2)}, u32[]{:S(2)}) collective-permute-start(s32[1,128]{1,0:T(1,128)S(1)} %add_bitcast_fusion), channel_id=1, source_target_pairs={{0,1},{1,128},{128,129},{129,0},{2,3},{3,130},{130,131},{131,2},{4... | collective-permute-start | bytes 1544 | tf_op jit(solution)/shard_map/s_meta/ppermute | solution.py:34
  13.8 2.9 %collective-permute-start.2 = (s32[1,128]{1,0:T(1,128)S(1)}, s32[1,128]{1,0:T(1,128)S(1)}, u32[]{:S(2)}, u32[]{:S(2)}) collective-permute-start(s32[1,128]{1,0:T(1,128)S(1)} %add_bitcast_fusion), channel_id=1, source_target_pairs={{0,128},{1,129},{128,0},{129,1},{2,130},{3,131},{130,2},{131,3},{4... | collective-permute-start | bytes 1544 | tf_op jit(solution)/shard_map/s_meta/ppermute | solution.py:34
  16.7 1.3 %collective-permute-start.3 = (s32[1,128]{1,0:T(1,128)S(1)}, s32[1,128]{1,0:T(1,128)S(1)}, u32[]{:S(2)}, u32[]{:S(2)}) collective-permute-start(s32[1,128]{1,0:T(1,128)S(1)} %add_bitcast_fusion), channel_id=1, source_target_pairs={{0,129},{1,0},{128,1},{129,128},{2,131},{3,2},{130,3},{131,130},{4... | collective-permute-start | bytes 1544 | tf_op jit(solution)/shard_map/s_meta/ppermute | solution.py:34
  18.1 4.6 %all-to-all-start = ((bf16[4,384,768]{2,1,0:T(8,128)(2,1)}), bf16[4,384,768]{2,1,0:T(8,128)(2,1)}, u32[]{:S(2)}, u32[]{:S(2)}) async-start(bf16[4,384,768]{2,1,0:T(8,128)(2,1)} %pad_maximum_fusion), calls=%async_computation | async-start | bytes 4718592 | tf_op jit(solution)/shard_map/all_to_all | solution.py:438
  22.9 3.2 %collective-permute-start.11 = (bf16[4,3,2,128,128]{4,3,2,1,0:T(8,128)(2,1)S(1)}, bf16[4,3,2,128,128]{4,3,2,1,0:T(8,128)(2,1)}, u32[]{:S(2)}, u32[]{:S(2)}) collective-permute-start(bf16[4,3,2,128,128]{4,3,2,1,0:T(8,128)(2,1)S(1)} %collective-permute-done.refs_7_), channel_id=1, source_target_pairs={{0,16},{16,32},{32,48},{48,64},{64,80},{80,96},{96,112},{112,0},{8... | collective-permute-start | bytes 2359304 | tf_op jit(solution)/shard_map/s_b1/ppermute | solution.py:46
  26.9 1.8 %convert_reduce_fusion = s32[5,16,20]{1,2,0:T(8,128)S(1)} fusion(pred[20,20]{1,0:T(8,128)(4,1)S(1)} %iota_compare_fusion.6, pred[5,16,20]{2,1,0:T(8,128)(4,1)S(1)} %get-tuple-element.74), kind=kLoop, calls=%fused_computation.5 | loop fusion | flops 94400 | bytes 8400 | tf_op jit(solution)/shard_map/reduce_sum | solution.py:402
  29.1 2.0 %collective-permute-start.6 = (bf16[512,384]{1,0:T(8,128)(2,1)}, bf16[512,384]{1,0:T(8,128)(2,1)}, u32[]{:S(2)}, u32[]{:S(2)}) collective-permute-start(bf16[512,384]{1,0:T(8,128)(2,1)} %collective-permute-done.5), channel_id=1, source_target_pairs={{0,1},{1,128},{128,129},{129,0},{2,3},{3,130},{130,131},{131,2},{4... | collective-permute-start | bytes 1179656 | tf_op jit(solution)/shard_map/s_q_far/ppermute | solution.py:34
  31.2 1.3 collective-permute-start.8
  32.8 1.8 %select_reduce_fusion = s32[5,16,20]{1,2,0:T(8,128)S(1)} fusion(s32[5,16,20]{2,1,0:T(8,128)S(1)} %get-tuple-element.88, s32[5,16,20]{2,1,0:T(8,128)S(1)} %copy.9, pred[5,16,20]{2,1,0:T(8,128)(4,1)S(1)} %get-tuple-element.74), kind=kLoop, calls=%fused_computation.3 | loop fusion | flops 126400 | bytes 20800 | tf_op jit(solution)/shard_map/reduce_sum | solution.py:404
  35.8 2.5 %collective-permute-start.16 = (bf16[4,3,2,128,128]{4,3,2,1,0:T(8,128)(2,1)}, bf16[4,3,2,128,128]{4,3,2,1,0:T(8,128)(2,1)}, u32[]{:S(2)}, u32[]{:S(2)}) collective-permute-start(bf16[4,3,2,128,128]{4,3,2,1,0:T(8,128)(2,1)} %collective-permute-done.11.refs_6_), channel_id=1, source_target_pairs={{0,16},{16,32},{32,48},{48,64},{64,80},{80,96},{96,112},{112,0},{8... | collective-permute-start | bytes 2359304 | tf_op jit(solution)/shard_map/s_b2/ppermute | solution.py:46
  38.5 1.5 %pad_maximum_fusion.1 = bf16[2048,384]{1,0:T(8,128)(2,1)S(1)} fusion(bf16[512,384]{1,0:T(8,128)(2,1)} %collective-permute-done.7, bf16[512,384]{1,0:T(8,128)(2,1)} %collective-permute-done.6, bf16[512,384]{1,0:T(8,128)(2,1)} %collective-permute-done.5, bf16[512,384]{1,0:T(8,128)(2,1)} %param.8), kind=kLoop, calls=%fused_computation.2 | loop fusion | flops 6291456 | bytes 3145728 | tf_op jit(solution)/shard_map/concatenate | solution.py:449
  40.0 4.2 %collective-permute-done.8.refs_8_ = bf16[4,3,2,128,128]{4,3,2,1,0:T(8,128)(2,1)} collective-permute-done((bf16[4,3,2,128,128]{4,3,2,1,0:T(8,128)(2,1)}, bf16[4,3,2,128,128]{4,3,2,1,0:T(8,128)(2,1)}, u32[]{:S(2)}, u32[]{:S(2)}) %collective-permute-start.8) | collective-permute-done | bytes 786464 | tf_op jit(solution)/shard_map/s_a2/ppermute | solution.py:46
  44.1 2.5 %collective-permute-start.9 = (bf16[4,3,2,128,128]{4,3,2,1,0:T(8,128)(2,1)}, bf16[4,3,2,128,128]{4,3,2,1,0:T(8,128)(2,1)}, u32[]{:S(2)}, u32[]{:S(2)}) collective-permute-start(bf16[4,3,2,128,128]{4,3,2,1,0:T(8,128)(2,1)} %collective-permute-done.8.refs_8_), channel_id=1, source_target_pairs={{0,16},{16,32},{32,48},{48,64},{64,80},{80,96},{96,112},{112,0},{8... | collective-permute-start | bytes 2359304 | tf_op jit(solution)/shard_map/s_a3/ppermute | solution.py:46
  46.6 5.9 %attend.5 = (f32[17,3,128,128]{3,2,1,0:T(8,128)S(1)}, f32[17,16,128]{2,1,0:T(8,128)S(1)}) custom-call(s32[16]{0:T(128)S(1)} %select_reduce_fusion.8.refs_0_, s32[256]{0:T(256)S(1)} %get-tuple-element.68.refs_1_, s32[256]{0:T(256)S(1)} %compare_select_fusion.3.refs_2_, s32[16]{0:T(128)S(1)} %get-tuple-element.94.refs_3_, ...), custom_call_target="tpu_custom_call" | custom-call | flops 15360000000 | bytes 3145728 | tf_op jit(solution)/shard_map/attend/pallas_call | solution.py:244
  52.5 1.7 %copy-done.4 = f32[17,3,128,128]{3,2,1,0:T(8,128)} copy-done((f32[17,3,128,128]{3,2,1,0:T(8,128)}, f32[17,3,128,128]{3,2,1,0:T(8,128)S(1)}, u32[]{:S(2)}) %copy-start.4) | copy-done | bytes 3342360
  54.2 0.8 collective-permute-start.17
  55.0 0.9 copy-done.2
  55.9 1.9 %dynamic-slice_bitcast_fusion = (bf16[384,768]{1,0:T(8,128)(2,1)S(1)}, bf16[384,768]{1,0:T(8,128)(2,1)S(1)}, bf16[384,768]{1,0:T(8,128)(2,1)S(1)}, bf16[384,768]{1,0:T(8,128)(2,1)S(1)}) fusion(bf16[4,384,768]{2,1,0:T(8,128)(2,1)} %all-to-all-done, s32[]{:T(128)S(6)} %select_n.247, s32[]{:T(128)S(6)} %select_n.245, s32[]{:T(128)S(6)} %select_n.243, ...), kind=kLoop, calls=%fused_computation.7 | loop fusion | bytes 4718608 | tf_op jit(solution)/shard_map/jit(dynamic_index_in_dim)/squeeze | solution.py:440
  57.8 3.1 %collective-permute-done.9.refs_8_ = bf16[4,3,2,128,128]{4,3,2,1,0:T(8,128)(2,1)} collective-permute-done((bf16[4,3,2,128,128]{4,3,2,1,0:T(8,128)(2,1)}, bf16[4,3,2,128,128]{4,3,2,1,0:T(8,128)(2,1)}, u32[]{:S(2)}, u32[]{:S(2)}) %collective-permute-start.9) | collective-permute-done | bytes 786464 | tf_op jit(solution)/shard_map/s_a3/ppermute | solution.py:46
  61.0 2.5 %collective-permute-start.10 = (bf16[4,3,2,128,128]{4,3,2,1,0:T(8,128)(2,1)}, bf16[4,3,2,128,128]{4,3,2,1,0:T(8,128)(2,1)S(1)}, u32[]{:S(2)}, u32[]{:S(2)}) collective-permute-start(bf16[4,3,2,128,128]{4,3,2,1,0:T(8,128)(2,1)} %collective-permute-done.9.refs_8_), channel_id=1, source_target_pairs={{0,16},{16,32},{32,48},{48,64},{64,80},{80,96},{96,112},{112,0},{8... | collective-permute-start | bytes 2359304 | tf_op jit(solution)/shard_map/s_a4/ppermute | solution.py:46
  63.5 5.5 %attend.6 = (f32[17,3,128,128]{3,2,1,0:T(8,128)S(1)}, f32[17,16,128]{2,1,0:T(8,128)S(1)}) custom-call(s32[16]{0:T(128)S(1)} %select_reduce_fusion.9.refs_0_, s32[256]{0:T(256)S(1)} %get-tuple-element.70.refs_1_, s32[256]{0:T(256)S(1)} %compare_select_fusion.4.refs_2_, s32[16]{0:T(128)S(1)} %get-tuple-element.93.refs_3_, ...), custom_call_target="tpu_custom_call" | custom-call | flops 15360000000 | bytes 3145728 | tf_op jit(solution)/shard_map/attend/pallas_call | solution.py:244
  69.4 8.4 %collective-permute-done.10.refs_6_ = bf16[4,3,2,128,128]{4,3,2,1,0:T(8,128)(2,1)S(1)} collective-permute-done((bf16[4,3,2,128,128]{4,3,2,1,0:T(8,128)(2,1)}, bf16[4,3,2,128,128]{4,3,2,1,0:T(8,128)(2,1)S(1)}, u32[]{:S(2)}, u32[]{:S(2)}) %collective-permute-start.10) | collective-permute-done | bytes 786464 | tf_op jit(solution)/shard_map/s_a4/ppermute | solution.py:46
  77.8 5.1 %attend.7 = (f32[17,3,128,128]{3,2,1,0:T(8,128)S(1)}, f32[17,16,128]{2,1,0:T(8,128)S(1)}) custom-call(s32[16]{0:T(128)S(1)} %select_reduce_fusion.6.refs_0_, s32[256]{0:T(256)S(1)} %get-tuple-element.64.refs_1_, s32[256]{0:T(256)S(1)} %compare_select_fusion.1.refs_2_, s32[16]{0:T(128)S(1)} %get-tuple-element.91.refs_3_, ...), custom_call_target="tpu_custom_call" | custom-call | flops 15360000000 | bytes 3145728 | tf_op jit(solution)/shard_map/attend/pallas_call | solution.py:244
  82.9 2.8 %attend.8 = (f32[17,3,128,128]{3,2,1,0:T(8,128)S(1)}, f32[17,16,128]{2,1,0:T(8,128)S(1)}) custom-call(s32[16]{0:T(128)S(1)} %select_reduce_fusion.7.refs_0_, s32[256]{0:T(256)S(1)} %get-tuple-element.66.refs_1_, s32[256]{0:T(256)S(1)} %compare_select_fusion.2.refs_2_, s32[16]{0:T(128)S(1)} %get-tuple-element.95.refs_3_, ...), custom_call_target="tpu_custom_call" | custom-call | flops 7680000000 | bytes 1572864 | tf_op jit(solution)/shard_map/attend/pallas_call | solution.py:244
  85.7 3.9 %attend.9 = (bf16[2,400,128]{2,1,0:T(8,128)(2,1)S(1)}, bf16[2,400,128]{2,1,0:T(8,128)(2,1)S(1)}, bf16[2,400,128]{2,1,0:T(8,128)(2,1)S(1)}, bf16[2,400,128]{2,1,0...) custom-call(s32[16]{0:T(128)S(1)} %select_reduce_fusion.10.refs_0_, ...), custom_call_target="tpu_custom_call" | custom-call | flops 7680000000 | bytes 1572864 | tf_op jit(solution)/shard_map/attend/pallas_call | solution.py:244
  89.7 2.2 %collective-permute-start.21 = (bf16[2,400,128]{2,1,0:T(8,128)(2,1)S(1)}, bf16[2,400,128]{2,1,0:T(8,128)(2,1)S(1)}, u32[]{:S(2)}, u32[]{:S(2)}) collective-permute-start(bf16[2,400,128]{2,1,0:T(8,128)(2,1)S(1)} %get-tuple-element.54), channel_id=1, source_target_pairs={{0,1},{1,128},{128,129},{129,0},{2,3},{3,130},{130,131},{131,2},{4... | collective-permute-start | bytes 614408 | tf_op jit(solution)/shard_map/s_f0/ppermute | solution.py:34
  91.9 1.9 %collective-permute-start.22 = (bf16[2,400,128]{2,1,0:T(8,128)(2,1)S(1)}, bf16[2,400,128]{2,1,0:T(8,128)(2,1)S(1)}, u32[]{:S(2)}, u32[]{:S(2)}) collective-permute-start(bf16[2,400,128]{2,1,0:T(8,128)(2,1)S(1)} %get-tuple-element.56), channel_id=1, source_target_pairs={{0,129},{1,0},{128,1},{129,128},{2,131},{3,2},{130,3},{131,130},{4... | collective-permute-start | bytes 614408 | tf_op jit(solution)/shard_map/s_f1/ppermute | solution.py:34
  93.8 4.2 %collective-permute-start.27 = (bf16[2,400,128]{2,1,0:T(8,128)(2,1)S(1)}, bf16[2,400,128]{2,1,0:T(8,128)(2,1)S(1)}, u32[]{:S(2)}, u32[]{:S(2)}) collective-permute-start(bf16[2,400,128]{2,1,0:T(8,128)(2,1)S(1)} %get-tuple-element.61), channel_id=1, source_target_pairs={{0,1},{1,128},{128,129},{129,0},{2,3},{3,130},{130,131},{131,2},{4... | collective-permute-start | bytes 614408 | tf_op jit(solution)/shard_map/s_prv1/ppermute | solution.py:34
  98.1 4.8 %collective-permute-done.22.b0 = bf16[2,400,128]{2,1,0:T(8,128)(2,1)S(1)} collective-permute-done((bf16[2,400,128]{2,1,0:T(8,128)(2,1)S(1)}, bf16[2,400,128]{2,1,0:T(8,128)(2,1)S(1)}, u32[]{:S(2)}, u32[]{:S(2)}) %collective-permute-start.22) | collective-permute-done | bytes 204832 | tf_op jit(solution)/shard_map/s_f1/ppermute | solution.py:34
  103.5 2.4 %collective-permute-start.24 = (bf16[2,400,128]{2,1,0:T(8,128)(2,1)S(1)}, bf16[2,400,128]{2,1,0:T(8,128)(2,1)S(1)}, u32[]{:S(2)}, u32[]{:S(2)}) collective-permute-start(bf16[2,400,128]{2,1,0:T(8,128)(2,1)S(1)} %get-tuple-element.59), channel_id=1, source_target_pairs={{0,129},{1,0},{128,1},{129,128},{2,131},{3,2},{130,3},{131,130},{4... | collective-permute-start | bytes 614408 | tf_op jit(solution)/shard_map/s_nxt0/ppermute | solution.py:34
  105.9 5.5 %collective-permute-done.28.p1 = bf16[2,400,128]{2,1,0:T(8,128)(2,1)S(1)} collective-permute-done((bf16[2,400,128]{2,1,0:T(8,128)(2,1)S(1)}, bf16[2,400,128]{2,1,0:T(8,128)(2,1)S(1)}, u32[]{:S(2)}, u32[]{:S(2)}) %collective-permute-start.28) | collective-permute-done | bytes 204832 | tf_op jit(solution)/shard_map/s_nxt1/ppermute | solution.py:34
  111.7 3.2 %collective-permute-start.29 = (bf16[256,384]{1,0:T(8,128)(2,1)S(1)}, bf16[256,384]{1,0:T(8,128)(2,1)S(1)}, u32[]{:S(2)}, u32[]{:S(2)}) collective-permute-start(bf16[256,384]{1,0:T(8,128)(2,1)S(1)} %combine.3.refs_1_), channel_id=1, source_target_pairs={{0,6},{2,0},{4,2},{6,4},{1,7},{3,1},{5,3},{7,5},{8,14},{10,8},{12,... | collective-permute-start | bytes 589832 | tf_op jit(solution)/shard_map/s_right1/ppermute | solution.py:34
  115.9 2.0 %collective-permute-start.25 = (bf16[256,384]{1,0:T(8,128)(2,1)S(1)}, bf16[256,384]{1,0:T(8,128)(2,1)S(1)}, u32[]{:S(2)}, u32[]{:S(2)}) collective-permute-start(bf16[256,384]{1,0:T(8,128)(2,1)S(1)} %combine.2.refs_0_), channel_id=1, source_target_pairs={{0,2},{2,4},{4,6},{6,0},{1,3},{3,5},{5,7},{7,1},{8,10},{10,12},{12... | collective-permute-start | bytes 589832 | tf_op jit(solution)/shard_map/s_left0/ppermute | solution.py:34
  118.0 1.5 %collective-permute-start.31 = (bf16[256,384]{1,0:T(8,128)(2,1)S(1)}, bf16[256,384]{1,0:T(8,128)(2,1)S(1)}, u32[]{:S(2)}, u32[]{:S(2)}) collective-permute-start(bf16[256,384]{1,0:T(8,128)(2,1)S(1)} %combine.3.refs_1_), channel_id=1, source_target_pairs={{0,2},{2,4},{4,6},{6,0},{1,3},{3,5},{5,7},{7,1},{8,10},{10,12},{12... | collective-permute-start | bytes 589832 | tf_op jit(solution)/shard_map/s_left1/ppermute | solution.py:34
  119.4 1.8 %collective-permute-start.32 = (bf16[256,384]{1,0:T(8,128)(2,1)S(1)}, bf16[256,384]{1,0:T(8,128)(2,1)S(1)}, u32[]{:S(2)}, u32[]{:S(2)}) collective-permute-start(bf16[256,384]{1,0:T(8,128)(2,1)S(1)} %combine.2.refs_0_), channel_id=1, source_target_pairs={{0,6},{2,0},{4,2},{6,4},{1,7},{3,1},{5,3},{7,5},{8,14},{10,8},{12,... | collective-permute-start | bytes 589832 | tf_op jit(solution)/shard_map/s_right0/ppermute | solution.py:34
  121.2 1.6 %collective-permute-start.30 = (bf16[256,384]{1,0:T(8,128)(2,1)S(1)}, bf16[256,384]{1,0:T(8,128)(2,1)S(1)}, u32[]{:S(2)}, u32[]{:S(2)}) collective-permute-start(bf16[256,384]{1,0:T(8,128)(2,1)S(1)} %collective-permute-done.29.refs_5_), channel_id=1, source_target_pairs={{0,6},{2,0},{4,2},{6,4},{1,7},{3,1},{5,3},{7,5},{8,14},{10,8},{12,... | collective-permute-start | bytes 589832 | tf_op jit(solution)/shard_map/s_r2/ppermute | solution.py:34
  122.8 2.2 %collective-permute-done.25.refs_2_ = bf16[256,384]{1,0:T(8,128)(2,1)S(1)} collective-permute-done((bf16[256,384]{1,0:T(8,128)(2,1)S(1)}, bf16[256,384]{1,0:T(8,128)(2,1)S(1)}, u32[]{:S(2)}, u32[]{:S(2)}) %collective-permute-start.25) | collective-permute-done | bytes 196640 | tf_op jit(solution)/shard_map/s_left0/ppermute | solution.py:34
  125.0 0.8 collective-permute-start.26
  125.7 3.4 %collective-permute-done.31.refs_3_ = bf16[256,384]{1,0:T(8,128)(2,1)S(1)} collective-permute-done((bf16[256,384]{1,0:T(8,128)(2,1)S(1)}, bf16[256,384]{1,0:T(8,128)(2,1)S(1)}, u32[]{:S(2)}, u32[]{:S(2)}) %collective-permute-start.31) | collective-permute-done | bytes 196640 | tf_op jit(solution)/shard_map/s_left1/ppermute | solution.py:34
  129.2 1.4 %project.2.refs_3_ = f32[512,768]{1,0:T(8,128)S(1)} custom-call(bf16[256,384]{1,0:T(8,128)(2,1)S(1)} %combine.2.refs_0_, bf16[256,384]{1,0:T(8,128)(2,1)S(1)} %combine.3.refs_1_, bf16[256,384]{1,0:T(8,128)(2,1)S(1)} %collective-permute-done.25.refs_2_, bf16[256,384]{1,0:T(8,128)(2,1)S(1)} %collective-permute-done.31.refs_3_, ...), custom_call_target="tpu_custom_call" | custom-call | flops 1000000000 | bytes 4194304 | tf_op jit(solution)/shard_map/project/pallas_call | solution.py:364
  130.6 2.0 %collective-permute-done.26.refs_0_ = bf16[256,384]{1,0:T(8,128)(2,1)S(1)} collective-permute-done((bf16[256,384]{1,0:T(8,128)(2,1)S(1)}, bf16[256,384]{1,0:T(8,128)(2,1)S(1)}, u32[]{:S(2)}, u32[]{:S(2)}) %collective-permute-start.26) | collective-permute-done | bytes 196640 | tf_op jit(solution)/shard_map/s_l2/ppermute | solution.py:34
  132.6 1.5 %project.3 = bf16[512,768]{1,0:T(8,128)(2,1)} custom-call(bf16[256,384]{1,0:T(8,128)(2,1)S(1)} %collective-permute-done.26.refs_0_, bf16[256,384]{1,0:T(8,128)(2,1)S(1)} %collective-permute-done.30.refs_1_, bf16[384,768]{1,0:T(8,128)(2,1)S(1)} %get-tuple-element.76.refs_2_, f32[512,768]{1,0:T(8,128)S(1)} %project.2.refs_3_), custom_call_target="tpu_custom_call" | custom-call | flops 1000000000 | bytes 4194304 | tf_op jit(solution)/shard_map/project/pallas_call | solution.py:364
  (106 shorter events, 6.7 us)
Async XLA Ops:
  0.0 11.2 %copy-start = (s32[1,32]{1,0:T(1,128)S(1)}, s32[1,32]{1,0:T(1,128)}, u32[]{:S(2)}) copy-start(s32[1,32]{1,0:T(1,128)} %param.11) | copy-start | bytes 388
  0.0 6.5 %copy-start.8 = (s32[4,16]{1,0:T(4,128)S(1)}, s32[4,16]{1,0:T(4,128)}, u32[]{:S(2)}) copy-start(s32[4,16]{1,0:T(4,128)} %param.12) | copy-start | bytes 772
  0.0 9.3 %copy-start.6 = (bf16[384,3072]{1,0:T(8,128)(2,1)S(1)}, bf16[384,3072]{1,0:T(8,128)(2,1)}, u32[]{:S(2)}) copy-start(bf16[384,3072]{1,0:T(8,128)(2,1)} %param.10) | copy-start | bytes 7077892
  4.9 2.5 %collective-permute-start = (bf16[4,3,2,128,128]{4,3,2,1,0:T(8,128)(2,1)}, bf16[4,3,2,128,128]{4,3,2,1,0:T(8,128)(2,1)S(1)}, u32[]{:S(2)}, u32[]{:S(2)}) collective-permute-start(bf16[4,3,2,128,128]{4,3,2,1,0:T(8,128)(2,1)} %squares.1.refs_6_), channel_id=1, source_target_pairs={{0,8},{8,0},{1,9},{9,1},{2,10},{10,2},{3,11},{11,3},{4,12},{12,4},... | collective-permute-start | bytes 2359304 | tf_op jit(solution)/shard_map/s_tw/ppermute | solution.py:39
  4.9 24.2 %collective-permute-start.5 = (bf16[512,384]{1,0:T(8,128)(2,1)}, bf16[512,384]{1,0:T(8,128)(2,1)}, u32[]{:S(2)}, u32[]{:S(2)}) collective-permute-start(bf16[512,384]{1,0:T(8,128)(2,1)} %param.8), channel_id=1, source_target_pairs={{0,1},{1,128},{128,129},{129,0},{2,3},{3,130},{130,131},{131,2},{4... | collective-permute-start | bytes 1179656 | tf_op jit(solution)/shard_map/s_q_back/ppermute | solution.py:34
  7.4 18.7 %collective-permute-start.4 = (bf16[4,3,2,128,128]{4,3,2,1,0:T(8,128)(2,1)}, bf16[4,3,2,128,128]{4,3,2,1,0:T(8,128)(2,1)}, u32[]{:S(2)}, u32[]{:S(2)}) collective-permute-start(bf16[4,3,2,128,128]{4,3,2,1,0:T(8,128)(2,1)} %squares.1.refs_6_), channel_id=1, source_target_pairs={{0,16},{16,32},{32,48},{48,64},{64,80},{80,96},{96,112},{112,0},{8... | collective-permute-start | bytes 2359304 | tf_op jit(solution)/shard_map/s_a1/ppermute | solution.py:46
  9.5 2.7 %copy-start.12 = (s32[4]{0:T(128)S(1)}, s32[4]{0:T(128)}, u32[]{:S(2)}) copy-start(s32[4]{0:T(128)} %param.13) | copy-start | bytes 52
  12.2 10.5 %collective-permute-start.1 = (s32[1,128]{1,0:T(1,128)S(1)}, s32[1,128]{1,0:T(1,128)S(1)}, u32[]{:S(2)}, u32[]{:S(2)}) collective-permute-start(s32[1,128]{1,0:T(1,128)S(1)} %add_bitcast_fusion), channel_id=1, source_target_pairs={{0,1},{1,128},{128,129},{129,0},{2,3},{3,130},{130,131},{131,2},{4... | collective-permute-start | bytes 1544 | tf_op jit(solution)/shard_map/s_meta/ppermute | solution.py:34
  13.8 9.0 %collective-permute-start.2 = (s32[1,128]{1,0:T(1,128)S(1)}, s32[1,128]{1,0:T(1,128)S(1)}, u32[]{:S(2)}, u32[]{:S(2)}) collective-permute-start(s32[1,128]{1,0:T(1,128)S(1)} %add_bitcast_fusion), channel_id=1, source_target_pairs={{0,128},{1,129},{128,0},{129,1},{2,130},{3,131},{130,2},{131,3},{4... | collective-permute-start | bytes 1544 | tf_op jit(solution)/shard_map/s_meta/ppermute | solution.py:34
  16.7 9.4 %collective-permute-start.3 = (s32[1,128]{1,0:T(1,128)S(1)}, s32[1,128]{1,0:T(1,128)S(1)}, u32[]{:S(2)}, u32[]{:S(2)}) collective-permute-start(s32[1,128]{1,0:T(1,128)S(1)} %add_bitcast_fusion), channel_id=1, source_target_pairs={{0,129},{1,0},{128,1},{129,128},{2,131},{3,2},{130,3},{131,130},{4... | collective-permute-start | bytes 1544 | tf_op jit(solution)/shard_map/s_meta/ppermute | solution.py:34
  18.1 4.7 %copy-start.7 = (bf16[512,384]{1,0:T(8,128)(2,1)S(1)}, bf16[512,384]{1,0:T(8,128)(2,1)}, u32[]{:S(2)}) copy-start(bf16[512,384]{1,0:T(8,128)(2,1)} %param.8) | copy-start | bytes 1179652
  18.1 8.6 %copy-start.9 = (s32[5]{0:T(128)S(1)}, s32[5]{0:T(128)}, u32[]{:S(2)}) copy-start(s32[5]{0:T(128)} %constant.234.clone) | copy-start | bytes 64
  18.1 8.6 %copy-start.10 = (s32[5]{0:T(128)S(1)}, s32[5]{0:T(128)}, u32[]{:S(2)}) copy-start(s32[5]{0:T(128)} %constant.235.clone) | copy-start | bytes 64
  18.1 8.6 %copy-start.11 = (s32[5]{0:T(128)S(1)}, s32[5]{0:T(128)}, u32[]{:S(2)}) copy-start(s32[5]{0:T(128)} %constant.243) | copy-start | bytes 64
  18.1 37.8 %all-to-all-start = ((bf16[4,384,768]{2,1,0:T(8,128)(2,1)}), bf16[4,384,768]{2,1,0:T(8,128)(2,1)}, u32[]{:S(2)}, u32[]{:S(2)}) async-start(bf16[4,384,768]{2,1,0:T(8,128)(2,1)} %pad_maximum_fusion), calls=%async_computation | async-start | bytes 4718592 | tf_op jit(solution)/shard_map/all_to_all | solution.py:438
  22.7 23.9 %copy-start.1 = (bf16[4,3,2,128,128]{4,3,2,1,0:T(8,128)(2,1)S(1)}, bf16[4,3,2,128,128]{4,3,2,1,0:T(8,128)(2,1)}, u32[]{:S(2)}) copy-start(bf16[4,3,2,128,128]{4,3,2,1,0:T(8,128)(2,1)} %squares.1.refs_6_) | copy-start | bytes 2359300
  22.8 13.0 %collective-permute-start.7 = (bf16[512,384]{1,0:T(8,128)(2,1)S(1)}, bf16[512,384]{1,0:T(8,128)(2,1)}, u32[]{:S(2)}, u32[]{:S(2)}) collective-permute-start(bf16[512,384]{1,0:T(8,128)(2,1)S(1)} %copy-done.7), channel_id=1, source_target_pairs={{0,129},{1,0},{128,1},{129,128},{2,131},{3,2},{130,3},{131,130},{4... | collective-permute-start | bytes 1179656 | tf_op jit(solution)/shard_map/s_q_next/ppermute | solution.py:34
  22.9 12.7 %collective-permute-start.11 = (bf16[4,3,2,128,128]{4,3,2,1,0:T(8,128)(2,1)S(1)}, bf16[4,3,2,128,128]{4,3,2,1,0:T(8,128)(2,1)}, u32[]{:S(2)}, u32[]{:S(2)}) collective-permute-start(bf16[4,3,2,128,128]{4,3,2,1,0:T(8,128)(2,1)S(1)} %collective-permute-done.refs_7_), channel_id=1, source_target_pairs={{0,16},{16,32},{32,48},{48,64},{64,80},{80,96},{96,112},{112,0},{8... | collective-permute-start | bytes 2359304 | tf_op jit(solution)/shard_map/s_b1/ppermute | solution.py:46
  29.1 9.4 %collective-permute-start.6 = (bf16[512,384]{1,0:T(8,128)(2,1)}, bf16[512,384]{1,0:T(8,128)(2,1)}, u32[]{:S(2)}, u32[]{:S(2)}) collective-permute-start(bf16[512,384]{1,0:T(8,128)(2,1)} %collective-permute-done.5), channel_id=1, source_target_pairs={{0,1},{1,128},{128,129},{129,0},{2,3},{3,130},{130,131},{131,2},{4... | collective-permute-start | bytes 1179656 | tf_op jit(solution)/shard_map/s_q_far/ppermute | solution.py:34
  31.2 12.9 %collective-permute-start.8 = (bf16[4,3,2,128,128]{4,3,2,1,0:T(8,128)(2,1)}, bf16[4,3,2,128,128]{4,3,2,1,0:T(8,128)(2,1)}, u32[]{:S(2)}, u32[]{:S(2)}) collective-permute-start(bf16[4,3,2,128,128]{4,3,2,1,0:T(8,128)(2,1)} %collective-permute-done.4.refs_8_), channel_id=1, source_target_pairs={{0,16},{16,32},{32,48},{48,64},{64,80},{80,96},{96,112},{112,0},{8... | collective-permute-start | bytes 2359304 | tf_op jit(solution)/shard_map/s_a2/ppermute | solution.py:46
  34.6 12.0 %collective-permute-start.14 = (bf16[4,3,2,128,128]{4,3,2,1,0:T(8,128)(2,1)}, bf16[4,3,2,128,128]{4,3,2,1,0:T(8,128)(2,1)}, u32[]{:S(2)}, u32[]{:S(2)}) collective-permute-start(bf16[4,3,2,128,128]{4,3,2,1,0:T(8,128)(2,1)} %collective-permute-done.4.refs_8_), channel_id=1, source_target_pairs={{0,8},{8,0},{1,9},{9,1},{2,10},{10,2},{3,11},{11,3},{4,12},{12,4},... | collective-permute-start | bytes 2359304 | tf_op jit(solution)/shard_map/s_ta1/ppermute | solution.py:39
  35.6 19.4 %collective-permute-start.12 = (bf16[4,3,2,128,128]{4,3,2,1,0:T(8,128)(2,1)}, bf16[4,3,2,128,128]{4,3,2,1,0:T(8,128)(2,1)S(1)}, u32[]{:S(2)}, u32[]{:S(2)}) collective-permute-start(bf16[4,3,2,128,128]{4,3,2,1,0:T(8,128)(2,1)} %collective-permute-done.11.refs_6_), channel_id=1, source_target_pairs={{0,8},{8,0},{1,9},{9,1},{2,10},{10,2},{3,11},{11,3},{4,12},{12,4},... | collective-permute-start | bytes 2359304 | tf_op jit(solution)/shard_map/s_tb1/ppermute | solution.py:39
  35.8 18.5 %collective-permute-start.16 = (bf16[4,3,2,128,128]{4,3,2,1,0:T(8,128)(2,1)}, bf16[4,3,2,128,128]{4,3,2,1,0:T(8,128)(2,1)}, u32[]{:S(2)}, u32[]{:S(2)}) collective-permute-start(bf16[4,3,2,128,128]{4,3,2,1,0:T(8,128)(2,1)} %collective-permute-done.11.refs_6_), channel_id=1, source_target_pairs={{0,16},{16,32},{32,48},{48,64},{64,80},{80,96},{96,112},{112,0},{8... | collective-permute-start | bytes 2359304 | tf_op jit(solution)/shard_map/s_b2/ppermute | solution.py:46
  44.1 19.3 %collective-permute-start.13 = (bf16[4,3,2,128,128]{4,3,2,1,0:T(8,128)(2,1)}, bf16[4,3,2,128,128]{4,3,2,1,0:T(8,128)(2,1)}, u32[]{:S(2)}, u32[]{:S(2)}) collective-permute-start(bf16[4,3,2,128,128]{4,3,2,1,0:T(8,128)(2,1)} %collective-permute-done.8.refs_8_), channel_id=1, source_target_pairs={{0,8},{8,0},{1,9},{9,1},{2,10},{10,2},{3,11},{11,3},{4,12},{12,4},... | collective-permute-start | bytes 2359304 | tf_op jit(solution)/shard_map/s_ta2/ppermute | solution.py:39
  44.1 16.8 %collective-permute-start.9 = (bf16[4,3,2,128,128]{4,3,2,1,0:T(8,128)(2,1)}, bf16[4,3,2,128,128]{4,3,2,1,0:T(8,128)(2,1)}, u32[]{:S(2)}, u32[]{:S(2)}) collective-permute-start(bf16[4,3,2,128,128]{4,3,2,1,0:T(8,128)(2,1)} %collective-permute-done.8.refs_8_), channel_id=1, source_target_pairs={{0,16},{16,32},{32,48},{48,64},{64,80},{80,96},{96,112},{112,0},{8... | collective-permute-start | bytes 2359304 | tf_op jit(solution)/shard_map/s_a3/ppermute | solution.py:46
  52.5 1.7 %copy-start.4 = (f32[17,3,128,128]{3,2,1,0:T(8,128)}, f32[17,3,128,128]{3,2,1,0:T(8,128)S(1)}, u32[]{:S(2)}) copy-start(f32[17,3,128,128]{3,2,1,0:T(8,128)S(1)} %get-tuple-element.41.refs_10_) | copy-start | bytes 10027012
  54.2 15.2 %collective-permute-start.17 = (bf16[4,3,2,128,128]{4,3,2,1,0:T(8,128)(2,1)}, bf16[4,3,2,128,128]{4,3,2,1,0:T(8,128)(2,1)S(1)}, u32[]{:S(2)}, u32[]{:S(2)}) collective-permute-start(bf16[4,3,2,128,128]{4,3,2,1,0:T(8,128)(2,1)} %collective-permute-done.16.refs_6_), channel_id=1, source_target_pairs={{0,16},{16,32},{32,48},{48,64},{64,80},{80,96},{96,112},{112,0},{8... | collective-permute-start | bytes 2359304 | tf_op jit(solution)/shard_map/s_b3/ppermute | solution.py:46
  55.0 22.8 %collective-permute-start.19 = (bf16[4,3,2,128,128]{4,3,2,1,0:T(8,128)(2,1)}, bf16[4,3,2,128,128]{4,3,2,1,0:T(8,128)(2,1)}, u32[]{:S(2)}, u32[]{:S(2)}) collective-permute-start(bf16[4,3,2,128,128]{4,3,2,1,0:T(8,128)(2,1)} %collective-permute-done.16.refs_6_), channel_id=1, source_target_pairs={{0,8},{8,0},{1,9},{9,1},{2,10},{10,2},{3,11},{11,3},{4,12},{12,4},... | collective-permute-start | bytes 2359304 | tf_op jit(solution)/shard_map/s_tb2/ppermute | solution.py:39
  55.0 0.9 copy-start.2
  55.9 7.5 %copy-start.3 = (bf16[4,3,2,128,128]{4,3,2,1,0:T(8,128)(2,1)S(1)}, bf16[4,3,2,128,128]{4,3,2,1,0:T(8,128)(2,1)}, u32[]{:S(2)}) copy-start(bf16[4,3,2,128,128]{4,3,2,1,0:T(8,128)(2,1)} %copy-done.2) | copy-start | bytes 2359300
  55.9 7.5 %copy-start.5 = (f32[17,3,128,128]{3,2,1,0:T(8,128)S(1)}, f32[17,3,128,128]{3,2,1,0:T(8,128)}, u32[]{:S(2)}) copy-start(f32[17,3,128,128]{3,2,1,0:T(8,128)} %copy-done.4) | copy-start | bytes 10027012
  61.0 16.9 %collective-permute-start.20 = (bf16[4,3,2,128,128]{4,3,2,1,0:T(8,128)(2,1)}, bf16[4,3,2,128,128]{4,3,2,1,0:T(8,128)(2,1)S(1)}, u32[]{:S(2)}, u32[]{:S(2)}) collective-permute-start(bf16[4,3,2,128,128]{4,3,2,1,0:T(8,128)(2,1)} %collective-permute-done.9.refs_8_), channel_id=1, source_target_pairs={{0,8},{8,0},{1,9},{9,1},{2,10},{10,2},{3,11},{11,3},{4,12},{12,4},... | collective-permute-start | bytes 2359304 | tf_op jit(solution)/shard_map/s_ta3/ppermute | solution.py:39
  61.0 16.8 %collective-permute-start.10 = (bf16[4,3,2,128,128]{4,3,2,1,0:T(8,128)(2,1)}, bf16[4,3,2,128,128]{4,3,2,1,0:T(8,128)(2,1)S(1)}, u32[]{:S(2)}, u32[]{:S(2)}) collective-permute-start(bf16[4,3,2,128,128]{4,3,2,1,0:T(8,128)(2,1)} %collective-permute-done.9.refs_8_), channel_id=1, source_target_pairs={{0,16},{16,32},{32,48},{48,64},{64,80},{80,96},{96,112},{112,0},{8... | collective-permute-start | bytes 2359304 | tf_op jit(solution)/shard_map/s_a4/ppermute | solution.py:46
  69.4 13.5 %collective-permute-start.18 = (bf16[4,3,2,128,128]{4,3,2,1,0:T(8,128)(2,1)S(1)}, bf16[4,3,2,128,128]{4,3,2,1,0:T(8,128)(2,1)S(1)}, u32[]{:S(2)}, u32[]{:S(2)}) collective-permute-start(bf16[4,3,2,128,128]{4,3,2,1,0:T(8,128)(2,1)S(1)} %collective-permute-done.17.refs_6_), channel_id=1, source_target_pairs={{0,8},{8,0},{1,9},{9,1},{2,10},{10,2},{3,11},{11,3},{4,12},{12,4},... | collective-permute-start | bytes 2359304 | tf_op jit(solution)/shard_map/s_tb3/ppermute | solution.py:39
  77.8 7.9 %collective-permute-start.15 = (bf16[4,3,2,128,128]{4,3,2,1,0:T(8,128)(2,1)S(1)}, bf16[4,3,2,128,128]{4,3,2,1,0:T(8,128)(2,1)S(1)}, u32[]{:S(2)}, u32[]{:S(2)}) collective-permute-start(bf16[4,3,2,128,128]{4,3,2,1,0:T(8,128)(2,1)S(1)} %collective-permute-done.10.refs_6_), channel_id=1, source_target_pairs={{0,8},{8,0},{1,9},{9,1},{2,10},{10,2},{3,11},{11,3},{4,12},{12,4},... | collective-permute-start | bytes 2359304 | tf_op jit(solution)/shard_map/s_ta4/ppermute | solution.py:39
  89.7 8.4 %collective-permute-start.21 = (bf16[2,400,128]{2,1,0:T(8,128)(2,1)S(1)}, bf16[2,400,128]{2,1,0:T(8,128)(2,1)S(1)}, u32[]{:S(2)}, u32[]{:S(2)}) collective-permute-start(bf16[2,400,128]{2,1,0:T(8,128)(2,1)S(1)} %get-tuple-element.54), channel_id=1, source_target_pairs={{0,1},{1,128},{128,129},{129,0},{2,3},{3,130},{130,131},{131,2},{4... | collective-permute-start | bytes 614408 | tf_op jit(solution)/shard_map/s_f0/ppermute | solution.py:34
  91.9 11.0 %collective-permute-start.22 = (bf16[2,400,128]{2,1,0:T(8,128)(2,1)S(1)}, bf16[2,400,128]{2,1,0:T(8,128)(2,1)S(1)}, u32[]{:S(2)}, u32[]{:S(2)}) collective-permute-start(bf16[2,400,128]{2,1,0:T(8,128)(2,1)S(1)} %get-tuple-element.56), channel_id=1, source_target_pairs={{0,129},{1,0},{128,1},{129,128},{2,131},{3,2},{130,3},{131,130},{4... | collective-permute-start | bytes 614408 | tf_op jit(solution)/shard_map/s_f1/ppermute | solution.py:34
  93.8 12.1 %collective-permute-start.27 = (bf16[2,400,128]{2,1,0:T(8,128)(2,1)S(1)}, bf16[2,400,128]{2,1,0:T(8,128)(2,1)S(1)}, u32[]{:S(2)}, u32[]{:S(2)}) collective-permute-start(bf16[2,400,128]{2,1,0:T(8,128)(2,1)S(1)} %get-tuple-element.61), channel_id=1, source_target_pairs={{0,1},{1,128},{128,129},{129,0},{2,3},{3,130},{130,131},{131,2},{4... | collective-permute-start | bytes 614408 | tf_op jit(solution)/shard_map/s_prv1/ppermute | solution.py:34
  103.1 8.3 %collective-permute-start.28 = (bf16[2,400,128]{2,1,0:T(8,128)(2,1)S(1)}, bf16[2,400,128]{2,1,0:T(8,128)(2,1)S(1)}, u32[]{:S(2)}, u32[]{:S(2)}) collective-permute-start(bf16[2,400,128]{2,1,0:T(8,128)(2,1)S(1)} %get-tuple-element.62), channel_id=1, source_target_pairs={{0,129},{1,0},{128,1},{129,128},{2,131},{3,2},{130,3},{131,130},{4... | collective-permute-start | bytes 614408 | tf_op jit(solution)/shard_map/s_nxt1/ppermute | solution.py:34
  103.5 12.2 %collective-permute-start.24 = (bf16[2,400,128]{2,1,0:T(8,128)(2,1)S(1)}, bf16[2,400,128]{2,1,0:T(8,128)(2,1)S(1)}, u32[]{:S(2)}, u32[]{:S(2)}) collective-permute-start(bf16[2,400,128]{2,1,0:T(8,128)(2,1)S(1)} %get-tuple-element.59), channel_id=1, source_target_pairs={{0,129},{1,0},{128,1},{129,128},{2,131},{3,2},{130,3},{131,130},{4... | collective-permute-start | bytes 614408 | tf_op jit(solution)/shard_map/s_nxt0/ppermute | solution.py:34
  105.9 9.8 %collective-permute-start.23 = (bf16[2,400,128]{2,1,0:T(8,128)(2,1)S(1)}, bf16[2,400,128]{2,1,0:T(8,128)(2,1)S(1)}, u32[]{:S(2)}, u32[]{:S(2)}) collective-permute-start(bf16[2,400,128]{2,1,0:T(8,128)(2,1)S(1)} %get-tuple-element.58), channel_id=1, source_target_pairs={{0,1},{1,128},{128,129},{129,0},{2,3},{3,130},{130,131},{131,2},{4... | collective-permute-start | bytes 614408 | tf_op jit(solution)/shard_map/s_prv0/ppermute | solution.py:34
  111.7 9.5 %collective-permute-start.29 = (bf16[256,384]{1,0:T(8,128)(2,1)S(1)}, bf16[256,384]{1,0:T(8,128)(2,1)S(1)}, u32[]{:S(2)}, u32[]{:S(2)}) collective-permute-start(bf16[256,384]{1,0:T(8,128)(2,1)S(1)} %combine.3.refs_1_), channel_id=1, source_target_pairs={{0,6},{2,0},{4,2},{6,4},{1,7},{3,1},{5,3},{7,5},{8,14},{10,8},{12,... | collective-permute-start | bytes 589832 | tf_op jit(solution)/shard_map/s_right1/ppermute | solution.py:34
  115.9 9.0 %collective-permute-start.25 = (bf16[256,384]{1,0:T(8,128)(2,1)S(1)}, bf16[256,384]{1,0:T(8,128)(2,1)S(1)}, u32[]{:S(2)}, u32[]{:S(2)}) collective-permute-start(bf16[256,384]{1,0:T(8,128)(2,1)S(1)} %combine.2.refs_0_), channel_id=1, source_target_pairs={{0,2},{2,4},{4,6},{6,0},{1,3},{3,5},{5,7},{7,1},{8,10},{10,12},{12... | collective-permute-start | bytes 589832 | tf_op jit(solution)/shard_map/s_left0/ppermute | solution.py:34
  118.0 11.2 %collective-permute-start.31 = (bf16[256,384]{1,0:T(8,128)(2,1)S(1)}, bf16[256,384]{1,0:T(8,128)(2,1)S(1)}, u32[]{:S(2)}, u32[]{:S(2)}) collective-permute-start(bf16[256,384]{1,0:T(8,128)(2,1)S(1)} %combine.3.refs_1_), channel_id=1, source_target_pairs={{0,2},{2,4},{4,6},{6,0},{1,3},{3,5},{5,7},{7,1},{8,10},{10,12},{12... | collective-permute-start | bytes 589832 | tf_op jit(solution)/shard_map/s_left1/ppermute | solution.py:34
  119.4 9.8 %collective-permute-start.32 = (bf16[256,384]{1,0:T(8,128)(2,1)S(1)}, bf16[256,384]{1,0:T(8,128)(2,1)S(1)}, u32[]{:S(2)}, u32[]{:S(2)}) collective-permute-start(bf16[256,384]{1,0:T(8,128)(2,1)S(1)} %combine.2.refs_0_), channel_id=1, source_target_pairs={{0,6},{2,0},{4,2},{6,4},{1,7},{3,1},{5,3},{7,5},{8,14},{10,8},{12,... | collective-permute-start | bytes 589832 | tf_op jit(solution)/shard_map/s_right0/ppermute | solution.py:34
  121.2 9.4 %collective-permute-start.30 = (bf16[256,384]{1,0:T(8,128)(2,1)S(1)}, bf16[256,384]{1,0:T(8,128)(2,1)S(1)}, u32[]{:S(2)}, u32[]{:S(2)}) collective-permute-start(bf16[256,384]{1,0:T(8,128)(2,1)S(1)} %collective-permute-done.29.refs_5_), channel_id=1, source_target_pairs={{0,6},{2,0},{4,2},{6,4},{1,7},{3,1},{5,3},{7,5},{8,14},{10,8},{12,... | collective-permute-start | bytes 589832 | tf_op jit(solution)/shard_map/s_r2/ppermute | solution.py:34
  125.0 7.7 %collective-permute-start.26 = (bf16[256,384]{1,0:T(8,128)(2,1)S(1)}, bf16[256,384]{1,0:T(8,128)(2,1)S(1)}, u32[]{:S(2)}, u32[]{:S(2)}) collective-permute-start(bf16[256,384]{1,0:T(8,128)(2,1)S(1)} %collective-permute-done.25.refs_2_), channel_id=1, source_target_pairs={{0,2},{2,4},{4,6},{6,0},{1,3},{3,5},{5,7},{7,1},{8,10},{10,12},{12... | collective-permute-start | bytes 589832 | tf_op jit(solution)/shard_map/s_l2/ppermute | solution.py:34

commit v4 on v3

--- a/solution.py
+++ b/solution.py
@@ -22,7 +22,7 @@
 N_Z = 8
 EXTRA = 16
 ITEMS = 256
-SPANS = ((0, 16), (16, 32), (32, 48), (48, 56), (56, 64))
+SPANS = ((0, 16), (16, 32), (32, 48), (48, 64))
 
 
 def shift(n, by):
@@ -459,11 +459,10 @@
     state = attend(heads, plans[1], q, [b1, after(tb1, by_peer), a2, twin(a2, "ta2")], state)
     b3, a4 = after(b3, state[1]), after(a4, state[1])
     state = attend(heads, plans[2], q, [b2, twin(b2, "tb2"), a3, twin(a3, "ta3")], state)
-    state = attend(heads, plans[3], q, [b3, twin(b3, "tb3")], state)
-    ends = [after(a4, *weights), twin(a4, "ta4")]
+    ends = [b3, twin(b3, "tb3"), after(a4, *weights), twin(a4, "ta4")]
 
     far0, far1, prv0, prv1, nxt0, nxt1, near0, near1 = attend(
-        heads, plans[4], q, ends, state, tuple((t, 2) for t in (8, 10, 12, 14, 4, 6, 0, 2))
+        heads, plans[3], q, ends, state, tuple((t, 2) for t in (8, 10, 12, 14, 4, 6, 0, 2))
     )
     far0, far1 = hop(far0, COLUMN, N_COL, 1, "f0"), hop(far1, COLUMN, N_COL, -1, "f1")
     prv1, nxt0 = hop(prv1, COLUMN, N_COL, 1, "prv1"), hop(nxt0, COLUMN, N_COL, -1, "nxt0")

time: 133 us -> 131 us (0.985); the launches traced: 134 us -> 129 us
  waiting for transfers between devices: 36.4 us -> 32.3 us
    ppermute x18, waiting for transfers between devices: 19.1 us -> 13.2 us  [hop(): return lax.ppermute(x, axis, shift(n, by))]
    ppermute x7, waiting for transfers between devices: 16.6 us -> 18.3 us  [ring(): return lax.ppermute(x, ('z', 'core'), up + down)]
    pallas_call x5 -> x4, Pallas kernels: 23.2 us -> 22.3 us  [attend(): pl.pallas_call(functools.partial(attend_kernel, heads, len(kvs), spans, f...]
  transfers between devices with their start and end apart: 34 -> 34, of which waited for: 14 -> 12; matrix products, arithmetic and copies ran while one was open for 9% -> 9% of each run, Pallas kernels for 16% -> 14%
where the time goes in v4:
time: 131 us; the launch traced here: 129 us
  starting transfers between devices  52.2 us (40%)
  waiting for transfers between devices  32.3 us (25%)
  Pallas kernels  30.7 us (23%)
  other arithmetic  7.65 us (6%)
  local copies, waits for them, and re-layouts  6.04 us (5%)
    ppermute x18, starting transfers between devices, hop(): return lax.ppermute(x, axis, shift(n, by))  31.8 us
    pallas_call x4, Pallas kernels, attend(): pl.pallas_call(functools.partial(attend_kernel, heads, len(kvs), spans, f...  22.3 us
    ppermute x7, waiting for transfers between devices, ring(): return lax.ppermute(x, ('z', 'core'), up + down)  18.3 us
    ppermute x7, starting transfers between devices, ring(): return lax.ppermute(x, ('z', 'core'), up + down)  15.5 us
    ppermute x18, waiting for transfers between devices, hop(): return lax.ppermute(x, axis, shift(n, by))  13.2 us
    all_to_all x1, starting transfers between devices, shards(): lax.all_to_all(pieces, 'x', split_axis=0, concat_axis=0, tiled=True)  4.63 us
    pallas_call x2, Pallas kernels, project(): pl.pallas_call(functools.partial(project_kernel, len(pairs), bool(more)),...  2.86 us
  transfers between devices with their start and end apart: 34, of which 12 were waited for; matrix products, arithmetic and copies ran while one was open for 9% of the time, Pallas kernels for 14%

profile of v4, /device:TPU:64, one launch (start us, length us, event | category | flops | bytes accessed | tf_op | source)
XLA Modules:
  0.0 129.3 jit_solution(6709555204218822609)
XLA Ops:
  0.0 2.3 %fetch.1 = bf16[4,3,128,2,128]{4,3,2,1,0:T(2,128)(2,1)} custom-call(s32[1]{0:T(128)} %bitcast.parity, bf16[1024,2,384]{2,1,0:T(2,128)(2,1)} %kv.1), custom_call_target="tpu_custom_call" | custom-call | tf_op jit(solution)/shard_map/fetch/pallas_call | solution.py:87
  2.3 2.6 %squares.1.refs_6_ = bf16[4,3,2,128,128]{4,3,2,1,0:T(8,128)(2,1)} custom-call(bf16[4,3,256,128]{3,2,1,0:T(8,128)(2,1)} %bitcast.60), custom_call_target="tpu_custom_call" | custom-call | tf_op jit(solution)/shard_map/squares/pallas_call | solution.py:95
  4.9 1.6 %collective-permute-start.5 = (bf16[512,384]{1,0:T(8,128)(2,1)}, bf16[512,384]{1,0:T(8,128)(2,1)}, u32[]{:S(2)}, u32[]{:S(2)}) collective-permute-start(bf16[512,384]{1,0:T(8,128)(2,1)} %param.8), channel_id=1, source_target_pairs={{0,1},{1,128},{128,129},{129,0},{2,3},{3,130},{130,131},{131,2},{4... | collective-permute-start | bytes 1179656 | tf_op jit(solution)/shard_map/s_q_back/ppermute | solution.py:34
  6.6 0.8 collective-permute-done.refs_7_
  7.4 1.9 %collective-permute-start.4 = (bf16[4,3,2,128,128]{4,3,2,1,0:T(8,128)(2,1)}, bf16[4,3,2,128,128]{4,3,2,1,0:T(8,128)(2,1)}, u32[]{:S(2)}, u32[]{:S(2)}) collective-permute-start(bf16[4,3,2,128,128]{4,3,2,1,0:T(8,128)(2,1)} %squares.1.refs_6_), channel_id=1, source_target_pairs={{0,16},{16,32},{32,48},{48,64},{64,80},{80,96},{96,112},{112,0},{8... | collective-permute-start | bytes 2359304 | tf_op jit(solution)/shard_map/s_a1/ppermute | solution.py:46
  9.5 1.7 %pad_maximum_fusion = bf16[4,384,768]{2,1,0:T(8,128)(2,1)} fusion(bf16[1,384,768]{2,1,0:T(8,128)(2,1)S(1)} %get-tuple-element.74, bf16[1,384,768]{2,1,0:T(8,128)(2,1)S(1)} %get-tuple-element.75, bf16[1,384,768]{2,1,0:T(8,128)(2,1)S(1)} %get-tuple-element.76, bf16[1,384,768]{2,1,0:T(8,128)(2,1)S(1)} %get-tuple-element.73), kind=kLoop, calls=%fused_computation.1 | loop fusion | flops 3538944 | bytes 4718592 | tf_op jit(solution)/shard_map/stack | solution.py:437
  12.3 1.6 %collective-permute-start.1 = (s32[1,128]{1,0:T(1,128)S(1)}, s32[1,128]{1,0:T(1,128)S(1)}, u32[]{:S(2)}, u32[]{:S(2)}) collective-permute-start(s32[1,128]{1,0:T(1,128)S(1)} %add_bitcast_fusion), channel_id=1, source_target_pairs={{0,1},{1,128},{128,129},{129,0},{2,3},{3,130},{130,131},{131,2},{4... | collective-permute-start | bytes 1544 | tf_op jit(solution)/shard_map/s_meta/ppermute | solution.py:34
  13.9 2.9 %collective-permute-start.2 = (s32[1,128]{1,0:T(1,128)S(1)}, s32[1,128]{1,0:T(1,128)S(1)}, u32[]{:S(2)}, u32[]{:S(2)}) collective-permute-start(s32[1,128]{1,0:T(1,128)S(1)} %add_bitcast_fusion), channel_id=1, source_target_pairs={{0,128},{1,129},{128,0},{129,1},{2,130},{3,131},{130,2},{131,3},{4... | collective-permute-start | bytes 1544 | tf_op jit(solution)/shard_map/s_meta/ppermute | solution.py:34
  16.8 1.3 %collective-permute-start.3 = (s32[1,128]{1,0:T(1,128)S(1)}, s32[1,128]{1,0:T(1,128)S(1)}, u32[]{:S(2)}, u32[]{:S(2)}) collective-permute-start(s32[1,128]{1,0:T(1,128)S(1)} %add_bitcast_fusion), channel_id=1, source_target_pairs={{0,129},{1,0},{128,1},{129,128},{2,131},{3,2},{130,3},{131,130},{4... | collective-permute-start | bytes 1544 | tf_op jit(solution)/shard_map/s_meta/ppermute | solution.py:34
  18.1 4.6 %all-to-all-start = ((bf16[4,384,768]{2,1,0:T(8,128)(2,1)}), bf16[4,384,768]{2,1,0:T(8,128)(2,1)}, u32[]{:S(2)}, u32[]{:S(2)}) async-start(bf16[4,384,768]{2,1,0:T(8,128)(2,1)} %pad_maximum_fusion), calls=%async_computation | async-start | bytes 4718592 | tf_op jit(solution)/shard_map/all_to_all | solution.py:438
  22.9 3.2 %collective-permute-start.8 = (bf16[4,3,2,128,128]{4,3,2,1,0:T(8,128)(2,1)S(1)}, bf16[4,3,2,128,128]{4,3,2,1,0:T(8,128)(2,1)}, u32[]{:S(2)}, u32[]{:S(2)}) collective-permute-start(bf16[4,3,2,128,128]{4,3,2,1,0:T(8,128)(2,1)S(1)} %collective-permute-done.refs_7_), channel_id=1, source_target_pairs={{0,16},{16,32},{32,48},{48,64},{64,80},{80,96},{96,112},{112,0},{8... | collective-permute-start | bytes 2359304 | tf_op jit(solution)/shard_map/s_b1/ppermute | solution.py:46
  27.0 1.4 %convert_reduce_fusion = s32[4,16,20]{1,2,0:T(8,128)S(1)} fusion(pred[20,20]{1,0:T(8,128)(4,1)S(1)} %iota_compare_fusion.5, pred[4,16,20]{2,1,0:T(8,128)(4,1)S(1)} %get-tuple-element.68), kind=kLoop, calls=%fused_computation.5 | loop fusion | flops 75520 | bytes 6800 | tf_op jit(solution)/shard_map/reduce_sum | solution.py:402
  28.8 2.0 %collective-permute-start.6 = (bf16[512,384]{1,0:T(8,128)(2,1)}, bf16[512,384]{1,0:T(8,128)(2,1)}, u32[]{:S(2)}, u32[]{:S(2)}) collective-permute-start(bf16[512,384]{1,0:T(8,128)(2,1)} %collective-permute-done.5), channel_id=1, source_target_pairs={{0,1},{1,128},{128,129},{129,0},{2,3},{3,130},{130,131},{131,2},{4... | collective-permute-start | bytes 1179656 | tf_op jit(solution)/shard_map/s_q_far/ppermute | solution.py:34
  30.8 1.0 collective-permute-start.13
  32.0 1.4 %select_reduce_fusion = s32[4,16,20]{1,2,0:T(8,128)S(1)} fusion(s32[4,16,20]{2,1,0:T(8,128)S(1)} %get-tuple-element.81, s32[4,16,20]{2,1,0:T(8,128)S(1)} %copy.9, pred[4,16,20]{2,1,0:T(8,128)(4,1)S(1)} %get-tuple-element.68), kind=kLoop, calls=%fused_computation.3 | loop fusion | flops 101120 | bytes 16640 | tf_op jit(solution)/shard_map/reduce_sum | solution.py:404
  34.1 1.5 %collective-permute-done.8.refs_6_ = bf16[4,3,2,128,128]{4,3,2,1,0:T(8,128)(2,1)} collective-permute-done((bf16[4,3,2,128,128]{4,3,2,1,0:T(8,128)(2,1)S(1)}, bf16[4,3,2,128,128]{4,3,2,1,0:T(8,128)(2,1)}, u32[]{:S(2)}, u32[]{:S(2)}) %collective-permute-start.8) | collective-permute-done | bytes 786464 | tf_op jit(solution)/shard_map/s_b1/ppermute | solution.py:46
  35.6 2.7 %collective-permute-start.9 = (bf16[4,3,2,128,128]{4,3,2,1,0:T(8,128)(2,1)}, bf16[4,3,2,128,128]{4,3,2,1,0:T(8,128)(2,1)}, u32[]{:S(2)}, u32[]{:S(2)}) collective-permute-start(bf16[4,3,2,128,128]{4,3,2,1,0:T(8,128)(2,1)} %collective-permute-done.8.refs_6_), channel_id=1, source_target_pairs={{0,16},{16,32},{32,48},{48,64},{64,80},{80,96},{96,112},{112,0},{8... | collective-permute-start | bytes 2359304 | tf_op jit(solution)/shard_map/s_b2/ppermute | solution.py:46
  38.3 1.5 %pad_maximum_fusion.1 = bf16[2048,384]{1,0:T(8,128)(2,1)S(1)} fusion(bf16[512,384]{1,0:T(8,128)(2,1)} %collective-permute-done.7, bf16[512,384]{1,0:T(8,128)(2,1)} %collective-permute-done.6, bf16[512,384]{1,0:T(8,128)(2,1)} %collective-permute-done.5, bf16[512,384]{1,0:T(8,128)(2,1)} %param.8), kind=kLoop, calls=%fused_computation.2 | loop fusion | flops 6291456 | bytes 3145728 | tf_op jit(solution)/shard_map/concatenate | solution.py:449
  39.8 4.3 %collective-permute-done.13.refs_8_ = bf16[4,3,2,128,128]{4,3,2,1,0:T(8,128)(2,1)} collective-permute-done((bf16[4,3,2,128,128]{4,3,2,1,0:T(8,128)(2,1)}, bf16[4,3,2,128,128]{4,3,2,1,0:T(8,128)(2,1)}, u32[]{:S(2)}, u32[]{:S(2)}) %collective-permute-start.13) | collective-permute-done | bytes 786464 | tf_op jit(solution)/shard_map/s_a2/ppermute | solution.py:46
  44.1 2.5 %collective-permute-start.16 = (bf16[4,3,2,128,128]{4,3,2,1,0:T(8,128)(2,1)}, bf16[4,3,2,128,128]{4,3,2,1,0:T(8,128)(2,1)}, u32[]{:S(2)}, u32[]{:S(2)}) collective-permute-start(bf16[4,3,2,128,128]{4,3,2,1,0:T(8,128)(2,1)} %collective-permute-done.13.refs_8_), channel_id=1, source_target_pairs={{0,16},{16,32},{32,48},{48,64},{64,80},{80,96},{96,112},{112,0},{8... | collective-permute-start | bytes 2359304 | tf_op jit(solution)/shard_map/s_a3/ppermute | solution.py:46
  46.6 5.4 %attend.4 = (f32[17,3,128,128]{3,2,1,0:T(8,128)S(1)}, f32[17,16,128]{2,1,0:T(8,128)S(1)}) custom-call(s32[16]{0:T(128)S(1)} %select_reduce_fusion.7.refs_0_, s32[256]{0:T(256)S(1)} %get-tuple-element.64.refs_1_, s32[256]{0:T(256)S(1)} %compare_select_fusion.3.refs_2_, s32[16]{0:T(128)S(1)} %get-tuple-element.86.refs_3_, ...), custom_call_target="tpu_custom_call" | custom-call | flops 15360000000 | bytes 3145728 | tf_op jit(solution)/shard_map/attend/pallas_call | solution.py:244
  52.0 1.7 %copy-done.4 = f32[17,3,128,128]{3,2,1,0:T(8,128)} copy-done((f32[17,3,128,128]{3,2,1,0:T(8,128)}, f32[17,3,128,128]{3,2,1,0:T(8,128)S(1)}, u32[]{:S(2)}) %copy-start.4) | copy-done | bytes 3342360
  53.7 1.7 %collective-permute-start.11 = (bf16[4,3,2,128,128]{4,3,2,1,0:T(8,128)(2,1)}, bf16[4,3,2,128,128]{4,3,2,1,0:T(8,128)(2,1)S(1)}, u32[]{:S(2)}, u32[]{:S(2)}) collective-permute-start(bf16[4,3,2,128,128]{4,3,2,1,0:T(8,128)(2,1)} %collective-permute-done.9.refs_6_), channel_id=1, source_target_pairs={{0,16},{16,32},{32,48},{48,64},{64,80},{80,96},{96,112},{112,0},{8... | collective-permute-start | bytes 2359304 | tf_op jit(solution)/shard_map/s_b3/ppermute | solution.py:46
  55.5 0.9 copy-done.2
  56.3 1.9 %dynamic-slice_bitcast_fusion = (bf16[384,768]{1,0:T(8,128)(2,1)S(1)}, bf16[384,768]{1,0:T(8,128)(2,1)S(1)}, bf16[384,768]{1,0:T(8,128)(2,1)S(1)}, bf16[384,768]{1,0:T(8,128)(2,1)S(1)}) fusion(bf16[4,384,768]{2,1,0:T(8,128)(2,1)} %all-to-all-done, s32[]{:T(128)S(6)} %select_n.228, s32[]{:T(128)S(6)} %select_n.226, s32[]{:T(128)S(6)} %select_n.224, ...), kind=kLoop, calls=%fused_computation.7 | loop fusion | bytes 4718608 | tf_op jit(solution)/shard_map/jit(dynamic_index_in_dim)/squeeze | solution.py:440
  58.2 2.7 %collective-permute-done.16.refs_8_ = bf16[4,3,2,128,128]{4,3,2,1,0:T(8,128)(2,1)} collective-permute-done((bf16[4,3,2,128,128]{4,3,2,1,0:T(8,128)(2,1)}, bf16[4,3,2,128,128]{4,3,2,1,0:T(8,128)(2,1)}, u32[]{:S(2)}, u32[]{:S(2)}) %collective-permute-start.16) | collective-permute-done | bytes 786464 | tf_op jit(solution)/shard_map/s_a3/ppermute | solution.py:46
  61.0 2.5 %collective-permute-start.17 = (bf16[4,3,2,128,128]{4,3,2,1,0:T(8,128)(2,1)}, bf16[4,3,2,128,128]{4,3,2,1,0:T(8,128)(2,1)S(1)}, u32[]{:S(2)}, u32[]{:S(2)}) collective-permute-start(bf16[4,3,2,128,128]{4,3,2,1,0:T(8,128)(2,1)} %collective-permute-done.16.refs_8_), channel_id=1, source_target_pairs={{0,16},{16,32},{32,48},{48,64},{64,80},{80,96},{96,112},{112,0},{8... | collective-permute-start | bytes 2359304 | tf_op jit(solution)/shard_map/s_a4/ppermute | solution.py:46
  63.5 4.5 %attend.5 = (f32[17,3,128,128]{3,2,1,0:T(8,128)S(1)}, f32[17,16,128]{2,1,0:T(8,128)S(1)}) custom-call(s32[16]{0:T(128)S(1)} %select_reduce_fusion.6.refs_0_, s32[256]{0:T(256)S(1)} %get-tuple-element.62.refs_1_, s32[256]{0:T(256)S(1)} %compare_select_fusion.2.refs_2_, s32[16]{0:T(128)S(1)} %get-tuple-element.87.refs_3_, ...), custom_call_target="tpu_custom_call" | custom-call | flops 15360000000 | bytes 3145728 | tf_op jit(solution)/shard_map/attend/pallas_call | solution.py:244
  68.0 1.4 %collective-permute-done.11.refs_6_ = bf16[4,3,2,128,128]{4,3,2,1,0:T(8,128)(2,1)S(1)} collective-permute-done((bf16[4,3,2,128,128]{4,3,2,1,0:T(8,128)(2,1)}, bf16[4,3,2,128,128]{4,3,2,1,0:T(8,128)(2,1)S(1)}, u32[]{:S(2)}, u32[]{:S(2)}) %collective-permute-start.11) | collective-permute-done | bytes 786464 | tf_op jit(solution)/shard_map/s_b3/ppermute | solution.py:46
  69.4 8.4 %collective-permute-done.17.refs_8_ = bf16[4,3,2,128,128]{4,3,2,1,0:T(8,128)(2,1)S(1)} collective-permute-done((bf16[4,3,2,128,128]{4,3,2,1,0:T(8,128)(2,1)}, bf16[4,3,2,128,128]{4,3,2,1,0:T(8,128)(2,1)S(1)}, u32[]{:S(2)}, u32[]{:S(2)}) %collective-permute-start.17) | collective-permute-done | bytes 786464 | tf_op jit(solution)/shard_map/s_a4/ppermute | solution.py:46
  77.8 6.3 %attend.6 = (f32[17,3,128,128]{3,2,1,0:T(8,128)S(1)}, f32[17,16,128]{2,1,0:T(8,128)S(1)}) custom-call(s32[16]{0:T(128)S(1)} %select_reduce_fusion.5.refs_0_, s32[256]{0:T(256)S(1)} %get-tuple-element.60.refs_1_, s32[256]{0:T(256)S(1)} %compare_select_fusion.1.refs_2_, s32[16]{0:T(128)S(1)} %get-tuple-element.84.refs_3_, ...), custom_call_target="tpu_custom_call" | custom-call | flops 15360000000 | bytes 3145728 | tf_op jit(solution)/shard_map/attend/pallas_call | solution.py:244
  84.2 6.1 %attend.7 = (bf16[2,400,128]{2,1,0:T(8,128)(2,1)S(1)}, bf16[2,400,128]{2,1,0:T(8,128)(2,1)S(1)}, bf16[2,400,128]{2,1,0:T(8,128)(2,1)S(1)}, bf16[2,400,128]{2,1,0...) custom-call(s32[16]{0:T(128)S(1)} %select_reduce_fusion.8.refs_0_, ...), custom_call_target="tpu_custom_call" | custom-call | flops 15360000000 | bytes 3145728 | tf_op jit(solution)/shard_map/attend/pallas_call | solution.py:244
  90.3 5.5 %collective-permute-start.22 = (bf16[2,400,128]{2,1,0:T(8,128)(2,1)S(1)}, bf16[2,400,128]{2,1,0:T(8,128)(2,1)S(1)}, u32[]{:S(2)}, u32[]{:S(2)}) collective-permute-start(bf16[2,400,128]{2,1,0:T(8,128)(2,1)S(1)} %get-tuple-element.52), channel_id=1, source_target_pairs={{0,129},{1,0},{128,1},{129,128},{2,131},{3,2},{130,3},{131,130},{4... | collective-permute-start | bytes 614408 | tf_op jit(solution)/shard_map/s_f1/ppermute | solution.py:34
  95.8 1.2 collective-permute-start.27
  97.0 4.1 %collective-permute-done.21.a0 = bf16[2,400,128]{2,1,0:T(8,128)(2,1)S(1)} collective-permute-done((bf16[2,400,128]{2,1,0:T(8,128)(2,1)S(1)}, bf16[2,400,128]{2,1,0:T(8,128)(2,1)S(1)}, u32[]{:S(2)}, u32[]{:S(2)}) %collective-permute-start.21) | collective-permute-done | bytes 204832 | tf_op jit(solution)/shard_map/s_f0/ppermute | solution.py:34
  101.4 2.7 %collective-permute-start.28 = (bf16[2,400,128]{2,1,0:T(8,128)(2,1)S(1)}, bf16[2,400,128]{2,1,0:T(8,128)(2,1)S(1)}, u32[]{:S(2)}, u32[]{:S(2)}) collective-permute-start(bf16[2,400,128]{2,1,0:T(8,128)(2,1)S(1)} %get-tuple-element.58), channel_id=1, source_target_pairs={{0,129},{1,0},{128,1},{129,128},{2,131},{3,2},{130,3},{131,130},{4... | collective-permute-start | bytes 614408 | tf_op jit(solution)/shard_map/s_nxt1/ppermute | solution.py:34
  104.1 1.7 %collective-permute-start.24 = (bf16[2,400,128]{2,1,0:T(8,128)(2,1)S(1)}, bf16[2,400,128]{2,1,0:T(8,128)(2,1)S(1)}, u32[]{:S(2)}, u32[]{:S(2)}) collective-permute-start(bf16[2,400,128]{2,1,0:T(8,128)(2,1)S(1)} %get-tuple-element.55), channel_id=1, source_target_pairs={{0,129},{1,0},{128,1},{129,128},{2,131},{3,2},{130,3},{131,130},{4... | collective-permute-start | bytes 614408 | tf_op jit(solution)/shard_map/s_nxt0/ppermute | solution.py:34
  106.1 2.0 %collective-permute-done.28.p1 = bf16[2,400,128]{2,1,0:T(8,128)(2,1)S(1)} collective-permute-done((bf16[2,400,128]{2,1,0:T(8,128)(2,1)S(1)}, bf16[2,400,128]{2,1,0:T(8,128)(2,1)S(1)}, u32[]{:S(2)}, u32[]{:S(2)}) %collective-permute-start.28) | collective-permute-done | bytes 204832 | tf_op jit(solution)/shard_map/s_nxt1/ppermute | solution.py:34
  108.3 3.2 %collective-permute-start.29 = (bf16[256,384]{1,0:T(8,128)(2,1)S(1)}, bf16[256,384]{1,0:T(8,128)(2,1)S(1)}, u32[]{:S(2)}, u32[]{:S(2)}) collective-permute-start(bf16[256,384]{1,0:T(8,128)(2,1)S(1)} %combine.3.refs_1_), channel_id=1, source_target_pairs={{0,6},{2,0},{4,2},{6,4},{1,7},{3,1},{5,3},{7,5},{8,14},{10,8},{12,... | collective-permute-start | bytes 589832 | tf_op jit(solution)/shard_map/s_right1/ppermute | solution.py:34
  111.6 1.2 collective-permute-done.23.p0
  113.0 2.0 %collective-permute-start.25 = (bf16[256,384]{1,0:T(8,128)(2,1)S(1)}, bf16[256,384]{1,0:T(8,128)(2,1)S(1)}, u32[]{:S(2)}, u32[]{:S(2)}) collective-permute-start(bf16[256,384]{1,0:T(8,128)(2,1)S(1)} %combine.2.refs_0_), channel_id=1, source_target_pairs={{0,2},{2,4},{4,6},{6,0},{1,3},{3,5},{5,7},{7,1},{8,10},{10,12},{12... | collective-permute-start | bytes 589832 | tf_op jit(solution)/shard_map/s_left0/ppermute | solution.py:34
  115.0 1.5 %collective-permute-start.31 = (bf16[256,384]{1,0:T(8,128)(2,1)S(1)}, bf16[256,384]{1,0:T(8,128)(2,1)S(1)}, u32[]{:S(2)}, u32[]{:S(2)}) collective-permute-start(bf16[256,384]{1,0:T(8,128)(2,1)S(1)} %combine.3.refs_1_), channel_id=1, source_target_pairs={{0,2},{2,4},{4,6},{6,0},{1,3},{3,5},{5,7},{7,1},{8,10},{10,12},{12... | collective-permute-start | bytes 589832 | tf_op jit(solution)/shard_map/s_left1/ppermute | solution.py:34
  116.5 1.8 %collective-permute-start.32 = (bf16[256,384]{1,0:T(8,128)(2,1)S(1)}, bf16[256,384]{1,0:T(8,128)(2,1)S(1)}, u32[]{:S(2)}, u32[]{:S(2)}) collective-permute-start(bf16[256,384]{1,0:T(8,128)(2,1)S(1)} %combine.2.refs_0_), channel_id=1, source_target_pairs={{0,6},{2,0},{4,2},{6,4},{1,7},{3,1},{5,3},{7,5},{8,14},{10,8},{12,... | collective-permute-start | bytes 589832 | tf_op jit(solution)/shard_map/s_right0/ppermute | solution.py:34
  118.3 2.3 %collective-permute-start.30 = (bf16[256,384]{1,0:T(8,128)(2,1)S(1)}, bf16[256,384]{1,0:T(8,128)(2,1)S(1)}, u32[]{:S(2)}, u32[]{:S(2)}) collective-permute-start(bf16[256,384]{1,0:T(8,128)(2,1)S(1)} %collective-permute-done.29.refs_5_), channel_id=1, source_target_pairs={{0,6},{2,0},{4,2},{6,4},{1,7},{3,1},{5,3},{7,5},{8,14},{10,8},{12,... | collective-permute-start | bytes 589832 | tf_op jit(solution)/shard_map/s_r2/ppermute | solution.py:34
  120.9 2.1 %collective-permute-done.31.refs_3_ = bf16[256,384]{1,0:T(8,128)(2,1)S(1)} collective-permute-done((bf16[256,384]{1,0:T(8,128)(2,1)S(1)}, bf16[256,384]{1,0:T(8,128)(2,1)S(1)}, u32[]{:S(2)}, u32[]{:S(2)}) %collective-permute-start.31) | collective-permute-done | bytes 196640 | tf_op jit(solution)/shard_map/s_left1/ppermute | solution.py:34
  123.0 1.4 %project.2.refs_3_ = f32[512,768]{1,0:T(8,128)S(1)} custom-call(bf16[256,384]{1,0:T(8,128)(2,1)S(1)} %combine.2.refs_0_, bf16[256,384]{1,0:T(8,128)(2,1)S(1)} %combine.3.refs_1_, bf16[256,384]{1,0:T(8,128)(2,1)S(1)} %collective-permute-done.25.refs_2_, bf16[256,384]{1,0:T(8,128)(2,1)S(1)} %collective-permute-done.31.refs_3_, ...), custom_call_target="tpu_custom_call" | custom-call | flops 1000000000 | bytes 4194304 | tf_op jit(solution)/shard_map/project/pallas_call | solution.py:364
  124.4 3.4 %collective-permute-done.26.refs_0_ = bf16[256,384]{1,0:T(8,128)(2,1)S(1)} collective-permute-done((bf16[256,384]{1,0:T(8,128)(2,1)S(1)}, bf16[256,384]{1,0:T(8,128)(2,1)S(1)}, u32[]{:S(2)}, u32[]{:S(2)}) %collective-permute-start.26) | collective-permute-done | bytes 196640 | tf_op jit(solution)/shard_map/s_l2/ppermute | solution.py:34
  127.8 1.5 %project.3 = bf16[512,768]{1,0:T(8,128)(2,1)} custom-call(bf16[256,384]{1,0:T(8,128)(2,1)S(1)} %collective-permute-done.26.refs_0_, bf16[256,384]{1,0:T(8,128)(2,1)S(1)} %collective-permute-done.30.refs_1_, bf16[384,768]{1,0:T(8,128)(2,1)S(1)} %get-tuple-element.70.refs_2_, f32[512,768]{1,0:T(8,128)S(1)} %project.2.refs_3_), custom_call_target="tpu_custom_call" | custom-call | flops 1000000000 | bytes 4194304 | tf_op jit(solution)/shard_map/project/pallas_call | solution.py:364
  (99 shorter events, 5.0 us)
Async XLA Ops:
  0.0 11.2 %copy-start = (s32[1,32]{1,0:T(1,128)S(1)}, s32[1,32]{1,0:T(1,128)}, u32[]{:S(2)}) copy-start(s32[1,32]{1,0:T(1,128)} %param.11) | copy-start | bytes 388
  0.0 6.5 %copy-start.8 = (s32[4,16]{1,0:T(4,128)S(1)}, s32[4,16]{1,0:T(4,128)}, u32[]{:S(2)}) copy-start(s32[4,16]{1,0:T(4,128)} %param.12) | copy-start | bytes 772
  0.0 9.3 %copy-start.6 = (bf16[384,3072]{1,0:T(8,128)(2,1)S(1)}, bf16[384,3072]{1,0:T(8,128)(2,1)}, u32[]{:S(2)}) copy-start(bf16[384,3072]{1,0:T(8,128)(2,1)} %param.10) | copy-start | bytes 7077892
  4.9 2.5 %collective-permute-start = (bf16[4,3,2,128,128]{4,3,2,1,0:T(8,128)(2,1)}, bf16[4,3,2,128,128]{4,3,2,1,0:T(8,128)(2,1)S(1)}, u32[]{:S(2)}, u32[]{:S(2)}) collective-permute-start(bf16[4,3,2,128,128]{4,3,2,1,0:T(8,128)(2,1)} %squares.1.refs_6_), channel_id=1, source_target_pairs={{0,8},{8,0},{1,9},{9,1},{2,10},{10,2},{3,11},{11,3},{4,12},{12,4},... | collective-permute-start | bytes 2359304 | tf_op jit(solution)/shard_map/s_tw/ppermute | solution.py:39
  4.9 23.9 %collective-permute-start.5 = (bf16[512,384]{1,0:T(8,128)(2,1)}, bf16[512,384]{1,0:T(8,128)(2,1)}, u32[]{:S(2)}, u32[]{:S(2)}) collective-permute-start(bf16[512,384]{1,0:T(8,128)(2,1)} %param.8), channel_id=1, source_target_pairs={{0,1},{1,128},{128,129},{129,0},{2,3},{3,130},{130,131},{131,2},{4... | collective-permute-start | bytes 1179656 | tf_op jit(solution)/shard_map/s_q_back/ppermute | solution.py:34
  7.4 18.7 %collective-permute-start.4 = (bf16[4,3,2,128,128]{4,3,2,1,0:T(8,128)(2,1)}, bf16[4,3,2,128,128]{4,3,2,1,0:T(8,128)(2,1)}, u32[]{:S(2)}, u32[]{:S(2)}) collective-permute-start(bf16[4,3,2,128,128]{4,3,2,1,0:T(8,128)(2,1)} %squares.1.refs_6_), channel_id=1, source_target_pairs={{0,16},{16,32},{32,48},{48,64},{64,80},{80,96},{96,112},{112,0},{8... | collective-permute-start | bytes 2359304 | tf_op jit(solution)/shard_map/s_a1/ppermute | solution.py:46
  9.5 2.7 %copy-start.10 = (s32[4]{0:T(128)S(1)}, s32[4]{0:T(128)}, u32[]{:S(2)}) copy-start(s32[4]{0:T(128)} %param.13) | copy-start | bytes 52
  12.3 10.5 %collective-permute-start.1 = (s32[1,128]{1,0:T(1,128)S(1)}, s32[1,128]{1,0:T(1,128)S(1)}, u32[]{:S(2)}, u32[]{:S(2)}) collective-permute-start(s32[1,128]{1,0:T(1,128)S(1)} %add_bitcast_fusion), channel_id=1, source_target_pairs={{0,1},{1,128},{128,129},{129,0},{2,3},{3,130},{130,131},{131,2},{4... | collective-permute-start | bytes 1544 | tf_op jit(solution)/shard_map/s_meta/ppermute | solution.py:34
  13.9 9.0 %collective-permute-start.2 = (s32[1,128]{1,0:T(1,128)S(1)}, s32[1,128]{1,0:T(1,128)S(1)}, u32[]{:S(2)}, u32[]{:S(2)}) collective-permute-start(s32[1,128]{1,0:T(1,128)S(1)} %add_bitcast_fusion), channel_id=1, source_target_pairs={{0,128},{1,129},{128,0},{129,1},{2,130},{3,131},{130,2},{131,3},{4... | collective-permute-start | bytes 1544 | tf_op jit(solution)/shard_map/s_meta/ppermute | solution.py:34
  16.8 9.3 %collective-permute-start.3 = (s32[1,128]{1,0:T(1,128)S(1)}, s32[1,128]{1,0:T(1,128)S(1)}, u32[]{:S(2)}, u32[]{:S(2)}) collective-permute-start(s32[1,128]{1,0:T(1,128)S(1)} %add_bitcast_fusion), channel_id=1, source_target_pairs={{0,129},{1,0},{128,1},{129,128},{2,131},{3,2},{130,3},{131,130},{4... | collective-permute-start | bytes 1544 | tf_op jit(solution)/shard_map/s_meta/ppermute | solution.py:34
  18.1 4.7 %copy-start.7 = (bf16[512,384]{1,0:T(8,128)(2,1)S(1)}, bf16[512,384]{1,0:T(8,128)(2,1)}, u32[]{:S(2)}) copy-start(bf16[512,384]{1,0:T(8,128)(2,1)} %param.8) | copy-start | bytes 1179652
  18.1 8.5 %copy-start.9 = (s32[4]{0:T(128)S(1)}, s32[4]{0:T(128)}, u32[]{:S(2)}) copy-start(s32[4]{0:T(128)} %constant.226.clone) | copy-start | bytes 52
  18.1 38.2 %all-to-all-start = ((bf16[4,384,768]{2,1,0:T(8,128)(2,1)}), bf16[4,384,768]{2,1,0:T(8,128)(2,1)}, u32[]{:S(2)}, u32[]{:S(2)}) async-start(bf16[4,384,768]{2,1,0:T(8,128)(2,1)} %pad_maximum_fusion), calls=%async_computation | async-start | bytes 4718592 | tf_op jit(solution)/shard_map/all_to_all | solution.py:438
  22.7 23.9 %copy-start.1 = (bf16[4,3,2,128,128]{4,3,2,1,0:T(8,128)(2,1)S(1)}, bf16[4,3,2,128,128]{4,3,2,1,0:T(8,128)(2,1)}, u32[]{:S(2)}) copy-start(bf16[4,3,2,128,128]{4,3,2,1,0:T(8,128)(2,1)} %squares.1.refs_6_) | copy-start | bytes 2359300
  22.8 12.8 %collective-permute-start.7 = (bf16[512,384]{1,0:T(8,128)(2,1)S(1)}, bf16[512,384]{1,0:T(8,128)(2,1)}, u32[]{:S(2)}, u32[]{:S(2)}) collective-permute-start(bf16[512,384]{1,0:T(8,128)(2,1)S(1)} %copy-done.7), channel_id=1, source_target_pairs={{0,129},{1,0},{128,1},{129,128},{2,131},{3,2},{130,3},{131,130},{4... | collective-permute-start | bytes 1179656 | tf_op jit(solution)/shard_map/s_q_next/ppermute | solution.py:34
  22.9 12.7 %collective-permute-start.8 = (bf16[4,3,2,128,128]{4,3,2,1,0:T(8,128)(2,1)S(1)}, bf16[4,3,2,128,128]{4,3,2,1,0:T(8,128)(2,1)}, u32[]{:S(2)}, u32[]{:S(2)}) collective-permute-start(bf16[4,3,2,128,128]{4,3,2,1,0:T(8,128)(2,1)S(1)} %collective-permute-done.refs_7_), channel_id=1, source_target_pairs={{0,16},{16,32},{32,48},{48,64},{64,80},{80,96},{96,112},{112,0},{8... | collective-permute-start | bytes 2359304 | tf_op jit(solution)/shard_map/s_b1/ppermute | solution.py:46
  28.8 9.5 %collective-permute-start.6 = (bf16[512,384]{1,0:T(8,128)(2,1)}, bf16[512,384]{1,0:T(8,128)(2,1)}, u32[]{:S(2)}, u32[]{:S(2)}) collective-permute-start(bf16[512,384]{1,0:T(8,128)(2,1)} %collective-permute-done.5), channel_id=1, source_target_pairs={{0,1},{1,128},{128,129},{129,0},{2,3},{3,130},{130,131},{131,2},{4... | collective-permute-start | bytes 1179656 | tf_op jit(solution)/shard_map/s_q_far/ppermute | solution.py:34
  30.8 13.3 %collective-permute-start.13 = (bf16[4,3,2,128,128]{4,3,2,1,0:T(8,128)(2,1)}, bf16[4,3,2,128,128]{4,3,2,1,0:T(8,128)(2,1)}, u32[]{:S(2)}, u32[]{:S(2)}) collective-permute-start(bf16[4,3,2,128,128]{4,3,2,1,0:T(8,128)(2,1)} %collective-permute-done.4.refs_8_), channel_id=1, source_target_pairs={{0,16},{16,32},{32,48},{48,64},{64,80},{80,96},{96,112},{112,0},{8... | collective-permute-start | bytes 2359304 | tf_op jit(solution)/shard_map/s_a2/ppermute | solution.py:46
  33.4 13.2 %collective-permute-start.10 = (bf16[4,3,2,128,128]{4,3,2,1,0:T(8,128)(2,1)}, bf16[4,3,2,128,128]{4,3,2,1,0:T(8,128)(2,1)}, u32[]{:S(2)}, u32[]{:S(2)}) collective-permute-start(bf16[4,3,2,128,128]{4,3,2,1,0:T(8,128)(2,1)} %collective-permute-done.4.refs_8_), channel_id=1, source_target_pairs={{0,8},{8,0},{1,9},{9,1},{2,10},{10,2},{3,11},{11,3},{4,12},{12,4},... | collective-permute-start | bytes 2359304 | tf_op jit(solution)/shard_map/s_ta1/ppermute | solution.py:39
  35.6 19.9 %collective-permute-start.12 = (bf16[4,3,2,128,128]{4,3,2,1,0:T(8,128)(2,1)}, bf16[4,3,2,128,128]{4,3,2,1,0:T(8,128)(2,1)S(1)}, u32[]{:S(2)}, u32[]{:S(2)}) collective-permute-start(bf16[4,3,2,128,128]{4,3,2,1,0:T(8,128)(2,1)} %collective-permute-done.8.refs_6_), channel_id=1, source_target_pairs={{0,8},{8,0},{1,9},{9,1},{2,10},{10,2},{3,11},{11,3},{4,12},{12,4},... | collective-permute-start | bytes 2359304 | tf_op jit(solution)/shard_map/s_tb1/ppermute | solution.py:39
  35.6 18.1 %collective-permute-start.9 = (bf16[4,3,2,128,128]{4,3,2,1,0:T(8,128)(2,1)}, bf16[4,3,2,128,128]{4,3,2,1,0:T(8,128)(2,1)}, u32[]{:S(2)}, u32[]{:S(2)}) collective-permute-start(bf16[4,3,2,128,128]{4,3,2,1,0:T(8,128)(2,1)} %collective-permute-done.8.refs_6_), channel_id=1, source_target_pairs={{0,16},{16,32},{32,48},{48,64},{64,80},{80,96},{96,112},{112,0},{8... | collective-permute-start | bytes 2359304 | tf_op jit(solution)/shard_map/s_b2/ppermute | solution.py:46
  44.1 19.3 %collective-permute-start.14 = (bf16[4,3,2,128,128]{4,3,2,1,0:T(8,128)(2,1)}, bf16[4,3,2,128,128]{4,3,2,1,0:T(8,128)(2,1)}, u32[]{:S(2)}, u32[]{:S(2)}) collective-permute-start(bf16[4,3,2,128,128]{4,3,2,1,0:T(8,128)(2,1)} %collective-permute-done.13.refs_8_), channel_id=1, source_target_pairs={{0,8},{8,0},{1,9},{9,1},{2,10},{10,2},{3,11},{11,3},{4,12},{12,4},... | collective-permute-start | bytes 2359304 | tf_op jit(solution)/shard_map/s_ta2/ppermute | solution.py:39
  44.1 16.8 %collective-permute-start.16 = (bf16[4,3,2,128,128]{4,3,2,1,0:T(8,128)(2,1)}, bf16[4,3,2,128,128]{4,3,2,1,0:T(8,128)(2,1)}, u32[]{:S(2)}, u32[]{:S(2)}) collective-permute-start(bf16[4,3,2,128,128]{4,3,2,1,0:T(8,128)(2,1)} %collective-permute-done.13.refs_8_), channel_id=1, source_target_pairs={{0,16},{16,32},{32,48},{48,64},{64,80},{80,96},{96,112},{112,0},{8... | collective-permute-start | bytes 2359304 | tf_op jit(solution)/shard_map/s_a3/ppermute | solution.py:46
  52.0 1.7 %copy-start.4 = (f32[17,3,128,128]{3,2,1,0:T(8,128)}, f32[17,3,128,128]{3,2,1,0:T(8,128)S(1)}, u32[]{:S(2)}) copy-start(f32[17,3,128,128]{3,2,1,0:T(8,128)S(1)} %get-tuple-element.41.refs_10_) | copy-start | bytes 10027012
  53.7 15.7 %collective-permute-start.11 = (bf16[4,3,2,128,128]{4,3,2,1,0:T(8,128)(2,1)}, bf16[4,3,2,128,128]{4,3,2,1,0:T(8,128)(2,1)S(1)}, u32[]{:S(2)}, u32[]{:S(2)}) collective-permute-start(bf16[4,3,2,128,128]{4,3,2,1,0:T(8,128)(2,1)} %collective-permute-done.9.refs_6_), channel_id=1, source_target_pairs={{0,16},{16,32},{32,48},{48,64},{64,80},{80,96},{96,112},{112,0},{8... | collective-permute-start | bytes 2359304 | tf_op jit(solution)/shard_map/s_b3/ppermute | solution.py:46
  55.4 22.4 %collective-permute-start.19 = (bf16[4,3,2,128,128]{4,3,2,1,0:T(8,128)(2,1)}, bf16[4,3,2,128,128]{4,3,2,1,0:T(8,128)(2,1)S(1)}, u32[]{:S(2)}, u32[]{:S(2)}) collective-permute-start(bf16[4,3,2,128,128]{4,3,2,1,0:T(8,128)(2,1)} %collective-permute-done.9.refs_6_), channel_id=1, source_target_pairs={{0,8},{8,0},{1,9},{9,1},{2,10},{10,2},{3,11},{11,3},{4,12},{12,4},... | collective-permute-start | bytes 2359304 | tf_op jit(solution)/shard_map/s_tb2/ppermute | solution.py:39
  55.5 0.9 copy-start.2
  56.3 7.1 %copy-start.3 = (bf16[4,3,2,128,128]{4,3,2,1,0:T(8,128)(2,1)S(1)}, bf16[4,3,2,128,128]{4,3,2,1,0:T(8,128)(2,1)}, u32[]{:S(2)}) copy-start(bf16[4,3,2,128,128]{4,3,2,1,0:T(8,128)(2,1)} %copy-done.2) | copy-start | bytes 2359300
  56.3 7.1 %copy-start.5 = (f32[17,3,128,128]{3,2,1,0:T(8,128)S(1)}, f32[17,3,128,128]{3,2,1,0:T(8,128)}, u32[]{:S(2)}) copy-start(f32[17,3,128,128]{3,2,1,0:T(8,128)} %copy-done.4) | copy-start | bytes 10027012
  61.0 16.9 %collective-permute-start.20 = (bf16[4,3,2,128,128]{4,3,2,1,0:T(8,128)(2,1)}, bf16[4,3,2,128,128]{4,3,2,1,0:T(8,128)(2,1)S(1)}, u32[]{:S(2)}, u32[]{:S(2)}) collective-permute-start(bf16[4,3,2,128,128]{4,3,2,1,0:T(8,128)(2,1)} %collective-permute-done.16.refs_8_), channel_id=1, source_target_pairs={{0,8},{8,0},{1,9},{9,1},{2,10},{10,2},{3,11},{11,3},{4,12},{12,4},... | collective-permute-start | bytes 2359304 | tf_op jit(solution)/shard_map/s_ta3/ppermute | solution.py:39
  61.0 16.8 %collective-permute-start.17 = (bf16[4,3,2,128,128]{4,3,2,1,0:T(8,128)(2,1)}, bf16[4,3,2,128,128]{4,3,2,1,0:T(8,128)(2,1)S(1)}, u32[]{:S(2)}, u32[]{:S(2)}) collective-permute-start(bf16[4,3,2,128,128]{4,3,2,1,0:T(8,128)(2,1)} %collective-permute-done.16.refs_8_), channel_id=1, source_target_pairs={{0,16},{16,32},{32,48},{48,64},{64,80},{80,96},{96,112},{112,0},{8... | collective-permute-start | bytes 2359304 | tf_op jit(solution)/shard_map/s_a4/ppermute | solution.py:46
  69.4 14.7 %collective-permute-start.15 = (bf16[4,3,2,128,128]{4,3,2,1,0:T(8,128)(2,1)S(1)}, bf16[4,3,2,128,128]{4,3,2,1,0:T(8,128)(2,1)S(1)}, u32[]{:S(2)}, u32[]{:S(2)}) collective-permute-start(bf16[4,3,2,128,128]{4,3,2,1,0:T(8,128)(2,1)S(1)} %collective-permute-done.11.refs_6_), channel_id=1, source_target_pairs={{0,8},{8,0},{1,9},{9,1},{2,10},{10,2},{3,11},{11,3},{4,12},{12,4},... | collective-permute-start | bytes 2359304 | tf_op jit(solution)/shard_map/s_tb3/ppermute | solution.py:39
  77.8 6.3 %collective-permute-start.18 = (bf16[4,3,2,128,128]{4,3,2,1,0:T(8,128)(2,1)S(1)}, bf16[4,3,2,128,128]{4,3,2,1,0:T(8,128)(2,1)S(1)}, u32[]{:S(2)}, u32[]{:S(2)}) collective-permute-start(bf16[4,3,2,128,128]{4,3,2,1,0:T(8,128)(2,1)S(1)} %collective-permute-done.17.refs_8_), channel_id=1, source_target_pairs={{0,8},{8,0},{1,9},{9,1},{2,10},{10,2},{3,11},{11,3},{4,12},{12,4},... | collective-permute-start | bytes 2359304 | tf_op jit(solution)/shard_map/s_ta4/ppermute | solution.py:39
  90.2 10.9 %collective-permute-start.21 = (bf16[2,400,128]{2,1,0:T(8,128)(2,1)S(1)}, bf16[2,400,128]{2,1,0:T(8,128)(2,1)S(1)}, u32[]{:S(2)}, u32[]{:S(2)}) collective-permute-start(bf16[2,400,128]{2,1,0:T(8,128)(2,1)S(1)} %get-tuple-element.50), channel_id=1, source_target_pairs={{0,1},{1,128},{128,129},{129,0},{2,3},{3,130},{130,131},{131,2},{4... | collective-permute-start | bytes 614408 | tf_op jit(solution)/shard_map/s_f0/ppermute | solution.py:34
  90.3 10.8 %collective-permute-start.22 = (bf16[2,400,128]{2,1,0:T(8,128)(2,1)S(1)}, bf16[2,400,128]{2,1,0:T(8,128)(2,1)S(1)}, u32[]{:S(2)}, u32[]{:S(2)}) collective-permute-start(bf16[2,400,128]{2,1,0:T(8,128)(2,1)S(1)} %get-tuple-element.52), channel_id=1, source_target_pairs={{0,129},{1,0},{128,1},{129,128},{2,131},{3,2},{130,3},{131,130},{4... | collective-permute-start | bytes 614408 | tf_op jit(solution)/shard_map/s_f1/ppermute | solution.py:34
  95.8 10.3 %collective-permute-start.27 = (bf16[2,400,128]{2,1,0:T(8,128)(2,1)S(1)}, bf16[2,400,128]{2,1,0:T(8,128)(2,1)S(1)}, u32[]{:S(2)}, u32[]{:S(2)}) collective-permute-start(bf16[2,400,128]{2,1,0:T(8,128)(2,1)S(1)} %get-tuple-element.57), channel_id=1, source_target_pairs={{0,1},{1,128},{128,129},{129,0},{2,3},{3,130},{130,131},{131,2},{4... | collective-permute-start | bytes 614408 | tf_op jit(solution)/shard_map/s_prv1/ppermute | solution.py:34
  101.4 6.7 %collective-permute-start.28 = (bf16[2,400,128]{2,1,0:T(8,128)(2,1)S(1)}, bf16[2,400,128]{2,1,0:T(8,128)(2,1)S(1)}, u32[]{:S(2)}, u32[]{:S(2)}) collective-permute-start(bf16[2,400,128]{2,1,0:T(8,128)(2,1)S(1)} %get-tuple-element.58), channel_id=1, source_target_pairs={{0,129},{1,0},{128,1},{129,128},{2,131},{3,2},{130,3},{131,130},{4... | collective-permute-start | bytes 614408 | tf_op jit(solution)/shard_map/s_nxt1/ppermute | solution.py:34
  104.1 7.5 %collective-permute-start.24 = (bf16[2,400,128]{2,1,0:T(8,128)(2,1)S(1)}, bf16[2,400,128]{2,1,0:T(8,128)(2,1)S(1)}, u32[]{:S(2)}, u32[]{:S(2)}) collective-permute-start(bf16[2,400,128]{2,1,0:T(8,128)(2,1)S(1)} %get-tuple-element.55), channel_id=1, source_target_pairs={{0,129},{1,0},{128,1},{129,128},{2,131},{3,2},{130,3},{131,130},{4... | collective-permute-start | bytes 614408 | tf_op jit(solution)/shard_map/s_nxt0/ppermute | solution.py:34
  105.8 7.0 %collective-permute-start.23 = (bf16[2,400,128]{2,1,0:T(8,128)(2,1)S(1)}, bf16[2,400,128]{2,1,0:T(8,128)(2,1)S(1)}, u32[]{:S(2)}, u32[]{:S(2)}) collective-permute-start(bf16[2,400,128]{2,1,0:T(8,128)(2,1)S(1)} %get-tuple-element.54), channel_id=1, source_target_pairs={{0,1},{1,128},{128,129},{129,0},{2,3},{3,130},{130,131},{131,2},{4... | collective-permute-start | bytes 614408 | tf_op jit(solution)/shard_map/s_prv0/ppermute | solution.py:34
  108.3 10.0 %collective-permute-start.29 = (bf16[256,384]{1,0:T(8,128)(2,1)S(1)}, bf16[256,384]{1,0:T(8,128)(2,1)S(1)}, u32[]{:S(2)}, u32[]{:S(2)}) collective-permute-start(bf16[256,384]{1,0:T(8,128)(2,1)S(1)} %combine.3.refs_1_), channel_id=1, source_target_pairs={{0,6},{2,0},{4,2},{6,4},{1,7},{3,1},{5,3},{7,5},{8,14},{10,8},{12,... | collective-permute-start | bytes 589832 | tf_op jit(solution)/shard_map/s_right1/ppermute | solution.py:34
  113.0 7.9 %collective-permute-start.25 = (bf16[256,384]{1,0:T(8,128)(2,1)S(1)}, bf16[256,384]{1,0:T(8,128)(2,1)S(1)}, u32[]{:S(2)}, u32[]{:S(2)}) collective-permute-start(bf16[256,384]{1,0:T(8,128)(2,1)S(1)} %combine.2.refs_0_), channel_id=1, source_target_pairs={{0,2},{2,4},{4,6},{6,0},{1,3},{3,5},{5,7},{7,1},{8,10},{10,12},{12... | collective-permute-start | bytes 589832 | tf_op jit(solution)/shard_map/s_left0/ppermute | solution.py:34
  115.0 8.0 %collective-permute-start.31 = (bf16[256,384]{1,0:T(8,128)(2,1)S(1)}, bf16[256,384]{1,0:T(8,128)(2,1)S(1)}, u32[]{:S(2)}, u32[]{:S(2)}) collective-permute-start(bf16[256,384]{1,0:T(8,128)(2,1)S(1)} %combine.3.refs_1_), channel_id=1, source_target_pairs={{0,2},{2,4},{4,6},{6,0},{1,3},{3,5},{5,7},{7,1},{8,10},{10,12},{12... | collective-permute-start | bytes 589832 | tf_op jit(solution)/shard_map/s_left1/ppermute | solution.py:34
  116.5 6.5 %collective-permute-start.32 = (bf16[256,384]{1,0:T(8,128)(2,1)S(1)}, bf16[256,384]{1,0:T(8,128)(2,1)S(1)}, u32[]{:S(2)}, u32[]{:S(2)}) collective-permute-start(bf16[256,384]{1,0:T(8,128)(2,1)S(1)} %combine.2.refs_0_), channel_id=1, source_target_pairs={{0,6},{2,0},{4,2},{6,4},{1,7},{3,1},{5,3},{7,5},{8,14},{10,8},{12,... | collective-permute-start | bytes 589832 | tf_op jit(solution)/shard_map/s_right0/ppermute | solution.py:34
  118.3 6.1 %collective-permute-start.30 = (bf16[256,384]{1,0:T(8,128)(2,1)S(1)}, bf16[256,384]{1,0:T(8,128)(2,1)S(1)}, u32[]{:S(2)}, u32[]{:S(2)}) collective-permute-start(bf16[256,384]{1,0:T(8,128)(2,1)S(1)} %collective-permute-done.29.refs_5_), channel_id=1, source_target_pairs={{0,6},{2,0},{4,2},{6,4},{1,7},{3,1},{5,3},{7,5},{8,14},{10,8},{12,... | collective-permute-start | bytes 589832 | tf_op jit(solution)/shard_map/s_r2/ppermute | solution.py:34
  120.9 6.9 %collective-permute-start.26 = (bf16[256,384]{1,0:T(8,128)(2,1)S(1)}, bf16[256,384]{1,0:T(8,128)(2,1)S(1)}, u32[]{:S(2)}, u32[]{:S(2)}) collective-permute-start(bf16[256,384]{1,0:T(8,128)(2,1)S(1)} %collective-permute-done.25.refs_2_), channel_id=1, source_target_pairs={{0,2},{2,4},{4,6},{6,0},{1,3},{3,5},{5,7},{7,1},{8,10},{10,12},{12... | collective-permute-start | bytes 589832 | tf_op jit(solution)/shard_map/s_l2/ppermute | solution.py:34

commit v5 on v4

--- a/solution.py
+++ b/solution.py
@@ -436,10 +436,6 @@
     out_weight = after(out_weight, tw)
     pieces = jnp.stack([out_weight[:, r * out_cols : (r + 1) * out_cols] for r in range(N_X)])
     by_peer = lax.all_to_all(pieces, "x", split_axis=0, concat_axis=0, tiled=True)
-    weights = [
-        lax.dynamic_index_in_dim(by_peer, (x - r) % N_X, axis=0, keepdims=False)
-        for r in range(N_X)
-    ]
 
     ids = jnp.take(after(fetch_list, pieces)[0], tile_lists, axis=0)
     meta = jnp.concatenate([ids.reshape(-1), event_offsets, jnp.zeros((60,), jnp.int32)])[None]
@@ -459,7 +455,7 @@
     state = attend(heads, plans[1], q, [b1, after(tb1, by_peer), a2, twin(a2, "ta2")], state)
     b3, a4 = after(b3, state[1]), after(a4, state[1])
     state = attend(heads, plans[2], q, [b2, twin(b2, "tb2"), a3, twin(a3, "ta3")], state)
-    ends = [b3, twin(b3, "tb3"), after(a4, *weights), twin(a4, "ta4")]
+    ends = [b3, twin(b3, "tb3"), a4, twin(a4, "ta4")]
 
     far0, far1, prv0, prv1, nxt0, nxt1, near0, near1 = attend(
         heads, plans[3], q, ends, state, tuple((t, 2) for t in (8, 10, 12, 14, 4, 6, 0, 2))
@@ -467,6 +463,11 @@
     far0, far1 = hop(far0, COLUMN, N_COL, 1, "f0"), hop(far1, COLUMN, N_COL, -1, "f1")
     prv1, nxt0 = hop(prv1, COLUMN, N_COL, 1, "prv1"), hop(nxt0, COLUMN, N_COL, -1, "nxt0")
     prv0, nxt1 = merge(far0, prv0, far1, nxt1)
+    by_peer = after(by_peer, nxt1)
+    weights = [
+        lax.dynamic_index_in_dim(by_peer, (x - r) % N_X, axis=0, keepdims=False)
+        for r in range(N_X)
+    ]
     prv0, nxt1 = hop(prv0, COLUMN, N_COL, 1, "prv0"), hop(nxt1, COLUMN, N_COL, -1, "nxt1")
     rows0, rows1 = combine(near0, prv0, nxt0), combine(near1, prv1, nxt1)
 

time: 131 us -> 132 us (level)
  starting transfers between devices: 52.2 us -> 60.1 us
  waiting for transfers between devices: 32.3 us -> 24.5 us
  local copies, waits for them, and re-layouts: 6.04 us -> 8.96 us
  Pallas kernels: 30.7 us -> 28 us
    ppermute x18, starting transfers between devices: 31.8 us -> 37.1 us  [hop(): return lax.ppermute(x, axis, shift(n, by))]
    ppermute x7, waiting for transfers between devices: 18.3 us -> 13.4 us  [ring(): return lax.ppermute(x, ('z', 'core'), up + down)]
    unnamed x22, local copies, waits for them, and re-layouts: 2.6 us -> 5.67 us
    ppermute x18, waiting for transfers between devices: 13.2 us -> 10.4 us  [hop(): return lax.ppermute(x, axis, shift(n, by))]
    pallas_call x4, Pallas kernels: 22.3 us -> 19.6 us  [attend(): pl.pallas_call(functools.partial(attend_kernel, heads, len(kvs), spans, f...]
    ppermute x7, starting transfers between devices: 15.5 us -> 18 us  [ring(): return lax.ppermute(x, ('z', 'core'), up + down)]
  transfers between devices with their start and end apart: 34 -> 34, of which waited for: 12 -> 12; matrix products, arithmetic and copies ran while one was open for 9% -> 8% of each run, Pallas kernels for 14% -> 14%
where the time goes in v5:
time: 132 us; the launch traced here: 130 us
  starting transfers between devices  60.1 us (46%)
  Pallas kernels  28 us (21%)
  waiting for transfers between devices  24.5 us (19%)
  local copies, waits for them, and re-layouts  8.96 us (7%)
  other arithmetic  7.65 us (6%)
    ppermute x18, starting transfers between devices, hop(): return lax.ppermute(x, axis, shift(n, by))  37.1 us
    pallas_call x4, Pallas kernels, attend(): pl.pallas_call(functools.partial(attend_kernel, heads, len(kvs), spans, f...  19.6 us
    ppermute x7, starting transfers between devices, ring(): return lax.ppermute(x, ('z', 'core'), up + down)  18 us
    ppermute x7, waiting for transfers between devices, ring(): return lax.ppermute(x, ('z', 'core'), up + down)  13.4 us
    ppermute x18, waiting for transfers between devices, hop(): return lax.ppermute(x, axis, shift(n, by))  10.4 us
    unnamed x22, local copies, waits for them, and re-layouts  5.67 us
    all_to_all x1, starting transfers between devices, shards(): lax.all_to_all(pieces, 'x', split_axis=0, concat_axis=0, tiled=True)  4.63 us
    pallas_call x2, Pallas kernels, project(): pl.pallas_call(functools.partial(project_kernel, len(pairs), bool(more)),...  2.86 us
  transfers between devices with their start and end apart: 34, of which 12 were waited for; matrix products, arithmetic and copies ran while one was open for 8% of the time, Pallas kernels for 14%

profile of v5, /device:TPU:64, one launch (start us, length us, event | category | flops | bytes accessed | tf_op | source)
XLA Modules:
  0.0 129.6 jit_solution(3996379479398023123)
XLA Ops:
  0.0 2.3 %fetch.1 = bf16[4,3,128,2,128]{4,3,2,1,0:T(2,128)(2,1)} custom-call(s32[1]{0:T(128)} %bitcast.parity, bf16[1024,2,384]{2,1,0:T(2,128)(2,1)} %kv.1), custom_call_target="tpu_custom_call" | custom-call | tf_op jit(solution)/shard_map/fetch/pallas_call | solution.py:87
  2.3 2.6 %squares.1.refs_6_ = bf16[4,3,2,128,128]{4,3,2,1,0:T(8,128)(2,1)} custom-call(bf16[4,3,256,128]{3,2,1,0:T(8,128)(2,1)} %bitcast.60), custom_call_target="tpu_custom_call" | custom-call | tf_op jit(solution)/shard_map/squares/pallas_call | solution.py:95
  4.9 1.6 %collective-permute-start.5 = (bf16[512,384]{1,0:T(8,128)(2,1)}, bf16[512,384]{1,0:T(8,128)(2,1)}, u32[]{:S(2)}, u32[]{:S(2)}) collective-permute-start(bf16[512,384]{1,0:T(8,128)(2,1)} %param.8), channel_id=1, source_target_pairs={{0,1},{1,128},{128,129},{129,0},{2,3},{3,130},{130,131},{131,2},{4... | collective-permute-start | bytes 1179656 | tf_op jit(solution)/shard_map/s_q_back/ppermute | solution.py:34
  7.4 1.9 %collective-permute-start.4 = (bf16[4,3,2,128,128]{4,3,2,1,0:T(8,128)(2,1)}, bf16[4,3,2,128,128]{4,3,2,1,0:T(8,128)(2,1)}, u32[]{:S(2)}, u32[]{:S(2)}) collective-permute-start(bf16[4,3,2,128,128]{4,3,2,1,0:T(8,128)(2,1)} %squares.1.refs_6_), channel_id=1, source_target_pairs={{0,16},{16,32},{32,48},{48,64},{64,80},{80,96},{96,112},{112,0},{8... | collective-permute-start | bytes 2359304 | tf_op jit(solution)/shard_map/s_a1/ppermute | solution.py:46
  9.5 1.7 %pad_maximum_fusion = bf16[4,384,768]{2,1,0:T(8,128)(2,1)} fusion(bf16[1,384,768]{2,1,0:T(8,128)(2,1)S(1)} %get-tuple-element.74, bf16[1,384,768]{2,1,0:T(8,128)(2,1)S(1)} %get-tuple-element.75, bf16[1,384,768]{2,1,0:T(8,128)(2,1)S(1)} %get-tuple-element.76, bf16[1,384,768]{2,1,0:T(8,128)(2,1)S(1)} %get-tuple-element.73), kind=kLoop, calls=%fused_computation.1 | loop fusion | flops 3538944 | bytes 4718592 | tf_op jit(solution)/shard_map/stack | solution.py:437
  12.3 1.6 %collective-permute-start.1 = (s32[1,128]{1,0:T(1,128)S(1)}, s32[1,128]{1,0:T(1,128)S(1)}, u32[]{:S(2)}, u32[]{:S(2)}) collective-permute-start(s32[1,128]{1,0:T(1,128)S(1)} %add_bitcast_fusion), channel_id=1, source_target_pairs={{0,1},{1,128},{128,129},{129,0},{2,3},{3,130},{130,131},{131,2},{4... | collective-permute-start | bytes 1544 | tf_op jit(solution)/shard_map/s_meta/ppermute | solution.py:34
  13.9 2.9 %collective-permute-start.2 = (s32[1,128]{1,0:T(1,128)S(1)}, s32[1,128]{1,0:T(1,128)S(1)}, u32[]{:S(2)}, u32[]{:S(2)}) collective-permute-start(s32[1,128]{1,0:T(1,128)S(1)} %add_bitcast_fusion), channel_id=1, source_target_pairs={{0,128},{1,129},{128,0},{129,1},{2,130},{3,131},{130,2},{131,3},{4... | collective-permute-start | bytes 1544 | tf_op jit(solution)/shard_map/s_meta/ppermute | solution.py:34
  16.8 1.3 %collective-permute-start.3 = (s32[1,128]{1,0:T(1,128)S(1)}, s32[1,128]{1,0:T(1,128)S(1)}, u32[]{:S(2)}, u32[]{:S(2)}) collective-permute-start(s32[1,128]{1,0:T(1,128)S(1)} %add_bitcast_fusion), channel_id=1, source_target_pairs={{0,129},{1,0},{128,1},{129,128},{2,131},{3,2},{130,3},{131,130},{4... | collective-permute-start | bytes 1544 | tf_op jit(solution)/shard_map/s_meta/ppermute | solution.py:34
  18.1 4.6 %all-to-all-start = ((bf16[4,384,768]{2,1,0:T(8,128)(2,1)}), bf16[4,384,768]{2,1,0:T(8,128)(2,1)}, u32[]{:S(2)}, u32[]{:S(2)}) async-start(bf16[4,384,768]{2,1,0:T(8,128)(2,1)} %pad_maximum_fusion), calls=%async_computation | async-start | bytes 4718592 | tf_op jit(solution)/shard_map/all_to_all | solution.py:438
  22.9 3.2 %collective-permute-start.8 = (bf16[4,3,2,128,128]{4,3,2,1,0:T(8,128)(2,1)S(1)}, bf16[4,3,2,128,128]{4,3,2,1,0:T(8,128)(2,1)}, u32[]{:S(2)}, u32[]{:S(2)}) collective-permute-start(bf16[4,3,2,128,128]{4,3,2,1,0:T(8,128)(2,1)S(1)} %collective-permute-done.refs_7_), channel_id=1, source_target_pairs={{0,16},{16,32},{32,48},{48,64},{64,80},{80,96},{96,112},{112,0},{8... | collective-permute-start | bytes 2359304 | tf_op jit(solution)/shard_map/s_b1/ppermute | solution.py:46
  27.0 1.4 %convert_reduce_fusion = s32[4,16,20]{1,2,0:T(8,128)S(1)} fusion(pred[20,20]{1,0:T(8,128)(4,1)S(1)} %iota_compare_fusion.5, pred[4,16,20]{2,1,0:T(8,128)(4,1)S(1)} %get-tuple-element.68), kind=kLoop, calls=%fused_computation.5 | loop fusion | flops 75520 | bytes 6800 | tf_op jit(solution)/shard_map/reduce_sum | solution.py:402
  28.8 2.0 %collective-permute-start.6 = (bf16[512,384]{1,0:T(8,128)(2,1)}, bf16[512,384]{1,0:T(8,128)(2,1)}, u32[]{:S(2)}, u32[]{:S(2)}) collective-permute-start(bf16[512,384]{1,0:T(8,128)(2,1)} %collective-permute-done.5), channel_id=1, source_target_pairs={{0,1},{1,128},{128,129},{129,0},{2,3},{3,130},{130,131},{131,2},{4... | collective-permute-start | bytes 1179656 | tf_op jit(solution)/shard_map/s_q_far/ppermute | solution.py:34
  30.8 1.0 collective-permute-start.13
  32.0 1.4 %select_reduce_fusion = s32[4,16,20]{1,2,0:T(8,128)S(1)} fusion(s32[4,16,20]{2,1,0:T(8,128)S(1)} %get-tuple-element.81, s32[4,16,20]{2,1,0:T(8,128)S(1)} %copy.9, pred[4,16,20]{2,1,0:T(8,128)(4,1)S(1)} %get-tuple-element.68), kind=kLoop, calls=%fused_computation.3 | loop fusion | flops 101120 | bytes 16640 | tf_op jit(solution)/shard_map/reduce_sum | solution.py:404
  34.1 1.5 %collective-permute-done.8.refs_6_ = bf16[4,3,2,128,128]{4,3,2,1,0:T(8,128)(2,1)} collective-permute-done((bf16[4,3,2,128,128]{4,3,2,1,0:T(8,128)(2,1)S(1)}, bf16[4,3,2,128,128]{4,3,2,1,0:T(8,128)(2,1)}, u32[]{:S(2)}, u32[]{:S(2)}) %collective-permute-start.8) | collective-permute-done | bytes 786464 | tf_op jit(solution)/shard_map/s_b1/ppermute | solution.py:46
  35.6 2.7 %collective-permute-start.9 = (bf16[4,3,2,128,128]{4,3,2,1,0:T(8,128)(2,1)}, bf16[4,3,2,128,128]{4,3,2,1,0:T(8,128)(2,1)}, u32[]{:S(2)}, u32[]{:S(2)}) collective-permute-start(bf16[4,3,2,128,128]{4,3,2,1,0:T(8,128)(2,1)} %collective-permute-done.8.refs_6_), channel_id=1, source_target_pairs={{0,16},{16,32},{32,48},{48,64},{64,80},{80,96},{96,112},{112,0},{8... | collective-permute-start | bytes 2359304 | tf_op jit(solution)/shard_map/s_b2/ppermute | solution.py:46
  38.3 1.5 %pad_maximum_fusion.1 = bf16[2048,384]{1,0:T(8,128)(2,1)S(1)} fusion(bf16[512,384]{1,0:T(8,128)(2,1)} %copy-done.7, bf16[512,384]{1,0:T(8,128)(2,1)} %collective-permute-done.6, bf16[512,384]{1,0:T(8,128)(2,1)} %collective-permute-done.5, bf16[512,384]{1,0:T(8,128)(2,1)} %param.8), kind=kLoop, calls=%fused_computation.2 | loop fusion | flops 6291456 | bytes 3145728 | tf_op jit(solution)/shard_map/concatenate | solution.py:445
  39.8 4.3 %collective-permute-done.13.refs_8_ = bf16[4,3,2,128,128]{4,3,2,1,0:T(8,128)(2,1)} collective-permute-done((bf16[4,3,2,128,128]{4,3,2,1,0:T(8,128)(2,1)}, bf16[4,3,2,128,128]{4,3,2,1,0:T(8,128)(2,1)}, u32[]{:S(2)}, u32[]{:S(2)}) %collective-permute-start.13) | collective-permute-done | bytes 786464 | tf_op jit(solution)/shard_map/s_a2/ppermute | solution.py:46
  44.1 2.5 %collective-permute-start.16 = (bf16[4,3,2,128,128]{4,3,2,1,0:T(8,128)(2,1)}, bf16[4,3,2,128,128]{4,3,2,1,0:T(8,128)(2,1)}, u32[]{:S(2)}, u32[]{:S(2)}) collective-permute-start(bf16[4,3,2,128,128]{4,3,2,1,0:T(8,128)(2,1)} %collective-permute-done.13.refs_8_), channel_id=1, source_target_pairs={{0,16},{16,32},{32,48},{48,64},{64,80},{80,96},{96,112},{112,0},{8... | collective-permute-start | bytes 2359304 | tf_op jit(solution)/shard_map/s_a3/ppermute | solution.py:46
  46.6 4.5 %attend.4 = (f32[17,3,128,128]{3,2,1,0:T(8,128)S(1)}, f32[17,16,128]{2,1,0:T(8,128)S(1)}) custom-call(s32[16]{0:T(128)S(1)} %select_reduce_fusion.7.refs_0_, s32[256]{0:T(256)S(1)} %get-tuple-element.64.refs_1_, s32[256]{0:T(256)S(1)} %compare_select_fusion.3.refs_2_, s32[16]{0:T(128)S(1)} %get-tuple-element.86.refs_3_, ...), custom_call_target="tpu_custom_call" | custom-call | flops 15360000000 | bytes 3145728 | tf_op jit(solution)/shard_map/attend/pallas_call | solution.py:244
  51.1 1.7 %copy-done.4 = f32[17,3,128,128]{3,2,1,0:T(8,128)} copy-done((f32[17,3,128,128]{3,2,1,0:T(8,128)}, f32[17,3,128,128]{3,2,1,0:T(8,128)S(1)}, u32[]{:S(2)}) %copy-start.4) | copy-done | bytes 3342360
  52.8 4.2 %collective-permute-start.11 = (bf16[4,3,2,128,128]{4,3,2,1,0:T(8,128)(2,1)}, bf16[4,3,2,128,128]{4,3,2,1,0:T(8,128)(2,1)S(1)}, u32[]{:S(2)}, u32[]{:S(2)}) collective-permute-start(bf16[4,3,2,128,128]{4,3,2,1,0:T(8,128)(2,1)} %collective-permute-done.9.refs_6_), channel_id=1, source_target_pairs={{0,16},{16,32},{32,48},{48,64},{64,80},{80,96},{96,112},{112,0},{8... | collective-permute-start | bytes 2359304 | tf_op jit(solution)/shard_map/s_b3/ppermute | solution.py:46
  57.9 3.1 %collective-permute-done.16.refs_8_ = bf16[4,3,2,128,128]{4,3,2,1,0:T(8,128)(2,1)} collective-permute-done((bf16[4,3,2,128,128]{4,3,2,1,0:T(8,128)(2,1)}, bf16[4,3,2,128,128]{4,3,2,1,0:T(8,128)(2,1)}, u32[]{:S(2)}, u32[]{:S(2)}) %collective-permute-start.16) | collective-permute-done | bytes 786464 | tf_op jit(solution)/shard_map/s_a3/ppermute | solution.py:46
  61.0 2.5 %collective-permute-start.17 = (bf16[4,3,2,128,128]{4,3,2,1,0:T(8,128)(2,1)}, bf16[4,3,2,128,128]{4,3,2,1,0:T(8,128)(2,1)S(1)}, u32[]{:S(2)}, u32[]{:S(2)}) collective-permute-start(bf16[4,3,2,128,128]{4,3,2,1,0:T(8,128)(2,1)} %collective-permute-done.16.refs_8_), channel_id=1, source_target_pairs={{0,16},{16,32},{32,48},{48,64},{64,80},{80,96},{96,112},{112,0},{8... | collective-permute-start | bytes 2359304 | tf_op jit(solution)/shard_map/s_a4/ppermute | solution.py:46
  63.5 1.1 copy-done.3
  64.6 1.9 %copy-done.5 = f32[17,3,128,128]{3,2,1,0:T(8,128)S(1)} copy-done((f32[17,3,128,128]{3,2,1,0:T(8,128)S(1)}, f32[17,3,128,128]{3,2,1,0:T(8,128)}, u32[]{:S(2)}) %copy-start.5) | copy-done | bytes 3342360
  66.5 6.6 %attend.5 = (f32[17,3,128,128]{3,2,1,0:T(8,128)S(1)}, f32[17,16,128]{2,1,0:T(8,128)S(1)}) custom-call(s32[16]{0:T(128)S(1)} %select_reduce_fusion.6.refs_0_, s32[256]{0:T(256)S(1)} %get-tuple-element.62.refs_1_, s32[256]{0:T(256)S(1)} %compare_select_fusion.2.refs_2_, s32[16]{0:T(128)S(1)} %get-tuple-element.87.refs_3_, ...), custom_call_target="tpu_custom_call" | custom-call | flops 15360000000 | bytes 3145728 | tf_op jit(solution)/shard_map/attend/pallas_call | solution.py:244
  73.3 4.5 %collective-permute-done.17.refs_8_ = bf16[4,3,2,128,128]{4,3,2,1,0:T(8,128)(2,1)S(1)} collective-permute-done((bf16[4,3,2,128,128]{4,3,2,1,0:T(8,128)(2,1)}, bf16[4,3,2,128,128]{4,3,2,1,0:T(8,128)(2,1)S(1)}, u32[]{:S(2)}, u32[]{:S(2)}) %collective-permute-start.17) | collective-permute-done | bytes 786464 | tf_op jit(solution)/shard_map/s_a4/ppermute | solution.py:46
  77.8 4.4 %attend.6 = (f32[17,3,128,128]{3,2,1,0:T(8,128)S(1)}, f32[17,16,128]{2,1,0:T(8,128)S(1)}) custom-call(s32[16]{0:T(128)S(1)} %select_reduce_fusion.5.refs_0_, s32[256]{0:T(256)S(1)} %get-tuple-element.60.refs_1_, s32[256]{0:T(256)S(1)} %compare_select_fusion.1.refs_2_, s32[16]{0:T(128)S(1)} %get-tuple-element.84.refs_3_, ...), custom_call_target="tpu_custom_call" | custom-call | flops 15360000000 | bytes 3145728 | tf_op jit(solution)/shard_map/attend/pallas_call | solution.py:244
  82.3 4.1 %attend.7 = (bf16[2,400,128]{2,1,0:T(8,128)(2,1)S(1)}, bf16[2,400,128]{2,1,0:T(8,128)(2,1)S(1)}, bf16[2,400,128]{2,1,0:T(8,128)(2,1)S(1)}, bf16[2,400,128]{2,1,0...) custom-call(s32[16]{0:T(128)S(1)} %select_reduce_fusion.8.refs_0_, ...), custom_call_target="tpu_custom_call" | custom-call | flops 15360000000 | bytes 3145728 | tf_op jit(solution)/shard_map/attend/pallas_call | solution.py:244
  86.3 5.1 %collective-permute-start.21 = (bf16[2,400,128]{2,1,0:T(8,128)(2,1)S(1)}, bf16[2,400,128]{2,1,0:T(8,128)(2,1)S(1)}, u32[]{:S(2)}, u32[]{:S(2)}) collective-permute-start(bf16[2,400,128]{2,1,0:T(8,128)(2,1)S(1)} %get-tuple-element.49), channel_id=1, source_target_pairs={{0,1},{1,128},{128,129},{129,0},{2,3},{3,130},{130,131},{131,2},{4... | collective-permute-start | bytes 614408 | tf_op jit(solution)/shard_map/s_f0/ppermute | solution.py:34
  91.4 2.1 %collective-permute-start.22 = (bf16[2,400,128]{2,1,0:T(8,128)(2,1)S(1)}, bf16[2,400,128]{2,1,0:T(8,128)(2,1)S(1)}, u32[]{:S(2)}, u32[]{:S(2)}) collective-permute-start(bf16[2,400,128]{2,1,0:T(8,128)(2,1)S(1)} %get-tuple-element.51), channel_id=1, source_target_pairs={{0,129},{1,0},{128,1},{129,128},{2,131},{3,2},{130,3},{131,130},{4... | collective-permute-start | bytes 614408 | tf_op jit(solution)/shard_map/s_f1/ppermute | solution.py:34
  93.5 3.3 %collective-permute-start.27 = (bf16[2,400,128]{2,1,0:T(8,128)(2,1)S(1)}, bf16[2,400,128]{2,1,0:T(8,128)(2,1)S(1)}, u32[]{:S(2)}, u32[]{:S(2)}) collective-permute-start(bf16[2,400,128]{2,1,0:T(8,128)(2,1)S(1)} %get-tuple-element.56), channel_id=1, source_target_pairs={{0,1},{1,128},{128,129},{129,0},{2,3},{3,130},{130,131},{131,2},{4... | collective-permute-start | bytes 614408 | tf_op jit(solution)/shard_map/s_prv1/ppermute | solution.py:34
  96.8 1.8 %collective-permute-done.21.a0 = bf16[2,400,128]{2,1,0:T(8,128)(2,1)S(1)} collective-permute-done((bf16[2,400,128]{2,1,0:T(8,128)(2,1)S(1)}, bf16[2,400,128]{2,1,0:T(8,128)(2,1)S(1)}, u32[]{:S(2)}, u32[]{:S(2)}) %collective-permute-start.21) | collective-permute-done | bytes 204832 | tf_op jit(solution)/shard_map/s_f0/ppermute | solution.py:34
  98.5 2.1 %collective-permute-done.22.b0 = bf16[2,400,128]{2,1,0:T(8,128)(2,1)S(1)} collective-permute-done((bf16[2,400,128]{2,1,0:T(8,128)(2,1)S(1)}, bf16[2,400,128]{2,1,0:T(8,128)(2,1)S(1)}, u32[]{:S(2)}, u32[]{:S(2)}) %collective-permute-start.22) | collective-permute-done | bytes 204832 | tf_op jit(solution)/shard_map/s_f1/ppermute | solution.py:34
  100.9 3.0 %collective-permute-start.28 = (bf16[2,400,128]{2,1,0:T(8,128)(2,1)S(1)}, bf16[2,400,128]{2,1,0:T(8,128)(2,1)S(1)}, u32[]{:S(2)}, u32[]{:S(2)}) collective-permute-start(bf16[2,400,128]{2,1,0:T(8,128)(2,1)S(1)} %get-tuple-element.57), channel_id=1, source_target_pairs={{0,129},{1,0},{128,1},{129,128},{2,131},{3,2},{130,3},{131,130},{4... | collective-permute-start | bytes 614408 | tf_op jit(solution)/shard_map/s_nxt1/ppermute | solution.py:34
  103.9 2.0 %collective-permute-start.24 = (bf16[2,400,128]{2,1,0:T(8,128)(2,1)S(1)}, bf16[2,400,128]{2,1,0:T(8,128)(2,1)S(1)}, u32[]{:S(2)}, u32[]{:S(2)}) collective-permute-start(bf16[2,400,128]{2,1,0:T(8,128)(2,1)S(1)} %get-tuple-element.54), channel_id=1, source_target_pairs={{0,129},{1,0},{128,1},{129,128},{2,131},{3,2},{130,3},{131,130},{4... | collective-permute-start | bytes 614408 | tf_op jit(solution)/shard_map/s_nxt0/ppermute | solution.py:34
  105.9 3.5 %collective-permute-done.28.p1 = bf16[2,400,128]{2,1,0:T(8,128)(2,1)S(1)} collective-permute-done((bf16[2,400,128]{2,1,0:T(8,128)(2,1)S(1)}, bf16[2,400,128]{2,1,0:T(8,128)(2,1)S(1)}, u32[]{:S(2)}, u32[]{:S(2)}) %collective-permute-start.28) | collective-permute-done | bytes 204832 | tf_op jit(solution)/shard_map/s_nxt1/ppermute | solution.py:34
  109.7 3.2 %collective-permute-start.29 = (bf16[256,384]{1,0:T(8,128)(2,1)S(1)}, bf16[256,384]{1,0:T(8,128)(2,1)S(1)}, u32[]{:S(2)}, u32[]{:S(2)}) collective-permute-start(bf16[256,384]{1,0:T(8,128)(2,1)S(1)} %combine.3.refs_1_), channel_id=1, source_target_pairs={{0,6},{2,0},{4,2},{6,4},{1,7},{3,1},{5,3},{7,5},{8,14},{10,8},{12,... | collective-permute-start | bytes 589832 | tf_op jit(solution)/shard_map/s_right1/ppermute | solution.py:34
  113.1 2.0 %collective-permute-start.25 = (bf16[256,384]{1,0:T(8,128)(2,1)S(1)}, bf16[256,384]{1,0:T(8,128)(2,1)S(1)}, u32[]{:S(2)}, u32[]{:S(2)}) collective-permute-start(bf16[256,384]{1,0:T(8,128)(2,1)S(1)} %combine.2.refs_0_), channel_id=1, source_target_pairs={{0,2},{2,4},{4,6},{6,0},{1,3},{3,5},{5,7},{7,1},{8,10},{10,12},{12... | collective-permute-start | bytes 589832 | tf_op jit(solution)/shard_map/s_left0/ppermute | solution.py:34
  115.1 1.5 %collective-permute-start.31 = (bf16[256,384]{1,0:T(8,128)(2,1)S(1)}, bf16[256,384]{1,0:T(8,128)(2,1)S(1)}, u32[]{:S(2)}, u32[]{:S(2)}) collective-permute-start(bf16[256,384]{1,0:T(8,128)(2,1)S(1)} %combine.3.refs_1_), channel_id=1, source_target_pairs={{0,2},{2,4},{4,6},{6,0},{1,3},{3,5},{5,7},{7,1},{8,10},{10,12},{12... | collective-permute-start | bytes 589832 | tf_op jit(solution)/shard_map/s_left1/ppermute | solution.py:34
  116.6 1.8 %collective-permute-start.32 = (bf16[256,384]{1,0:T(8,128)(2,1)S(1)}, bf16[256,384]{1,0:T(8,128)(2,1)S(1)}, u32[]{:S(2)}, u32[]{:S(2)}) collective-permute-start(bf16[256,384]{1,0:T(8,128)(2,1)S(1)} %combine.2.refs_0_), channel_id=1, source_target_pairs={{0,6},{2,0},{4,2},{6,4},{1,7},{3,1},{5,3},{7,5},{8,14},{10,8},{12,... | collective-permute-start | bytes 589832 | tf_op jit(solution)/shard_map/s_right0/ppermute | solution.py:34
  118.3 2.3 %collective-permute-start.30 = (bf16[256,384]{1,0:T(8,128)(2,1)S(1)}, bf16[256,384]{1,0:T(8,128)(2,1)S(1)}, u32[]{:S(2)}, u32[]{:S(2)}) collective-permute-start(bf16[256,384]{1,0:T(8,128)(2,1)S(1)} %collective-permute-done.29.refs_5_), channel_id=1, source_target_pairs={{0,6},{2,0},{4,2},{6,4},{1,7},{3,1},{5,3},{7,5},{8,14},{10,8},{12,... | collective-permute-start | bytes 589832 | tf_op jit(solution)/shard_map/s_r2/ppermute | solution.py:34
  121.2 1.5 %collective-permute-start.26 = (bf16[256,384]{1,0:T(8,128)(2,1)S(1)}, bf16[256,384]{1,0:T(8,128)(2,1)S(1)}, u32[]{:S(2)}, u32[]{:S(2)}) collective-permute-start(bf16[256,384]{1,0:T(8,128)(2,1)S(1)} %collective-permute-done.25.refs_2_), channel_id=1, source_target_pairs={{0,2},{2,4},{4,6},{6,0},{1,3},{3,5},{5,7},{7,1},{8,10},{10,12},{12... | collective-permute-start | bytes 589832 | tf_op jit(solution)/shard_map/s_l2/ppermute | solution.py:34
  122.7 1.8 %dynamic-slice_bitcast_fusion = (bf16[384,768]{1,0:T(8,128)(2,1)S(1)}, bf16[384,768]{1,0:T(8,128)(2,1)S(1)}, bf16[384,768]{1,0:T(8,128)(2,1)S(1)}, bf16[384,768]{1,0:T(8,128)(2,1)S(1)}) fusion(bf16[4,384,768]{2,1,0:T(8,128)(2,1)} %all-to-all-done, s32[]{:T(128)S(6)} %select_n.233, s32[]{:T(128)S(6)} %select_n.231, s32[]{:T(128)S(6)} %select_n.229, ...), kind=kLoop, calls=%fused_computation.7 | loop fusion | bytes 4718608 | tf_op jit(solution)/shard_map/jit(dynamic_index_in_dim)/squeeze | solution.py:468
  124.9 1.4 %project.2.refs_3_ = f32[512,768]{1,0:T(8,128)S(1)} custom-call(bf16[256,384]{1,0:T(8,128)(2,1)S(1)} %combine.2.refs_0_, bf16[256,384]{1,0:T(8,128)(2,1)S(1)} %combine.3.refs_1_, bf16[256,384]{1,0:T(8,128)(2,1)S(1)} %collective-permute-done.25.refs_2_, bf16[256,384]{1,0:T(8,128)(2,1)S(1)} %collective-permute-done.31.refs_3_, ...), custom_call_target="tpu_custom_call" | custom-call | flops 1000000000 | bytes 4194304 | tf_op jit(solution)/shard_map/project/pallas_call | solution.py:364
  126.3 1.8 %collective-permute-done.26.refs_0_ = bf16[256,384]{1,0:T(8,128)(2,1)S(1)} collective-permute-done((bf16[256,384]{1,0:T(8,128)(2,1)S(1)}, bf16[256,384]{1,0:T(8,128)(2,1)S(1)}, u32[]{:S(2)}, u32[]{:S(2)}) %collective-permute-start.26) | collective-permute-done | bytes 196640 | tf_op jit(solution)/shard_map/s_l2/ppermute | solution.py:34
  128.1 1.5 %project.3 = bf16[512,768]{1,0:T(8,128)(2,1)} custom-call(bf16[256,384]{1,0:T(8,128)(2,1)S(1)} %collective-permute-done.26.refs_0_, bf16[256,384]{1,0:T(8,128)(2,1)S(1)} %collective-permute-done.30.refs_1_, bf16[384,768]{1,0:T(8,128)(2,1)S(1)} %get-tuple-element.72.refs_2_, f32[512,768]{1,0:T(8,128)S(1)} %project.2.refs_3_), custom_call_target="tpu_custom_call" | custom-call | flops 1000000000 | bytes 4194304 | tf_op jit(solution)/shard_map/project/pallas_call | solution.py:364
  (99 shorter events, 7.2 us)
Async XLA Ops:
  0.0 11.2 %copy-start = (s32[1,32]{1,0:T(1,128)S(1)}, s32[1,32]{1,0:T(1,128)}, u32[]{:S(2)}) copy-start(s32[1,32]{1,0:T(1,128)} %param.11) | copy-start | bytes 388
  0.0 6.5 %copy-start.8 = (s32[4,16]{1,0:T(4,128)S(1)}, s32[4,16]{1,0:T(4,128)}, u32[]{:S(2)}) copy-start(s32[4,16]{1,0:T(4,128)} %param.12) | copy-start | bytes 772
  0.0 9.3 %copy-start.6 = (bf16[384,3072]{1,0:T(8,128)(2,1)S(1)}, bf16[384,3072]{1,0:T(8,128)(2,1)}, u32[]{:S(2)}) copy-start(bf16[384,3072]{1,0:T(8,128)(2,1)} %param.10) | copy-start | bytes 7077892
  4.9 2.5 %collective-permute-start = (bf16[4,3,2,128,128]{4,3,2,1,0:T(8,128)(2,1)}, bf16[4,3,2,128,128]{4,3,2,1,0:T(8,128)(2,1)S(1)}, u32[]{:S(2)}, u32[]{:S(2)}) collective-permute-start(bf16[4,3,2,128,128]{4,3,2,1,0:T(8,128)(2,1)} %squares.1.refs_6_), channel_id=1, source_target_pairs={{0,8},{8,0},{1,9},{9,1},{2,10},{10,2},{3,11},{11,3},{4,12},{12,4},... | collective-permute-start | bytes 2359304 | tf_op jit(solution)/shard_map/s_tw/ppermute | solution.py:39
  4.9 23.9 %collective-permute-start.5 = (bf16[512,384]{1,0:T(8,128)(2,1)}, bf16[512,384]{1,0:T(8,128)(2,1)}, u32[]{:S(2)}, u32[]{:S(2)}) collective-permute-start(bf16[512,384]{1,0:T(8,128)(2,1)} %param.8), channel_id=1, source_target_pairs={{0,1},{1,128},{128,129},{129,0},{2,3},{3,130},{130,131},{131,2},{4... | collective-permute-start | bytes 1179656 | tf_op jit(solution)/shard_map/s_q_back/ppermute | solution.py:34
  7.4 18.7 %collective-permute-start.4 = (bf16[4,3,2,128,128]{4,3,2,1,0:T(8,128)(2,1)}, bf16[4,3,2,128,128]{4,3,2,1,0:T(8,128)(2,1)}, u32[]{:S(2)}, u32[]{:S(2)}) collective-permute-start(bf16[4,3,2,128,128]{4,3,2,1,0:T(8,128)(2,1)} %squares.1.refs_6_), channel_id=1, source_target_pairs={{0,16},{16,32},{32,48},{48,64},{64,80},{80,96},{96,112},{112,0},{8... | collective-permute-start | bytes 2359304 | tf_op jit(solution)/shard_map/s_a1/ppermute | solution.py:46
  9.5 2.7 %copy-start.10 = (s32[4]{0:T(128)S(1)}, s32[4]{0:T(128)}, u32[]{:S(2)}) copy-start(s32[4]{0:T(128)} %param.13) | copy-start | bytes 52
  12.3 10.5 %collective-permute-start.1 = (s32[1,128]{1,0:T(1,128)S(1)}, s32[1,128]{1,0:T(1,128)S(1)}, u32[]{:S(2)}, u32[]{:S(2)}) collective-permute-start(s32[1,128]{1,0:T(1,128)S(1)} %add_bitcast_fusion), channel_id=1, source_target_pairs={{0,1},{1,128},{128,129},{129,0},{2,3},{3,130},{130,131},{131,2},{4... | collective-permute-start | bytes 1544 | tf_op jit(solution)/shard_map/s_meta/ppermute | solution.py:34
  13.9 9.0 %collective-permute-start.2 = (s32[1,128]{1,0:T(1,128)S(1)}, s32[1,128]{1,0:T(1,128)S(1)}, u32[]{:S(2)}, u32[]{:S(2)}) collective-permute-start(s32[1,128]{1,0:T(1,128)S(1)} %add_bitcast_fusion), channel_id=1, source_target_pairs={{0,128},{1,129},{128,0},{129,1},{2,130},{3,131},{130,2},{131,3},{4... | collective-permute-start | bytes 1544 | tf_op jit(solution)/shard_map/s_meta/ppermute | solution.py:34
  16.8 9.3 %collective-permute-start.3 = (s32[1,128]{1,0:T(1,128)S(1)}, s32[1,128]{1,0:T(1,128)S(1)}, u32[]{:S(2)}, u32[]{:S(2)}) collective-permute-start(s32[1,128]{1,0:T(1,128)S(1)} %add_bitcast_fusion), channel_id=1, source_target_pairs={{0,129},{1,0},{128,1},{129,128},{2,131},{3,2},{130,3},{131,130},{4... | collective-permute-start | bytes 1544 | tf_op jit(solution)/shard_map/s_meta/ppermute | solution.py:34
  18.1 8.5 %copy-start.9 = (s32[4]{0:T(128)S(1)}, s32[4]{0:T(128)}, u32[]{:S(2)}) copy-start(s32[4]{0:T(128)} %constant.226.clone) | copy-start | bytes 52
  18.1 39.8 %all-to-all-start = ((bf16[4,384,768]{2,1,0:T(8,128)(2,1)}), bf16[4,384,768]{2,1,0:T(8,128)(2,1)}, u32[]{:S(2)}, u32[]{:S(2)}) async-start(bf16[4,384,768]{2,1,0:T(8,128)(2,1)} %pad_maximum_fusion), calls=%async_computation | async-start | bytes 4718592 | tf_op jit(solution)/shard_map/all_to_all | solution.py:438
  22.7 23.9 %copy-start.1 = (bf16[4,3,2,128,128]{4,3,2,1,0:T(8,128)(2,1)S(1)}, bf16[4,3,2,128,128]{4,3,2,1,0:T(8,128)(2,1)}, u32[]{:S(2)}) copy-start(bf16[4,3,2,128,128]{4,3,2,1,0:T(8,128)(2,1)} %squares.1.refs_6_) | copy-start | bytes 2359300
  22.8 12.8 %collective-permute-start.7 = (bf16[512,384]{1,0:T(8,128)(2,1)}, bf16[512,384]{1,0:T(8,128)(2,1)S(1)}, u32[]{:S(2)}, u32[]{:S(2)}) collective-permute-start(bf16[512,384]{1,0:T(8,128)(2,1)} %param.8), channel_id=1, source_target_pairs={{0,129},{1,0},{128,1},{129,128},{2,131},{3,2},{130,3},{131,130},{4... | collective-permute-start | bytes 1179656 | tf_op jit(solution)/shard_map/s_q_next/ppermute | solution.py:34
  22.9 12.7 %collective-permute-start.8 = (bf16[4,3,2,128,128]{4,3,2,1,0:T(8,128)(2,1)S(1)}, bf16[4,3,2,128,128]{4,3,2,1,0:T(8,128)(2,1)}, u32[]{:S(2)}, u32[]{:S(2)}) collective-permute-start(bf16[4,3,2,128,128]{4,3,2,1,0:T(8,128)(2,1)S(1)} %collective-permute-done.refs_7_), channel_id=1, source_target_pairs={{0,16},{16,32},{32,48},{48,64},{64,80},{80,96},{96,112},{112,0},{8... | collective-permute-start | bytes 2359304 | tf_op jit(solution)/shard_map/s_b1/ppermute | solution.py:46
  28.8 9.5 %collective-permute-start.6 = (bf16[512,384]{1,0:T(8,128)(2,1)}, bf16[512,384]{1,0:T(8,128)(2,1)}, u32[]{:S(2)}, u32[]{:S(2)}) collective-permute-start(bf16[512,384]{1,0:T(8,128)(2,1)} %collective-permute-done.5), channel_id=1, source_target_pairs={{0,1},{1,128},{128,129},{129,0},{2,3},{3,130},{130,131},{131,2},{4... | collective-permute-start | bytes 1179656 | tf_op jit(solution)/shard_map/s_q_far/ppermute | solution.py:34
  30.8 13.3 %collective-permute-start.13 = (bf16[4,3,2,128,128]{4,3,2,1,0:T(8,128)(2,1)}, bf16[4,3,2,128,128]{4,3,2,1,0:T(8,128)(2,1)}, u32[]{:S(2)}, u32[]{:S(2)}) collective-permute-start(bf16[4,3,2,128,128]{4,3,2,1,0:T(8,128)(2,1)} %collective-permute-done.4.refs_8_), channel_id=1, source_target_pairs={{0,16},{16,32},{32,48},{48,64},{64,80},{80,96},{96,112},{112,0},{8... | collective-permute-start | bytes 2359304 | tf_op jit(solution)/shard_map/s_a2/ppermute | solution.py:46
  33.4 13.2 %collective-permute-start.10 = (bf16[4,3,2,128,128]{4,3,2,1,0:T(8,128)(2,1)}, bf16[4,3,2,128,128]{4,3,2,1,0:T(8,128)(2,1)}, u32[]{:S(2)}, u32[]{:S(2)}) collective-permute-start(bf16[4,3,2,128,128]{4,3,2,1,0:T(8,128)(2,1)} %collective-permute-done.4.refs_8_), channel_id=1, source_target_pairs={{0,8},{8,0},{1,9},{9,1},{2,10},{10,2},{3,11},{11,3},{4,12},{12,4},... | collective-permute-start | bytes 2359304 | tf_op jit(solution)/shard_map/s_ta1/ppermute | solution.py:39
  35.6 21.4 %collective-permute-start.12 = (bf16[4,3,2,128,128]{4,3,2,1,0:T(8,128)(2,1)}, bf16[4,3,2,128,128]{4,3,2,1,0:T(8,128)(2,1)S(1)}, u32[]{:S(2)}, u32[]{:S(2)}) collective-permute-start(bf16[4,3,2,128,128]{4,3,2,1,0:T(8,128)(2,1)} %collective-permute-done.8.refs_6_), channel_id=1, source_target_pairs={{0,8},{8,0},{1,9},{9,1},{2,10},{10,2},{3,11},{11,3},{4,12},{12,4},... | collective-permute-start | bytes 2359304 | tf_op jit(solution)/shard_map/s_tb1/ppermute | solution.py:39
  35.6 2.7 %copy-start.7 = (bf16[512,384]{1,0:T(8,128)(2,1)}, bf16[512,384]{1,0:T(8,128)(2,1)S(1)}, u32[]{:S(2)}) copy-start(bf16[512,384]{1,0:T(8,128)(2,1)S(1)} %collective-permute-done.7) | copy-start | bytes 1179652
  35.6 17.1 %collective-permute-start.9 = (bf16[4,3,2,128,128]{4,3,2,1,0:T(8,128)(2,1)}, bf16[4,3,2,128,128]{4,3,2,1,0:T(8,128)(2,1)}, u32[]{:S(2)}, u32[]{:S(2)}) collective-permute-start(bf16[4,3,2,128,128]{4,3,2,1,0:T(8,128)(2,1)} %collective-permute-done.8.refs_6_), channel_id=1, source_target_pairs={{0,16},{16,32},{32,48},{48,64},{64,80},{80,96},{96,112},{112,0},{8... | collective-permute-start | bytes 2359304 | tf_op jit(solution)/shard_map/s_b2/ppermute | solution.py:46
  44.1 19.3 %collective-permute-start.14 = (bf16[4,3,2,128,128]{4,3,2,1,0:T(8,128)(2,1)}, bf16[4,3,2,128,128]{4,3,2,1,0:T(8,128)(2,1)}, u32[]{:S(2)}, u32[]{:S(2)}) collective-permute-start(bf16[4,3,2,128,128]{4,3,2,1,0:T(8,128)(2,1)} %collective-permute-done.13.refs_8_), channel_id=1, source_target_pairs={{0,8},{8,0},{1,9},{9,1},{2,10},{10,2},{3,11},{11,3},{4,12},{12,4},... | collective-permute-start | bytes 2359304 | tf_op jit(solution)/shard_map/s_ta2/ppermute | solution.py:39
  44.1 16.8 %collective-permute-start.16 = (bf16[4,3,2,128,128]{4,3,2,1,0:T(8,128)(2,1)}, bf16[4,3,2,128,128]{4,3,2,1,0:T(8,128)(2,1)}, u32[]{:S(2)}, u32[]{:S(2)}) collective-permute-start(bf16[4,3,2,128,128]{4,3,2,1,0:T(8,128)(2,1)} %collective-permute-done.13.refs_8_), channel_id=1, source_target_pairs={{0,16},{16,32},{32,48},{48,64},{64,80},{80,96},{96,112},{112,0},{8... | collective-permute-start | bytes 2359304 | tf_op jit(solution)/shard_map/s_a3/ppermute | solution.py:46
  51.1 1.7 %copy-start.4 = (f32[17,3,128,128]{3,2,1,0:T(8,128)}, f32[17,3,128,128]{3,2,1,0:T(8,128)S(1)}, u32[]{:S(2)}) copy-start(f32[17,3,128,128]{3,2,1,0:T(8,128)S(1)} %get-tuple-element.41.refs_10_) | copy-start | bytes 10027012
  52.8 20.4 %collective-permute-start.11 = (bf16[4,3,2,128,128]{4,3,2,1,0:T(8,128)(2,1)}, bf16[4,3,2,128,128]{4,3,2,1,0:T(8,128)(2,1)S(1)}, u32[]{:S(2)}, u32[]{:S(2)}) collective-permute-start(bf16[4,3,2,128,128]{4,3,2,1,0:T(8,128)(2,1)} %collective-permute-done.9.refs_6_), channel_id=1, source_target_pairs={{0,16},{16,32},{32,48},{48,64},{64,80},{80,96},{96,112},{112,0},{8... | collective-permute-start | bytes 2359304 | tf_op jit(solution)/shard_map/s_b3/ppermute | solution.py:46
  57.0 20.8 %collective-permute-start.19 = (bf16[4,3,2,128,128]{4,3,2,1,0:T(8,128)(2,1)}, bf16[4,3,2,128,128]{4,3,2,1,0:T(8,128)(2,1)S(1)}, u32[]{:S(2)}, u32[]{:S(2)}) collective-permute-start(bf16[4,3,2,128,128]{4,3,2,1,0:T(8,128)(2,1)} %collective-permute-done.9.refs_6_), channel_id=1, source_target_pairs={{0,8},{8,0},{1,9},{9,1},{2,10},{10,2},{3,11},{11,3},{4,12},{12,4},... | collective-permute-start | bytes 2359304 | tf_op jit(solution)/shard_map/s_tb2/ppermute | solution.py:39
  57.0 0.9 copy-start.2
  61.0 16.9 %collective-permute-start.20 = (bf16[4,3,2,128,128]{4,3,2,1,0:T(8,128)(2,1)}, bf16[4,3,2,128,128]{4,3,2,1,0:T(8,128)(2,1)S(1)}, u32[]{:S(2)}, u32[]{:S(2)}) collective-permute-start(bf16[4,3,2,128,128]{4,3,2,1,0:T(8,128)(2,1)} %collective-permute-done.16.refs_8_), channel_id=1, source_target_pairs={{0,8},{8,0},{1,9},{9,1},{2,10},{10,2},{3,11},{11,3},{4,12},{12,4},... | collective-permute-start | bytes 2359304 | tf_op jit(solution)/shard_map/s_ta3/ppermute | solution.py:39
  61.0 16.8 %collective-permute-start.17 = (bf16[4,3,2,128,128]{4,3,2,1,0:T(8,128)(2,1)}, bf16[4,3,2,128,128]{4,3,2,1,0:T(8,128)(2,1)S(1)}, u32[]{:S(2)}, u32[]{:S(2)}) collective-permute-start(bf16[4,3,2,128,128]{4,3,2,1,0:T(8,128)(2,1)} %collective-permute-done.16.refs_8_), channel_id=1, source_target_pairs={{0,16},{16,32},{32,48},{48,64},{64,80},{80,96},{96,112},{112,0},{8... | collective-permute-start | bytes 2359304 | tf_op jit(solution)/shard_map/s_a4/ppermute | solution.py:46
  63.5 1.1 copy-start.3
  64.6 1.9 %copy-start.5 = (f32[17,3,128,128]{3,2,1,0:T(8,128)S(1)}, f32[17,3,128,128]{3,2,1,0:T(8,128)}, u32[]{:S(2)}) copy-start(f32[17,3,128,128]{3,2,1,0:T(8,128)} %copy-done.4) | copy-start | bytes 10027012
  73.2 9.1 %collective-permute-start.15 = (bf16[4,3,2,128,128]{4,3,2,1,0:T(8,128)(2,1)S(1)}, bf16[4,3,2,128,128]{4,3,2,1,0:T(8,128)(2,1)S(1)}, u32[]{:S(2)}, u32[]{:S(2)}) collective-permute-start(bf16[4,3,2,128,128]{4,3,2,1,0:T(8,128)(2,1)S(1)} %collective-permute-done.11.refs_6_), channel_id=1, source_target_pairs={{0,8},{8,0},{1,9},{9,1},{2,10},{10,2},{3,11},{11,3},{4,12},{12,4},... | collective-permute-start | bytes 2359304 | tf_op jit(solution)/shard_map/s_tb3/ppermute | solution.py:39
  77.8 4.4 %collective-permute-start.18 = (bf16[4,3,2,128,128]{4,3,2,1,0:T(8,128)(2,1)S(1)}, bf16[4,3,2,128,128]{4,3,2,1,0:T(8,128)(2,1)S(1)}, u32[]{:S(2)}, u32[]{:S(2)}) collective-permute-start(bf16[4,3,2,128,128]{4,3,2,1,0:T(8,128)(2,1)S(1)} %collective-permute-done.17.refs_8_), channel_id=1, source_target_pairs={{0,8},{8,0},{1,9},{9,1},{2,10},{10,2},{3,11},{11,3},{4,12},{12,4},... | collective-permute-start | bytes 2359304 | tf_op jit(solution)/shard_map/s_ta4/ppermute | solution.py:39
  86.3 12.2 %collective-permute-start.21 = (bf16[2,400,128]{2,1,0:T(8,128)(2,1)S(1)}, bf16[2,400,128]{2,1,0:T(8,128)(2,1)S(1)}, u32[]{:S(2)}, u32[]{:S(2)}) collective-permute-start(bf16[2,400,128]{2,1,0:T(8,128)(2,1)S(1)} %get-tuple-element.49), channel_id=1, source_target_pairs={{0,1},{1,128},{128,129},{129,0},{2,3},{3,130},{130,131},{131,2},{4... | collective-permute-start | bytes 614408 | tf_op jit(solution)/shard_map/s_f0/ppermute | solution.py:34
  91.4 9.2 %collective-permute-start.22 = (bf16[2,400,128]{2,1,0:T(8,128)(2,1)S(1)}, bf16[2,400,128]{2,1,0:T(8,128)(2,1)S(1)}, u32[]{:S(2)}, u32[]{:S(2)}) collective-permute-start(bf16[2,400,128]{2,1,0:T(8,128)(2,1)S(1)} %get-tuple-element.51), channel_id=1, source_target_pairs={{0,129},{1,0},{128,1},{129,128},{2,131},{3,2},{130,3},{131,130},{4... | collective-permute-start | bytes 614408 | tf_op jit(solution)/shard_map/s_f1/ppermute | solution.py:34
  93.5 12.4 %collective-permute-start.27 = (bf16[2,400,128]{2,1,0:T(8,128)(2,1)S(1)}, bf16[2,400,128]{2,1,0:T(8,128)(2,1)S(1)}, u32[]{:S(2)}, u32[]{:S(2)}) collective-permute-start(bf16[2,400,128]{2,1,0:T(8,128)(2,1)S(1)} %get-tuple-element.56), channel_id=1, source_target_pairs={{0,1},{1,128},{128,129},{129,0},{2,3},{3,130},{130,131},{131,2},{4... | collective-permute-start | bytes 614408 | tf_op jit(solution)/shard_map/s_prv1/ppermute | solution.py:34
  100.9 8.5 %collective-permute-start.28 = (bf16[2,400,128]{2,1,0:T(8,128)(2,1)S(1)}, bf16[2,400,128]{2,1,0:T(8,128)(2,1)S(1)}, u32[]{:S(2)}, u32[]{:S(2)}) collective-permute-start(bf16[2,400,128]{2,1,0:T(8,128)(2,1)S(1)} %get-tuple-element.57), channel_id=1, source_target_pairs={{0,129},{1,0},{128,1},{129,128},{2,131},{3,2},{130,3},{131,130},{4... | collective-permute-start | bytes 614408 | tf_op jit(solution)/shard_map/s_nxt1/ppermute | solution.py:34
  103.9 8.9 %collective-permute-start.24 = (bf16[2,400,128]{2,1,0:T(8,128)(2,1)S(1)}, bf16[2,400,128]{2,1,0:T(8,128)(2,1)S(1)}, u32[]{:S(2)}, u32[]{:S(2)}) collective-permute-start(bf16[2,400,128]{2,1,0:T(8,128)(2,1)S(1)} %get-tuple-element.54), channel_id=1, source_target_pairs={{0,129},{1,0},{128,1},{129,128},{2,131},{3,2},{130,3},{131,130},{4... | collective-permute-start | bytes 614408 | tf_op jit(solution)/shard_map/s_nxt0/ppermute | solution.py:34
  105.9 7.0 %collective-permute-start.23 = (bf16[2,400,128]{2,1,0:T(8,128)(2,1)S(1)}, bf16[2,400,128]{2,1,0:T(8,128)(2,1)S(1)}, u32[]{:S(2)}, u32[]{:S(2)}) collective-permute-start(bf16[2,400,128]{2,1,0:T(8,128)(2,1)S(1)} %get-tuple-element.53), channel_id=1, source_target_pairs={{0,1},{1,128},{128,129},{129,0},{2,3},{3,130},{130,131},{131,2},{4... | collective-permute-start | bytes 614408 | tf_op jit(solution)/shard_map/s_prv0/ppermute | solution.py:34
  109.7 8.7 %collective-permute-start.29 = (bf16[256,384]{1,0:T(8,128)(2,1)S(1)}, bf16[256,384]{1,0:T(8,128)(2,1)S(1)}, u32[]{:S(2)}, u32[]{:S(2)}) collective-permute-start(bf16[256,384]{1,0:T(8,128)(2,1)S(1)} %combine.3.refs_1_), channel_id=1, source_target_pairs={{0,6},{2,0},{4,2},{6,4},{1,7},{3,1},{5,3},{7,5},{8,14},{10,8},{12,... | collective-permute-start | bytes 589832 | tf_op jit(solution)/shard_map/s_right1/ppermute | solution.py:34
  113.1 8.1 %collective-permute-start.25 = (bf16[256,384]{1,0:T(8,128)(2,1)S(1)}, bf16[256,384]{1,0:T(8,128)(2,1)S(1)}, u32[]{:S(2)}, u32[]{:S(2)}) collective-permute-start(bf16[256,384]{1,0:T(8,128)(2,1)S(1)} %combine.2.refs_0_), channel_id=1, source_target_pairs={{0,2},{2,4},{4,6},{6,0},{1,3},{3,5},{5,7},{7,1},{8,10},{10,12},{12... | collective-permute-start | bytes 589832 | tf_op jit(solution)/shard_map/s_left0/ppermute | solution.py:34
  115.1 9.8 %collective-permute-start.31 = (bf16[256,384]{1,0:T(8,128)(2,1)S(1)}, bf16[256,384]{1,0:T(8,128)(2,1)S(1)}, u32[]{:S(2)}, u32[]{:S(2)}) collective-permute-start(bf16[256,384]{1,0:T(8,128)(2,1)S(1)} %combine.3.refs_1_), channel_id=1, source_target_pairs={{0,2},{2,4},{4,6},{6,0},{1,3},{3,5},{5,7},{7,1},{8,10},{10,12},{12... | collective-permute-start | bytes 589832 | tf_op jit(solution)/shard_map/s_left1/ppermute | solution.py:34
  116.6 8.4 %collective-permute-start.32 = (bf16[256,384]{1,0:T(8,128)(2,1)S(1)}, bf16[256,384]{1,0:T(8,128)(2,1)S(1)}, u32[]{:S(2)}, u32[]{:S(2)}) collective-permute-start(bf16[256,384]{1,0:T(8,128)(2,1)S(1)} %combine.2.refs_0_), channel_id=1, source_target_pairs={{0,6},{2,0},{4,2},{6,4},{1,7},{3,1},{5,3},{7,5},{8,14},{10,8},{12,... | collective-permute-start | bytes 589832 | tf_op jit(solution)/shard_map/s_right0/ppermute | solution.py:34
  118.3 8.0 %collective-permute-start.30 = (bf16[256,384]{1,0:T(8,128)(2,1)S(1)}, bf16[256,384]{1,0:T(8,128)(2,1)S(1)}, u32[]{:S(2)}, u32[]{:S(2)}) collective-permute-start(bf16[256,384]{1,0:T(8,128)(2,1)S(1)} %collective-permute-done.29.refs_5_), channel_id=1, source_target_pairs={{0,6},{2,0},{4,2},{6,4},{1,7},{3,1},{5,3},{7,5},{8,14},{10,8},{12,... | collective-permute-start | bytes 589832 | tf_op jit(solution)/shard_map/s_r2/ppermute | solution.py:34
  121.2 6.9 %collective-permute-start.26 = (bf16[256,384]{1,0:T(8,128)(2,1)S(1)}, bf16[256,384]{1,0:T(8,128)(2,1)S(1)}, u32[]{:S(2)}, u32[]{:S(2)}) collective-permute-start(bf16[256,384]{1,0:T(8,128)(2,1)S(1)} %collective-permute-done.25.refs_2_), channel_id=1, source_target_pairs={{0,2},{2,4},{4,6},{6,0},{1,3},{3,5},{5,7},{7,1},{8,10},{10,12},{12... | collective-permute-start | bytes 589832 | tf_op jit(solution)/shard_map/s_l2/ppermute | solution.py:34
